TPU v7x, 32 devices: a whole 2x2x4 slice. The times are simulated.
32 devices in a mesh: dp: 8 (over z, y), tensor: 4 (over x, core).
Axes of the slice: x: 2, y: 2, z: 4, core: 2. Of those that a mesh axis runs over, the one named last changes fastest.
Arguments:
- residual: bfloat16 [2048, 8192], P(('dp', 'tensor')), may hold values from -6 to 6
- streams: bfloat16 [3, 2048, 8192], P(None, 'dp', 'tensor'), may hold values from -6 to 6
- short_filter: float32 [3, 3, 8192], P(None, None, 'tensor'), may hold values from -3 to 3
- long_filter: float32 [512, 128], P('tensor'), may hold values from -0.5 to 0.5
- skip: float32 [8192], P('tensor'), may hold values from -4 to 4
- gain: float32 [8192], replicated, may hold values from 0.5 to 1.5
- cotangent: bfloat16 [2048, 8192], P(('dp', 'tensor')), may hold values from -6 to 6
Outputs:
- normed: bfloat16 [2048, 8192], P(('dp', 'tensor'))
- grad_residual: bfloat16 [2048, 8192], P(('dp', 'tensor'))
- stream_grad: bfloat16 [3, 2048, 8192], P(None, 'dp', 'tensor')
- long_grad: float32 [512, 128], P('tensor')
- short_grad: float32 [3, 3, 8192], P(None, None, 'tensor')
- skip_grad: float32 [8192], P('tensor')
- gain_grad: float32 [8192], P('tensor')
All inputs are finite; a program needn't handle non-finite values.
Results may differ from a plain program's by a relative error of at most 0.025.
Values may be sent and summed in bfloat16 or wider, within the bound.
No kernel may reach another device: no remote copies, remote signals or barrier semaphores. Data moves between devices by JAX's collectives and lax.ppermute only.
A program may use at most 192 MiB of HBM per device.

v0:
```python
import jax
import jax.numpy as jnp
from jax import lax
from jax.sharding import PartitionSpec as P

norm_eps = 1e-05


def from_behind(value, axis, steps):
    count = lax.axis_size(axis)
    first, last = (max(0, -steps), min(count, count - steps))
    return lax.ppermute(value, axis, [(source, source + steps) for source in range(first, last)])


def featurize(padded, short_taps):
    length = padded.shape[1] - 2
    return (
        short_taps[:, 0][:, None, :] * padded[:, 2:]
        + short_taps[:, 1][:, None, :] * padded[:, 1 : length + 1]
        + short_taps[:, 2][:, None, :] * padded[:, :length]
    )


def band_matrix(row_vector, tap_count):
    groups = row_vector.shape[0]
    tiled_rows = jnp.broadcast_to(row_vector[:, None, :], (groups, tap_count, 2 * tap_count + 1))
    tiled_rows = tiled_rows.reshape(groups, tap_count * (2 * tap_count + 1))
    return tiled_rows[:, : tap_count * 2 * tap_count].reshape(groups, tap_count, 2 * tap_count)


def windows(extended, tap_count, group_width):
    blocks = extended.reshape(extended.shape[0] // tap_count, tap_count, extended.shape[1])
    joined = jnp.concatenate([blocks[:-1], blocks[1:]], axis=1)
    return joined.reshape(
        joined.shape[0], 2 * tap_count, extended.shape[1] // group_width, group_width
    )


def apply_band(matrix, window_set):
    result = jnp.einsum("gij,bjgc->bigc", matrix, window_set, preferred_element_type=jnp.float32)
    return result.reshape(result.shape[0] * result.shape[1], result.shape[2] * result.shape[3])


def local(residual, streams, short_filter, long_filter, skip, gain, cotangent):
    tokens_here = streams.shape[1]
    channels = streams.shape[2]
    tap_count = long_filter.shape[1]
    groups = long_filter.shape[0]
    group_width = channels // groups
    width_all = residual.shape[1]
    edge_rows = from_behind(streams[:, tokens_here - 2 :], "dp", 1)
    padded = jnp.concatenate([edge_rows, streams], axis=1)
    features = featurize(padded, short_filter)
    gated_rows = (features[1] * features[2]).astype(jnp.bfloat16)
    gated_edge = from_behind(gated_rows[tokens_here - tap_count :], "dp", 1)
    gated_ext = jnp.concatenate([gated_edge, gated_rows], axis=0)
    filter_half = long_filter.astype(jnp.bfloat16)
    zero_one = jnp.zeros((groups, 1), jnp.bfloat16)
    zero_span = jnp.zeros((groups, tap_count), jnp.bfloat16)
    ahead_band = band_matrix(
        jnp.concatenate([zero_one, filter_half[:, ::-1], zero_span], axis=1), tap_count
    )
    behind = band_matrix(jnp.concatenate([filter_half, zero_span, zero_one], axis=1), tap_count)
    gated_windows = windows(gated_ext, tap_count, group_width)
    gated_float = gated_rows.astype(jnp.float32)
    mixed_rows = apply_band(ahead_band, gated_windows) + skip[None, :] * gated_float
    output = (features[0] * mixed_rows).astype(jnp.bfloat16)
    resid_cols, cot_cols = (
        lax.all_to_all(residual, "tensor", split_axis=1, concat_axis=0, tiled=True),
        lax.all_to_all(cotangent, "tensor", split_axis=1, concat_axis=0, tiled=True),
    )
    gain_cols = lax.dynamic_slice_in_dim(gain, lax.axis_index("tensor") * channels, channels)
    summed = resid_cols.astype(jnp.float32) + output.astype(jnp.float32)
    squares = lax.psum(jnp.sum(summed * summed, axis=1), "tensor")
    inverse = lax.rsqrt(squares[:, None] / width_all + norm_eps)
    unit_rows = summed * inverse
    normed_cols = (unit_rows * gain_cols[None, :]).astype(jnp.bfloat16)
    cot_float = cot_cols.astype(jnp.float32)
    scaled = cot_float * gain_cols[None, :]
    products = lax.psum(jnp.sum(scaled * unit_rows, axis=1), "tensor")
    along_unit = products[:, None] / width_all
    grad_out = (inverse * (scaled - unit_rows * along_unit)).astype(jnp.bfloat16)
    gain_share = jnp.sum(cot_float * unit_rows, axis=0)
    normed, grad_residual = (
        lax.all_to_all(normed_cols, "tensor", split_axis=0, concat_axis=1, tiled=True),
        lax.all_to_all(grad_out, "tensor", split_axis=0, concat_axis=1, tiled=True),
    )
    grad_float = grad_out.astype(jnp.float32)
    grad_mixed = (grad_float * features[0]).astype(jnp.bfloat16)
    grad_query = grad_float * mixed_rows
    grad_next = from_behind(grad_mixed[:tap_count], "dp", -1)
    grad_ext = jnp.concatenate([grad_mixed, grad_next], axis=0)
    grad_mixed_float = grad_mixed.astype(jnp.float32)
    grad_gated = (
        apply_band(behind, windows(grad_ext, tap_count, group_width))
        + skip[None, :] * grad_mixed_float
    )
    feature_grad = jnp.stack([grad_query, grad_gated * features[2], grad_gated * features[1]])
    feature_next = from_behind(feature_grad[:, :2], "dp", -1)
    feature_ext = jnp.concatenate([feature_grad, feature_next], axis=1)
    stream_grad = (
        short_filter[:, 0][:, None, :] * feature_ext[:, :tokens_here]
        + short_filter[:, 1][:, None, :] * feature_ext[:, 1 : tokens_here + 1]
        + short_filter[:, 2][:, None, :] * feature_ext[:, 2:]
    ).astype(jnp.bfloat16)
    short_share = jnp.stack(
        [
            jnp.sum(feature_grad * padded[:, 2 - offset : 2 - offset + tokens_here], axis=1)
            for offset in range(3)
        ],
        axis=1,
    )
    grad_blocks = grad_mixed.reshape(tokens_here // tap_count, tap_count, groups, group_width)
    pair_sums = jnp.einsum(
        "bigc,bjgc->gij", grad_blocks, gated_windows, preferred_element_type=jnp.float32
    )
    flattened = jnp.pad(
        pair_sums.reshape(groups, tap_count * 2 * tap_count), ((0, 0), (0, tap_count))
    )
    skewed = flattened.reshape(groups, tap_count, 2 * tap_count + 1)
    diagonals = jnp.sum(skewed[:, :, 1 : tap_count + 1], axis=1)
    filter_share = diagonals[:, ::-1]
    skip_share = jnp.sum(grad_mixed_float * gated_float, axis=0)
    long_grad, short_grad, skip_grad, gain_grad = (
        lax.psum(filter_share.astype(jnp.bfloat16), "dp").astype(jnp.float32),
        lax.psum(short_share.astype(jnp.bfloat16), "dp").astype(jnp.float32),
        lax.psum(skip_share.astype(jnp.bfloat16), "dp").astype(jnp.float32),
        lax.psum(gain_share.astype(jnp.bfloat16), "dp").astype(jnp.float32),
    )
    return (normed, grad_residual, stream_grad, long_grad, short_grad, skip_grad, gain_grad)


def solution(mesh):
    placed = (
        P(("dp", "tensor"), None),
        P(None, "dp", "tensor"),
        P(None, None, "tensor"),
        P("tensor", None),
        P("tensor"),
        P(),
        P(("dp", "tensor"), None),
    )
    return jax.shard_map(
        local,
        mesh=mesh,
        in_specs=placed,
        out_specs=(
            P(("dp", "tensor"), None),
            P(("dp", "tensor"), None),
            P(None, "dp", "tensor"),
            P("tensor", None),
            P(None, None, "tensor"),
            P("tensor"),
            P("tensor"),
        ),
        check_vma=False,
    )
```

profile of v0, /device:TPU:0, one launch (start us, length us, event | category | flops | bytes accessed | tf_op | source)
XLA Modules:
  0.0 436.6 jit_solution(17662403761569482565)
XLA Ops:
  8.1 4.9 %collective-permute-start = (bf16[3,2,2048]{2,1,0:T(2,128)(2,1)S(1)}, bf16[3,2,2048]{2,1,0:T(2,128)(2,1)S(1)}, u32[]{:S(2)}, u32[]{:S(2)}) collective-permute-start(bf16[3,2,2048]{2,1,0:T(2,128)(2,1)S(1)} %slice.76), channel_id=1, source_target_pairs={{0,4},{4,8},{8,12},{12,16},{16,20},{20,24},{24,28},{1,5},{5,9},{9,... | collective-permute-start | bytes 73736 | tf_op jit(solution)/shard_map/ppermute | solution.py:12
  15.1 5.5 %fusion.1 = f32[3,256,2048]{2,1,0:T(8,128)S(1)} fusion(bf16[3,256,2048]{2,1,0:T(8,128)(2,1)} %param.8, bf16[3,2,2048]{2,1,0:T(2,128)(2,1)S(1)} %collective-permute-done, f32[3,2048]{1,0:T(4,128)S(1)} %get-tuple-element.73, f32[3,2048]{1,0:T(4,128)S(1)} %get-tuple-element.74, f32[3,2048]{1,0:T(4,128)S(1)} %bitcast.172), kind=kLoop, calls=%fused_computation.10 | loop fusion | flops 22020096 | bytes 9535488 | tf_op jit(solution)/shard_map/add | solution.py:18
  24.8 5.1 %collective-permute-start.1 = (bf16[128,2048]{1,0:T(8,128)(2,1)}, bf16[128,2048]{1,0:T(8,128)(2,1)}, u32[]{:S(2)}, u32[]{:S(2)}) collective-permute-start(bf16[128,2048]{1,0:T(8,128)(2,1)} %slice_bitcast_fusion), channel_id=1, source_target_pairs={{0,4},{4,8},{8,12},{12,16},{16,20},{20,24},{24,28},{1,5},{5,9},{9,... | collective-permute-start | bytes 1572872 | tf_op jit(solution)/shard_map/ppermute | solution.py:12
  30.9 3.6 all-to-all-start.2
  38.2 4.5 %broadcast_in_dim.10 = bf16[128,128,257]{0,2,1:T(8,128)(2,1)} broadcast(bf16[128,257]{0,1:T(8,128)(2,1)S(1)} %copy.150), dimensions={0,2} | broadcast | bytes 8487168 | tf_op jit(solution)/shard_map/broadcast_in_dim | solution.py:26
  42.7 12.9 %reshape.359 = bf16[128,32896]{0,1:T(8,128)(2,1)} reshape(bf16[128,128,257]{0,2,1:T(8,128)(2,1)} %broadcast_in_dim.10) | data formatting | bytes 16842752 | tf_op jit(solution)/shard_map/reshape | solution.py:27
  55.6 7.1 %slice.100 = bf16[128,32768]{0,1:T(8,128)(2,1)} slice(bf16[128,32896]{0,1:T(8,128)(2,1)} %reshape.359), slice={[0:128], [0:32768]} | slice | bytes 16777216 | tf_op jit(solution)/shard_map/slice | solution.py:28
  62.7 12.4 %copy.182 = bf16[128,128,256,1]{2,1,3,0:T(8,128)(2,1)} copy(bf16[128,128,256,1]{0,2,1,3:T(8,128)(2,1)} %bitcast.162) | data formatting | bytes 16777216 | tf_op jit(solution)/shard_map/reshape | solution.py:28
  75.1 4.5 %broadcast_in_dim.11 = bf16[128,128,257]{0,2,1:T(8,128)(2,1)} broadcast(bf16[128,257]{0,1:T(8,128)(2,1)S(1)} %copy.175), dimensions={0,2} | broadcast | bytes 8487168 | tf_op jit(solution)/shard_map/broadcast_in_dim | solution.py:26
  79.5 12.9 %reshape.364 = bf16[128,32896]{0,1:T(8,128)(2,1)} reshape(bf16[128,128,257]{0,2,1:T(8,128)(2,1)} %broadcast_in_dim.11) | data formatting | bytes 16842752 | tf_op jit(solution)/shard_map/reshape | solution.py:27
  92.4 7.1 %slice.102 = bf16[128,32768]{0,1:T(8,128)(2,1)} slice(bf16[128,32896]{0,1:T(8,128)(2,1)} %reshape.364), slice={[0:128], [0:32768]} | slice | bytes 16777216 | tf_op jit(solution)/shard_map/slice | solution.py:28
  99.5 12.8 %copy.183 = bf16[128,128,256,1]{2,1,3,0:T(8,128)(2,1)} copy(bf16[128,128,256,1]{0,2,1,3:T(8,128)(2,1)} %bitcast.163) | data formatting | bytes 16777216 | tf_op jit(solution)/shard_map/reshape | solution.py:28
  115.0 3.3 copy.166
  118.3 3.3 squeeze.13
  131.7 3.7 all-to-all-start
  135.4 7.0 %convolution_bitcast_fusion.1 = f32[2,128,128,16]{1,3,0,2:T(8,128)S(1)} fusion(bf16[2,256,128,16]{1,3,0,2:T(8,128)(2,1)} %copy_dynamic-update-slice_fusion.1, bf16[128,128,256,1]{2,1,3,0:T(8,128)(2,1)} %copy.182), kind=kOutput, calls=%fused_computation.77 | convolution fusion | flops 268435456 | bytes 12582912 | tf_op jit(solution)/shard_map/gij,bjgc->bigc/dot_general | solution.py:40
  143.8 2.5 copy.152
  146.3 3.9 reshape.362
  150.2 6.0 %reshape.361 = f32[4,64,2048]{1,0,2:T(4,128)} reshape(f32[2,128,128,16]{1,0,3,2:T(2,128)} %copy.152) | data formatting | bytes 4194304 | tf_op jit(solution)/shard_map/reshape | solution.py:41
  156.2 3.1 copy.235
  159.2 3.0 copy.172
  162.2 2.9 copy.162
  165.1 4.8 %copy.153 = f32[4,64,2048]{2,1,0:T(8,128)} copy(f32[4,64,2048]{1,0,2:T(4,128)} %reshape.361) | data formatting | bytes 4194304 | tf_op jit(solution)/shard_map/reshape | solution.py:41
  171.5 4.8 %copy.163 = f32[4,64,2048]{1,0,2:T(4,128)} copy(f32[4,64,2048]{2,1,0:T(8,128)} %convert_bitcast_fusion) | data formatting | bytes 4194304 | tf_op jit(solution)/shard_map/convert_element_type | solution.py:78
  176.2 5.8 %reshape.372 = f32[2,128,128,16]{1,0,3,2:T(2,128)} reshape(f32[4,64,2048]{1,0,2:T(4,128)} %copy.163) | data formatting | bytes 4194304 | tf_op jit(solution)/shard_map/convert_element_type | solution.py:78
  183.6 4.8 %copy.165 = f32[4,64,2048]{1,0,2:T(4,128)} copy(f32[4,64,2048]{2,1,0:T(8,128)} %convert_bitcast_fusion.1) | data formatting | bytes 4194304 | tf_op jit(solution)/shard_map/convert_element_type | solution.py:73
  188.4 5.8 %reshape.373 = f32[2,128,128,16]{1,0,3,2:T(2,128)} reshape(f32[4,64,2048]{1,0,2:T(4,128)} %copy.165) | data formatting | bytes 4194304 | tf_op jit(solution)/shard_map/convert_element_type | solution.py:73
  194.2 4.1 multiply_reduce_fusion.2
  198.4 7.3 %psum.42 = f32[256]{0:T(256)S(1)} all-reduce(f32[256]{0:T(256)S(1)} %reduce_sum.77), channel_id=1, replica_groups=mesh['dp'=8,'tensor'=4] {'tensor'}, use_global_device_ids=true, to_apply=%region_1.0 | all-reduce | flops 256 | bytes 2048 | tf_op jit(solution)/shard_map/psum | solution.py:74
  205.8 2.9 multiply_reduce_fusion
  208.8 5.7 %psum.43 = f32[256]{0:T(256)S(1)} all-reduce(f32[256]{0:T(256)S(1)} %reduce_sum.79), channel_id=1, replica_groups=mesh['dp'=8,'tensor'=4] {'tensor'}, use_global_device_ids=true, to_apply=%region_3.0 | all-reduce | flops 256 | bytes 2048 | tf_op jit(solution)/shard_map/psum | solution.py:80
  214.6 3.5 multiply_convert_fusion.3
  218.1 4.2 all-to-all-start.3
  222.4 4.3 fusion.13
  231.4 9.7 %convolution_bitcast_fusion = f32[128,128,256]{2,1,0:T(8,128)} fusion(bf16[2,128,128,16]{1,3,0,2:T(8,128)(2,1)S(1)} %multiply_convert_fusion, bf16[2,256,128,16]{1,3,0,2:T(8,128)(2,1)} %copy_dynamic-update-slice_fusion.1), kind=kOutput, calls=%fused_computation | convolution fusion | flops 268435456 | bytes 19922944 | tf_op jit(solution)/shard_map/bigc,bjgc->gij/dot_general | solution.py:114
  241.1 17.8 %copy.191 = f32[128,128,256]{0,2,1:T(8,128)} copy(f32[128,128,256]{2,1,0:T(8,128)} %convolution_bitcast_fusion) | data formatting | bytes 33554432 | tf_op jit(solution)/shard_map/reshape | solution.py:118
  259.0 13.3 %pad.4 = f32[128,32896]{0,1:T(8,128)} pad(f32[128,32768]{0,1:T(8,128)} %bitcast.158, f32[]{:T(128)} %constant.9.clone.1), padding=0_0x0_128 | pad | bytes 33619972 | tf_op jit(solution)/shard_map/jit(_pad)/pad | solution.py:117
  272.3 17.5 %reshape.368 = f32[128,128,257]{0,2,1:T(8,128)} reshape(f32[128,32896]{0,1:T(8,128)} %pad.4) | data formatting | bytes 33685504 | tf_op jit(solution)/shard_map/reshape | solution.py:120
  289.7 5.1 %convert_multiply_fusion.9 = (f32[1,256,2048]{2,1,0:T(8,128)}, bf16[1,256,2048]{2,1,0:T(8,128)(2,1)}) fusion(f32[1,256,2048]{2,1,0:T(8,128)} %copy.162, f32[2048]{0:T(1024)S(1)} %copy-done.21, bf16[1,256,2048]{2,1,0:T(8,128)(2,1)S(1)} %get-tuple-element.60, f32[256]{0:T(256)S(1)} %get-tuple-element.72, f32[3,256,2048]{2,1,0:T(8,128)} %copy-done, ...), kind=kLoop, calls=%fused_computation.27 | loop fusion | flops 8912896 | bytes 10504192 | tf_op jit(solution)/shard_map/mul | solution.py:90
  297.7 6.3 %fusion.34 = f32[2,128,128,16]{1,3,0,2:T(8,128)S(1)} fusion(bf16[128,128,256,1]{2,1,3,0:T(8,128)(2,1)} %copy.183, bf16[2,128,128,16]{1,3,0,2:T(8,128)(2,1)S(1)} %copy.174, bf16[2,128,128,16]{1,3,0,2:T(8,128)(2,1)S(1)} %copy-done.7), kind=kOutput, calls=%fused_computation.76 | convolution fusion | flops 272629760 | bytes 12582912 | tf_op jit(solution)/shard_map/gij,bjgc->bigc/dot_general | solution.py:40
  305.1 2.7 reshape.366
  307.8 3.0 copy.178
  310.8 4.6 %slice_multiply_fusion.2 = (f32[1,256,2048]{2,1,0:T(8,128)S(1)}, f32[1,256,2048]{2,1,0:T(8,128)S(1)}) fusion(f32[3,256,2048]{2,1,0:T(8,128)} %copy-done, f32[1,256,2048]{2,1,0:T(8,128)} %copy.178, f32[2048]{0:T(1024)S(1)} %copy-done.21, bf16[1,256,2048]{2,1,0:T(8,128)(2,1)S(1)} %copy-done.15), kind=kLoop, calls=%fused_computation.74 | loop fusion | flops 4194304 | bytes 13639680 | tf_op jit(solution)/shard_map/mul | solution.py:98
  319.0 4.4 %slice_reduce_fusion = bf16[128,128]{0,1:T(8,128)(2,1)S(1)} fusion(f32[128,128,257]{0,2,1:T(8,128)} %reshape.368), kind=kLoop, calls=%fused_computation.1 | loop fusion | flops 2080768 | bytes 8421376 | tf_op jit(solution)/shard_map/reduce_sum | solution.py:121
  324.1 4.7 %pad_maximum_fusion = f32[3,258,2048]{2,1,0:T(8,128)} fusion(f32[3,2,2048]{2,1,0:T(2,128)S(1)} %collective-permute-done.3, f32[1,256,2048]{2,1,0:T(8,128)} %copy-done.3, f32[1,256,2048]{2,1,0:T(8,128)} %copy-done.2, f32[1,256,2048]{2,1,0:T(8,128)S(1)} %copy-done.1), kind=kLoop, calls=%fused_computation.8 | loop fusion | flops 4755456 | bytes 12681216 | tf_op jit(solution)/shard_map/concatenate | solution.py:100
  328.8 3.7 all-to-all-start.1
  332.5 12.5 %fusion.3 = (bf16[3,2048]{1,0:T(4,128)(2,1)S(1)}, bf16[3,2048]{1,0:T(4,128)(2,1)S(1)}, bf16[3,2048]{1,0:T(4,128)(2,1)S(1)}, bf16[3,256,2048]{2,1,0:T(8,128)(2,1)}) fusion(bf16[3,256,2048]{2,1,0:T(8,128)(2,1)} %param.8, bf16[3,2,2048]{2,1,0:T(2,128)(2,1)S(1)} %copy-done.23, f32[1,256,2048]{2,1,0:T(8,128)} %copy-done.3, f32[1,256,2048]{2,1,0:T(8,128)} %copy-done.2, ...), kind=kLoop, calls=%fused_computation.12 | loop fusion | flops 36157440 | bytes 25300992 | tf_op jit(solution)/shard_map/reduce_sum | solution.py:108
  345.7 75.2 %all-reduce.4.cloned.1.call-done = (bf16[128,128]{0,1:T(8,128)(2,1)}, bf16[3,3,2048]{2,0,1:T(4,128)(2,1)}, bf16[2048]{0:T(1024)(128)(2,1)}, bf16[2048]{0:T(1024)(128)(2,1)}) async-done(((bf16[128,128]{0,1:T(8,128)(2,1)}, bf16[3,3,2048]{2,0,1:T(4,128)(2,1)}, bf16[2048]{0:T(1024)(128)(2,1)}, bf16[2048]{0:T(1024)(128)(2,1)}), (bf16[128,128]{0,1:T(8,128)(2,1)}, bf16[3,3,2048]{2,0,1:T(4,128)(2,1)}, ...) | async-done | bytes 77840 | tf_op jit(solution)/shard_map/psum | solution.py:125
  (112 shorter events, 51.9 us)
Async XLA Ops:
  8.1 6.4 %collective-permute-start = (bf16[3,2,2048]{2,1,0:T(2,128)(2,1)S(1)}, bf16[3,2,2048]{2,1,0:T(2,128)(2,1)S(1)}, u32[]{:S(2)}, u32[]{:S(2)}) collective-permute-start(bf16[3,2,2048]{2,1,0:T(2,128)(2,1)S(1)} %slice.76), channel_id=1, source_target_pairs={{0,4},{4,8},{8,12},{12,16},{16,20},{20,24},{24,28},{1,5},{5,9},{9,... | collective-permute-start | bytes 73736 | tf_op jit(solution)/shard_map/ppermute | solution.py:12
  14.5 0.6 copy-start.22
  20.6 3.3 copy-start
  20.6 9.2 %copy-start.16 = (bf16[64,8192]{1,0:T(8,128)(2,1)S(1)}, bf16[64,8192]{1,0:T(8,128)(2,1)}, u32[]{:S(2)}) copy-start(bf16[64,8192]{1,0:T(8,128)(2,1)} %param.13) | copy-start | bytes 3145732
  24.8 96.8 %collective-permute-start.1 = (bf16[128,2048]{1,0:T(8,128)(2,1)}, bf16[128,2048]{1,0:T(8,128)(2,1)}, u32[]{:S(2)}, u32[]{:S(2)}) collective-permute-start(bf16[128,2048]{1,0:T(8,128)(2,1)} %slice_bitcast_fusion), channel_id=1, source_target_pairs={{0,4},{4,8},{8,12},{12,16},{16,20},{20,24},{24,28},{1,5},{5,9},{9,... | collective-permute-start | bytes 1572872 | tf_op jit(solution)/shard_map/ppermute | solution.py:12
  29.8 4.7 %copy-start.24 = (f32[128,128]{1,0:T(8,128)S(1)}, f32[128,128]{1,0:T(8,128)}, u32[]{:S(2)}) copy-start(f32[128,128]{1,0:T(8,128)} %param.10) | copy-start | bytes 196612
  29.8 6.3 %copy-start.20 = (f32[2048]{0:T(1024)S(1)}, f32[2048]{0:T(1024)}, u32[]{:S(2)}) copy-start(f32[2048]{0:T(1024)} %param.11) | copy-start | bytes 24580
  30.9 6.3 %copy-start.17 = (bf16[64,8192]{1,0:T(8,128)(2,1)S(1)}, bf16[64,8192]{1,0:T(8,128)(2,1)}, u32[]{:S(2)}) copy-start(bf16[64,8192]{1,0:T(8,128)(2,1)} %param.7) | copy-start | bytes 3145732
  30.9 100.8 %all-to-all-start.2 = ((bf16[64,4,2048]{2,0,1:T(8,128)(2,1)}), bf16[64,4,2048]{2,0,1:T(8,128)(2,1)S(1)}, u32[]{:S(2)}, u32[]{:S(2)}) async-start(bf16[64,4,2048]{2,0,1:T(8,128)(2,1)} %bitcast.155), calls=%async_computation.2 | async-start | bytes 2097152 | tf_op jit(solution)/shard_map/all_to_all | solution.py:70
  115.0 15.5 %copy-start.8 = (bf16[2,128,128,16]{1,0,3,2:T(2,128)(2,1)}, bf16[2,128,128,16]{1,0,3,2:T(2,128)(2,1)S(1)}, u32[]{:S(2)}) copy-start(bf16[2,128,128,16]{1,0,3,2:T(2,128)(2,1)S(1)} %convert_element_type.257) | copy-start | bytes 3145732
  131.7 50.3 %all-to-all-start = ((bf16[64,4,2048]{2,0,1:T(8,128)(2,1)}), bf16[64,4,2048]{2,0,1:T(8,128)(2,1)S(1)}, u32[]{:S(2)}, u32[]{:S(2)}) async-start(bf16[64,4,2048]{2,0,1:T(8,128)(2,1)} %bitcast.166), calls=%async_computation | async-start | bytes 2097152 | tf_op jit(solution)/shard_map/all_to_all | solution.py:69
  142.4 1.4 copy-start.4
  188.4 5.8 %copy-start.21 = (f32[2048]{0:T(1024)S(1)}, f32[2048]{0:T(1024)}, u32[]{:S(2)}) copy-start(f32[2048]{0:T(1024)} %param.11) | copy-start | bytes 24580
  214.6 14.6 %copy-start.18 = (f32[128,16]{1,0:T(8,128)S(1)}, f32[128,16]{1,0:T(8,128)}, u32[]{:S(2)}) copy-start(f32[128,16]{1,0:T(8,128)} %mul.336) | copy-start | bytes 24580
  214.6 14.6 %copy-start.19 = (f32[128,16]{1,0:T(8,128)S(1)}, f32[128,16]{1,0:T(8,128)}, u32[]{:S(2)}) copy-start(f32[128,16]{1,0:T(8,128)} %mul.339) | copy-start | bytes 24580
  218.1 110.6 %all-to-all-start.3 = ((bf16[4,64,2048]{2,1,0:T(8,128)(2,1)}), bf16[4,64,2048]{2,1,0:T(8,128)(2,1)}, u32[]{:S(2)}, u32[]{:S(2)}) async-start(bf16[4,64,2048]{2,1,0:T(8,128)(2,1)} %get-tuple-element.62), calls=%async_computation.3 | async-start | bytes 2097152 | tf_op jit(solution)/shard_map/all_to_all | solution.py:86
  222.4 6.8 %copy-start.5 = (f32[2,128,128,16]{1,3,0,2:T(8,128)S(1)}, f32[2,128,128,16]{1,3,0,2:T(8,128)}, u32[]{:S(2)}) copy-start(f32[2,128,128,16]{1,3,0,2:T(8,128)} %copy-done.4) | copy-start | bytes 6291460
  222.4 6.8 %copy-start.9 = (bf16[2,128,128,16]{1,0,3,2:T(2,128)(2,1)S(1)}, bf16[2,128,128,16]{1,0,3,2:T(2,128)(2,1)}, u32[]{:S(2)}) copy-start(bf16[2,128,128,16]{1,0,3,2:T(2,128)(2,1)} %copy-done.8) | copy-start | bytes 3145732
  222.4 6.8 %copy-start.10 = (f32[2,128,128,16]{1,0,3,2:T(2,128)S(1)}, f32[2,128,128,16]{1,0,3,2:T(2,128)}, u32[]{:S(2)}) copy-start(f32[2,128,128,16]{1,0,3,2:T(2,128)} %reshape.372) | copy-start | bytes 6291460
  222.4 6.8 %copy-start.11 = (f32[2,128,128,16]{1,0,3,2:T(2,128)S(1)}, f32[2,128,128,16]{1,0,3,2:T(2,128)}, u32[]{:S(2)}) copy-start(f32[2,128,128,16]{1,0,3,2:T(2,128)} %reshape.373) | copy-start | bytes 6291460
  222.4 6.8 %copy-start.12 = (f32[2,128,128,16]{1,0,3,2:T(2,128)S(1)}, f32[2,128,128,16]{1,0,3,2:T(2,128)}, u32[]{:S(2)}) copy-start(f32[2,128,128,16]{1,0,3,2:T(2,128)} %squeeze.13) | copy-start | bytes 6291460
  226.8 2.4 copy-start.13
  227.6 67.2 %collective-permute-start.2 = (bf16[128,2048]{1,0:T(8,128)(2,1)}, bf16[128,2048]{1,0:T(8,128)(2,1)}, u32[]{:S(2)}, u32[]{:S(2)}) collective-permute-start(bf16[128,2048]{1,0:T(8,128)(2,1)} %slice.101), channel_id=1, source_target_pairs={{4,0},{8,4},{12,8},{16,12},{20,16},{24,20},{28,24},{5,1},{9,5},{13... | collective-permute-start | bytes 1572872 | tf_op jit(solution)/shard_map/ppermute | solution.py:12
  230.4 1.0 copy-start.6
  289.7 5.1 %copy-start.14 = (bf16[256,2048]{1,0:T(8,128)(2,1)S(1)}, bf16[256,2048]{1,0:T(8,128)(2,1)}, u32[]{:S(2)}) copy-start(bf16[256,2048]{1,0:T(8,128)(2,1)} %copy-done.13) | copy-start | bytes 3145732
  296.5 1.2 copy-start.7
  307.8 3.0 copy-start.15
  310.8 4.6 %copy-start.1 = (f32[1,256,2048]{2,1,0:T(8,128)S(1)}, f32[1,256,2048]{2,1,0:T(8,128)}, u32[]{:S(2)}) copy-start(f32[1,256,2048]{2,1,0:T(8,128)} %get-tuple-element.53) | copy-start | bytes 6291460
  315.4 1.6 copy-start.2
  315.4 2.0 copy-start.3
  317.4 6.6 %collective-permute-start.3 = (f32[3,2,2048]{2,1,0:T(2,128)S(1)}, f32[3,2,2048]{2,1,0:T(2,128)S(1)}, u32[]{:S(2)}, u32[]{:S(2)}) collective-permute-start(f32[3,2,2048]{2,1,0:T(2,128)S(1)} %slice.103), channel_id=1, source_target_pairs={{4,0},{8,4},{12,8},{16,12},{20,16},{24,20},{28,24},{5,1},{9,5},{13... | collective-permute-start | bytes 147464 | tf_op jit(solution)/shard_map/ppermute | solution.py:12
  328.8 3.7 copy-start.23
  328.8 99.9 %all-to-all-start.1 = ((bf16[4,64,2048]{2,1,0:T(8,128)(2,1)}), bf16[4,64,2048]{2,1,0:T(8,128)(2,1)S(1)}, u32[]{:S(2)}, u32[]{:S(2)}) async-start(bf16[4,64,2048]{2,1,0:T(8,128)(2,1)} %get-tuple-element.63), calls=%async_computation.1 | async-start | bytes 2097152 | tf_op jit(solution)/shard_map/all_to_all | solution.py:85
  332.4 88.4 %all-reduce.4.cloned.1.call-start = ((), (), s32[]{:S(2)}) async-start(), calls=%async_computation.4 | async-start | bytes 180224 | tf_op jit(solution)/shard_map/psum | solution.py:125
Sparse Core Ops, SparseCore 0:
  345.8 74.9 all-reduce.3
where the time goes:
time: 440 us; the launch traced here: 437 us
  local copies, waits for them, and re-layouts  217 us (49%)
  waiting for transfers between devices  75.5 us (17%)
  other arithmetic  65.1 us (15%)
  starting transfers between devices  28.3 us (6%)
  matrix products  23 us (5%)
  between operations  14.5 us (3%)
  blocking collectives  13.1 us (3%)
    psum x1, waiting for transfers between devices, local(): lax.psum(filter_share.astype(jnp.bfloat16), 'dp').astype(jnp.float32)  75.2 us
    reshape x7, local copies, waits for them, and re-layouts, apply_band(): result.reshape(result.shape[0] * result.shape[1], result.shape[2] * resul...  26.3 us
    reshape x2, local copies, waits for them, and re-layouts, band_matrix(): tiled_rows = tiled_rows.reshape(groups, tap_count * (2 * tap_count + 1))  25.8 us
    reshape x2, local copies, waits for them, and re-layouts, band_matrix(): tiled_rows[:, :tap_count * 2 * tap_count]  25.1 us
    reshape x1, local copies, waits for them, and re-layouts, local(): pair_sums.reshape(groups, tap_count * 2 * tap_count)  17.8 us
    reshape x1, local copies, waits for them, and re-layouts, local(): skewed = flattened.reshape(groups, tap_count, 2 * tap_count + 1)  17.5 us
    unnamed x56, local copies, waits for them, and re-layouts  14.9 us
    slice x2, local copies, waits for them, and re-layouts, band_matrix(): tiled_rows[:, :tap_count * 2 * tap_count]  14.2 us
  transfers between devices with their start and end apart: 9, of which 2 were waited for; matrix products, arithmetic and copies ran while one was open for 61% of the time, Pallas kernels for 0%

commit v1 on v0

v1 whole, which is shorter than its diff:
```python
import functools

import jax
import jax.numpy as jnp
from jax import lax
from jax.experimental import pallas as pl
from jax.experimental.pallas import tpu as pltpu
from jax.sharding import PartitionSpec as P

norm_eps = 1e-05
LANES = 128
TAPS = 128
WIDTH = 16
PER = LANES // WIDTH
VMEM_LIMIT = 40 * 2**20
f32 = jnp.float32
bf16 = jnp.bfloat16


def params():
    return pltpu.CompilerParams(vmem_limit_bytes=VMEM_LIMIT)


def dot(a, b):
    return lax.dot_general(a, b, (((1,), (0,)), ((), ())), preferred_element_type=f32)


def dot_nt(a, b):
    return lax.dot_general(a, b, (((1,), (1,)), ((), ())), preferred_element_type=f32)


def lane_group(shape):
    return lax.broadcasted_iota(jnp.int32, shape, len(shape) - 1) % LANES // WIDTH


def pick_groups(stacked, rows):
    out = stacked[:rows]
    which = lane_group(out.shape)
    for g in range(1, PER):
        out = jnp.where(which == g, stacked[g * rows : (g + 1) * rows], out)
    return out


def shifted(scratch, halo, current):
    length = current.shape[0]
    scratch[6:8, :] = halo
    scratch[8 : 8 + length, :] = current
    return scratch[7 : 7 + length, :], scratch[6 : 6 + length, :]


def feature(scratch, halo_ref, streams_ref, taps_ref, s, lanes):
    now = streams_ref[s, :, lanes].astype(f32)
    one, two = shifted(scratch, halo_ref[s, :, lanes].astype(f32), now)
    taps = taps_ref[s, :, lanes]
    return taps[0:1] * now + taps[1:2] * one + taps[2:3] * two


def bands_kernel(filter_ref, ahead_ref, behind_ref):
    rows = filter_ref[...]
    half = rows.astype(bf16)
    flip = (
        lax.broadcasted_iota(jnp.int32, (TAPS, TAPS), 0) + lax.broadcasted_iota(jnp.int32, (TAPS, TAPS), 1) == TAPS - 1
    )
    back = dot(half, flip.astype(f32).astype(bf16))
    fore = half.astype(f32)
    zero = jnp.zeros((TAPS, TAPS), f32)
    for g in range(rows.shape[0]):
        for source, out, first in ((back, ahead_ref, 1), (fore, behind_ref, 0)):
            wide = jnp.concatenate([jnp.broadcast_to(source[g : g + 1], (TAPS, TAPS)), zero], axis=1)
            out[g] = pltpu.roll(wide, first, 1, stride=1, stride_axis=0).astype(bf16)


def forward_kernel(
    streams_ref, edge_ref, before_ref, taps_ref, skip_ref, ahead_ref, output_ref, mixed_ref, gated_ref, scratch
):
    length = streams_ref.shape[1]
    for col in range(streams_ref.shape[2] // LANES):
        lanes = slice(col * LANES, (col + 1) * LANES)
        f0, f1, f2 = (
            feature(scratch.at[s], edge_ref, streams_ref, taps_ref, s, lanes) for s in range(3)
        )
        gated = (f1 * f2).astype(bf16)
        gated_ref[:, lanes] = gated
        extended = jnp.concatenate([before_ref[:, lanes], gated], axis=0)
        bands = ahead_ref[col * PER : (col + 1) * PER].reshape(PER * TAPS, 2 * TAPS)
        skip = skip_ref[:, lanes]
        for pair in range(length // (2 * TAPS)):
            at = pair * 2 * TAPS
            both = jnp.concatenate([extended[at : at + 2 * TAPS], extended[at + TAPS : at + 3 * TAPS]], axis=1)
            result = pick_groups(dot(bands, both), TAPS)
            for b in range(2):
                rows = slice(at + b * TAPS, at + (b + 1) * TAPS)
                mixed = result[:, b * LANES : (b + 1) * LANES] + skip * gated[rows].astype(f32)
                mixed_ref[rows, lanes] = mixed
                output_ref[rows, lanes] = (f0[rows] * mixed).astype(bf16)


def norm_kernel(chunks, *refs):
    received, rest = refs[:chunks], refs[chunks:]
    residual_ref, cot_ref, gain_ref, normed_ref, grad_ref = rest[:5]
    sent, (share_ref, summed_ref, total_ref) = rest[5 : 5 + chunks], rest[5 + chunks :]
    sources, rows, part = received[0].shape
    width_all = residual_ref.shape[1]
    squares = jnp.zeros((rows, LANES), f32)
    products = jnp.zeros((rows, LANES), f32)
    pieces = [
        (s, k, slice((s * chunks + k) * part, (s * chunks + k + 1) * part))
        for s in range(sources)
        for k in range(chunks)
    ]
    for s, k, where in pieces:
        summed = residual_ref[:, where].astype(f32) + received[k][s].astype(f32)
        summed_ref[:, where] = summed
        scaled = cot_ref[:, where].astype(f32) * gain_ref[:, where]
        both = (summed * summed, scaled * summed)
        for col in range(part // LANES):
            lanes = slice(col * LANES, (col + 1) * LANES)
            squares = squares + both[0][:, lanes]
            products = products + both[1][:, lanes]
    inverse = lax.rsqrt(jnp.sum(squares, axis=1, keepdims=True) / width_all + norm_eps)
    along = inverse * jnp.sum(products, axis=1, keepdims=True) / width_all
    first = pl.program_id(0) == 0
    for s, k, where in pieces:
        unit = summed_ref[:, where] * inverse
        gain = gain_ref[:, where]
        cot = cot_ref[:, where].astype(f32)
        normed_ref[:, where] = (unit * gain).astype(bf16)
        grad = (inverse * (cot * gain - unit * along)).astype(bf16)
        grad_ref[:, where] = grad
        sent[k][s] = grad
        share = jnp.sum((cot * unit).reshape(rows // 8, 8, part), axis=0)
        total_ref[:, where] = jnp.where(first, share, total_ref[:, where] + share)

    @pl.when(pl.program_id(0) == pl.num_programs(0) - 1)
    def _():
        share_ref[...] = jnp.sum(total_ref[...], axis=0, keepdims=True)


def head_kernel(
    streams_ref, edge_ref, taps_ref, skip_ref, behind_ref, grad_ref, mixed_ref, inner_ref, head_ref, scratch
):
    for col in range(streams_ref.shape[2] // LANES):
        lanes = slice(col * LANES, (col + 1) * LANES)
        f0 = feature(scratch, edge_ref, streams_ref, taps_ref, 0, lanes)
        inner = (grad_ref[:, lanes].astype(f32) * f0).astype(bf16)
        inner_ref[:, lanes] = inner
        early = [
            taps_ref[s, 0:1, lanes] * streams_ref[s, 0:16, lanes].astype(f32)[:8]
            for s in range(3)
        ]
        features = []
        for s in (1, 2):
            taps = taps_ref[s, :, lanes]
            now = streams_ref[s, 0:16, lanes].astype(f32)
            scratch[6:8, :] = edge_ref[s, :, lanes].astype(f32)
            scratch[8:24, :] = now
            features.append(early[s] + taps[1:2] * scratch[7:15, :] + taps[2:3] * scratch[6:14, :])
        bands = behind_ref[col * PER : (col + 1) * PER, 0:16, :].reshape(PER * 16, 2 * TAPS)
        conv = pick_groups(dot(bands, inner[: 2 * TAPS]), 16)[:8]
        grad_gated = conv + skip_ref[:, lanes] * inner[0:16].astype(f32)[:8]
        head_ref[0, :, lanes] = (grad_ref[0:16, lanes].astype(f32)[:8] * mixed_ref[0:8, lanes])[:2]
        head_ref[1, :, lanes] = (grad_gated * features[1])[:2]
        head_ref[2, :, lanes] = (grad_gated * features[0])[:2]


def sums_kernel(
    streams_ref, edge_ref, gated_ref, before_ref, inner_ref, grad_ref, mixed_ref, gain_ref, early_ref, scratch
):
    length = streams_ref.shape[1]
    flip = (
        lax.broadcasted_iota(jnp.int32, (2 * TAPS, 2 * TAPS), 0)
        + lax.broadcasted_iota(jnp.int32, (2 * TAPS, 2 * TAPS), 1)
        == 2 * TAPS - 1
    )
    flip = flip.astype(f32).astype(bf16)
    which = lane_group((TAPS, 2 * LANES))
    masks = [jnp.where(which == g, 1.0, 0.0).astype(bf16) for g in range(PER)]
    for col in range(streams_ref.shape[2] // LANES):
        lanes = slice(col * LANES, (col + 1) * LANES)
        gated = gated_ref[:, lanes]
        inner = inner_ref[:, lanes]
        extended = jnp.concatenate([before_ref[:, lanes], gated], axis=0)
        pairs = 0.0
        for pair in range(length // (2 * TAPS)):
            at = pair * 2 * TAPS
            both = jnp.concatenate([extended[at : at + 2 * TAPS], extended[at + TAPS : at + 3 * TAPS]], axis=1)
            backward = dot(flip, both).astype(bf16)
            grads = jnp.concatenate([inner[at : at + TAPS], inner[at + TAPS : at + 2 * TAPS]], axis=1)
            stacked = jnp.concatenate([grads * mask for mask in masks], axis=0)
            pairs = pairs + dot_nt(stacked, backward)
        base = col * 16
        for g in range(PER):
            skewed = pltpu.roll(pairs[g * TAPS : (g + 1) * TAPS], TAPS + 1, 1, stride=1, stride_axis=0)
            early_ref[base + g : base + g + 1, :] = jnp.sum(skewed[:, :TAPS], axis=0, keepdims=True)
        early_ref[base + 8 : base + 9, :] = jnp.sum(inner.astype(f32) * gated.astype(f32), axis=0, keepdims=True)
        early_ref[base + 9 : base + 10, :] = jnp.sum(gain_ref[:, lanes], axis=0, keepdims=True)
        grad_query = grad_ref[:, lanes].astype(f32) * mixed_ref[:, lanes]
        now = streams_ref[0, :, lanes].astype(f32)
        one, two = shifted(scratch, edge_ref[0, :, lanes].astype(f32), now)
        for j, shift in enumerate((now, one, two)):
            early_ref[base + 10 + j : base + 11 + j, :] = jnp.sum(grad_query * shift, axis=0, keepdims=True)
        early_ref[base + 13 : base + 16, :] = jnp.zeros((3, LANES), f32)


def backward_kernel(
    aliased,
    streams_ref,
    edge_ref,
    taps_ref,
    skip_ref,
    behind_ref,
    grad_ref,
    mixed_ref,
    inner_ref,
    after_ref,
    next_ref,
    *refs,
):
    stream_grad_ref, late_ref, scratch, ahead = refs[1:] if aliased else refs
    length = streams_ref.shape[1]
    for col in range(streams_ref.shape[2] // LANES):
        lanes = slice(col * LANES, (col + 1) * LANES)
        inner = inner_ref[:, lanes]
        extended = jnp.concatenate([inner, after_ref[:, lanes]], axis=0)
        bands = behind_ref[col * PER : (col + 1) * PER].reshape(PER * TAPS, 2 * TAPS)
        parts = []
        for pair in range(length // (2 * TAPS)):
            at = pair * 2 * TAPS
            both = jnp.concatenate([extended[at : at + 2 * TAPS], extended[at + TAPS : at + 3 * TAPS]], axis=1)
            result = pick_groups(dot(bands, both), TAPS)
            parts += [result[:, :LANES], result[:, LANES:]]
        grad_gated = jnp.concatenate(parts, axis=0) + skip_ref[:, lanes] * inner.astype(f32)
        shifts, features = {}, {}
        for s in (1, 2):
            now = streams_ref[s, :, lanes].astype(f32)
            one, two = shifted(scratch.at[s], edge_ref[s, :, lanes].astype(f32), now)
            taps = taps_ref[s, :, lanes]
            shifts[s] = (now, one, two)
            features[s] = taps[0:1] * now + taps[1:2] * one + taps[2:3] * two
        grads = (
            grad_ref[:, lanes].astype(f32) * mixed_ref[:, lanes],
            grad_gated * features[2],
            grad_gated * features[1],
        )
        for s in range(3):
            ahead[s, 0:length, :] = grads[s]
            ahead[s, length : length + 2, :] = next_ref[s, :, lanes]
            taps = taps_ref[s, :, lanes]
            stream_grad_ref[s, :, lanes] = (
                taps[0:1] * grads[s] + taps[1:2] * ahead[s, 1 : length + 1, :] + taps[2:3] * ahead[s, 2 : length + 2, :]
            ).astype(bf16)
        for s in (1, 2):
            for j in range(3):
                row = col * 8 + (s - 1) * 3 + j
                late_ref[row : row + 1, :] = jnp.sum(grads[s] * shifts[s][j], axis=0, keepdims=True)
        late_ref[col * 8 + 6 : col * 8 + 8, :] = jnp.zeros((2, LANES), f32)


def from_behind(value, axis, steps):
    count = lax.axis_size(axis)
    first, last = (max(0, -steps), min(count, count - steps))
    return lax.ppermute(value, axis, [(source, source + steps) for source in range(first, last)])


def sum_over(value, axis):
    count, reach = lax.axis_size(axis), 1
    while reach < count:
        value = lax.reduce_precision(value, 8, 7)
        other = lax.ppermute(value.astype(bf16), axis, [(i, i ^ reach) for i in range(count)])
        value = value + other.astype(f32)
        reach *= 2
    return value


def local(residual, streams, short_filter, long_filter, skip, gain, cotangent):
    tokens_here, channels = streams.shape[1:]
    groups = long_filter.shape[0]
    rows_here, width_all = residual.shape
    owners = lax.axis_size("tensor")
    assert long_filter.shape[1] == TAPS and channels == groups * WIDTH and tokens_here % (2 * TAPS) == 0
    chunks = 2
    part = channels // chunks
    step = min(part, 512)
    steps = part // step
    cols = step // LANES
    skip_row = skip[None, :]
    gain_row = gain[None, :]

    def spec(shape, index):
        return pl.BlockSpec(shape, index)

    def wide(rows, offset=0):
        return spec((rows, step), lambda i: (0, i + offset))

    def deep(first, rows, offset=0):
        return spec((first, rows, step), lambda i: (0, 0, i + offset))

    def band(offset):
        return spec((step // WIDTH, TAPS, 2 * TAPS), lambda i: (i + offset, 0, 0))

    def padded(count=None):
        shape = (tokens_here + 8, LANES)
        return pltpu.VMEM(shape if count is None else (count,) + shape, f32)

    edge = from_behind(streams[:, tokens_here - 2 :], "dp", 1)
    tail = streams[1:, tokens_here - TAPS - 2 :].astype(f32)
    tail_features = (
        short_filter[1:, 0][:, None, :] * tail[:, 2:]
        + short_filter[1:, 1][:, None, :] * tail[:, 1:-1]
        + short_filter[1:, 2][:, None, :] * tail[:, :-2]
    )
    tail_gated = (tail_features[0] * tail_features[1]).astype(bf16)
    before = [from_behind(tail_gated[:, k * part : (k + 1) * part], "dp", 1) for k in range(chunks)]

    band_shape = jax.ShapeDtypeStruct((groups, TAPS, 2 * TAPS), bf16)
    ahead_bands, behind_bands = pl.pallas_call(
        bands_kernel,
        grid=(groups // PER,),
        in_specs=[spec((PER, TAPS), lambda i: (i, 0))],
        out_specs=[spec((PER, TAPS, 2 * TAPS), lambda i: (i, 0, 0))] * 2,
        out_shape=[band_shape] * 2,
        compiler_params=params(),
        name="bands",
    )(long_filter)

    mixed, gated, received = [], [], []
    for k in range(chunks):
        output, mixed_k, gated_k = pl.pallas_call(
            forward_kernel,
            grid=(steps,),
            in_specs=[
                deep(3, tokens_here, k * steps),
                deep(3, 2, k * steps),
                wide(TAPS),
                deep(3, 3, k * steps),
                wide(1, k * steps),
                band(k * steps),
            ],
            out_specs=[wide(tokens_here)] * 3,
            out_shape=[jax.ShapeDtypeStruct((tokens_here, part), t) for t in (bf16, f32, bf16)],
            scratch_shapes=[padded(3)],
            compiler_params=params(),
            name="forward",
        )(streams, edge, before[k], short_filter, skip_row, ahead_bands)
        mixed.append(mixed_k)
        gated.append(gated_k)
        received.append(
            lax.all_to_all(output.reshape(owners, rows_here, part), "tensor", split_axis=0, concat_axis=0, tiled=True)
        )

    block = min(rows_here, 16)
    by_rows = spec((block, width_all), lambda i: (i, 0))
    by_owner = spec((owners, block, part), lambda i: (0, i, 0))
    whole_row = spec((1, width_all), lambda i: (0, 0))
    results = pl.pallas_call(
        functools.partial(norm_kernel, chunks),
        grid=(rows_here // block,),
        in_specs=[by_owner] * chunks + [by_rows, by_rows, whole_row],
        out_specs=[by_rows, by_rows] + [by_owner] * chunks + [whole_row],
        out_shape=[jax.ShapeDtypeStruct(residual.shape, bf16)] * 2
        + [jax.ShapeDtypeStruct((owners, rows_here, part), bf16)] * chunks
        + [jax.ShapeDtypeStruct((1, width_all), f32)],
        scratch_shapes=[pltpu.VMEM((block, width_all), f32), pltpu.VMEM((8, width_all), f32)],
        compiler_params=params(),
        name="norm",
    )(*received, residual, cotangent, gain_row)
    normed, grad_residual, sent, gain_share = results[0], results[1], results[2 : 2 + chunks], results[-1]

    grads = [
        lax.all_to_all(piece, "tensor", split_axis=0, concat_axis=0, tiled=True).reshape(tokens_here, part)
        for piece in sent
    ]
    gain_parts = lax.all_to_all(
        gain_share.reshape(owners, channels), "tensor", split_axis=0, concat_axis=0, tiled=True
    )

    inner, after, following = [], [], []
    for k in range(chunks):
        inner_k, head_k = pl.pallas_call(
            head_kernel,
            grid=(steps,),
            in_specs=[
                deep(3, tokens_here, k * steps),
                deep(3, 2, k * steps),
                deep(3, 3, k * steps),
                wide(1, k * steps),
                band(k * steps),
                wide(tokens_here),
                wide(tokens_here),
            ],
            out_specs=[wide(tokens_here), deep(3, 2)],
            out_shape=[
                jax.ShapeDtypeStruct((tokens_here, part), bf16),
                jax.ShapeDtypeStruct((3, 2, part), f32),
            ],
            scratch_shapes=[padded()],
            compiler_params=params(),
            name="head",
        )(streams, edge, short_filter, skip_row, behind_bands, grads[k], mixed[k])
        inner.append(inner_k)
        after.append(from_behind(inner_k[:TAPS], "dp", -1))
        following.append(from_behind(head_k, "dp", -1))

    early = []
    for k in range(chunks):
        early.append(
            pl.pallas_call(
                sums_kernel,
                grid=(steps,),
                in_specs=[
                    deep(1, tokens_here, k * steps),
                    deep(1, 2, k * steps),
                    wide(tokens_here),
                    wide(TAPS),
                    wide(tokens_here),
                    wide(tokens_here),
                    wide(tokens_here),
                    wide(owners, k * steps),
                ],
                out_specs=spec((cols * 16, LANES), lambda i: (i, 0)),
                out_shape=jax.ShapeDtypeStruct((part // LANES * 16, LANES), f32),
                scratch_shapes=[padded()],
                compiler_params=params(),
                name="sums",
            )(streams, edge, gated[k], before[k], inner[k], grads[k], mixed[k], gain_parts)
        )
    early = sum_over(jnp.concatenate(early, axis=0), "dp").reshape(channels // LANES, 16, LANES)

    stream_grad, late = None, []
    for k in range(chunks):
        aliased = stream_grad is not None
        operands = [streams, edge, short_filter, skip_row, behind_bands, grads[k], mixed[k], inner[k], after[k], following[k]]
        in_specs = [
            deep(3, tokens_here, k * steps),
            deep(3, 2, k * steps),
            deep(3, 3, k * steps),
            wide(1, k * steps),
            band(k * steps),
            wide(tokens_here),
            wide(tokens_here),
            wide(tokens_here),
            wide(TAPS),
            deep(3, 2),
        ]
        if aliased:
            operands.append(stream_grad)
            in_specs.append(pl.BlockSpec(memory_space=pl.ANY))
        stream_grad, late_k = pl.pallas_call(
            functools.partial(backward_kernel, aliased),
            grid=(steps,),
            in_specs=in_specs,
            out_specs=[
                deep(3, tokens_here, k * steps),
                spec((cols * 8, LANES), lambda i: (i, 0)),
            ],
            out_shape=[
                jax.ShapeDtypeStruct(streams.shape, bf16),
                jax.ShapeDtypeStruct((part // LANES * 8, LANES), f32),
            ],
            scratch_shapes=[padded(3), padded(3)],
            input_output_aliases={len(operands) - 1: 0} if aliased else {},
            compiler_params=params(),
            name="backward",
        )(*operands)
        late.append(late_k)
    late = sum_over(jnp.concatenate(late, axis=0), "dp").reshape(channels // LANES, 8, LANES)

    long_grad = early[:, :8].reshape(groups, TAPS)
    skip_grad = early[:, 8].reshape(channels)
    gain_grad = early[:, 9].reshape(channels)
    short_rows = jnp.concatenate([early[:, 10:13], late[:, :6]], axis=1)
    short_grad = jnp.swapaxes(short_rows, 0, 1).reshape(3, 3, channels)
    return (normed, grad_residual, stream_grad, long_grad, short_grad, skip_grad, gain_grad)


def solution(mesh):
    placed = (
        P(("dp", "tensor"), None),
        P(None, "dp", "tensor"),
        P(None, None, "tensor"),
        P("tensor", None),
        P("tensor"),
        P(),
        P(("dp", "tensor"), None),
    )
    return jax.shard_map(
        local,
        mesh=mesh,
        in_specs=placed,
        out_specs=(
            P(("dp", "tensor"), None),
            P(("dp", "tensor"), None),
            P(None, "dp", "tensor"),
            P("tensor", None),
            P(None, None, "tensor"),
            P("tensor"),
            P("tensor"),
        ),
        check_vma=False,
    )
```

time: 440 us -> 172 us (0.39)
  local copies, waits for them, and re-layouts: 217 us -> 33.6 us
  other arithmetic: 65.1 us -> 2.5 us
  waiting for transfers between devices: 75.5 us -> 18.1 us
  Pallas kernels: 0 us -> 40.6 us
  matrix products: 23 us -> 0 us
  blocking collectives: 13.1 us -> 31.2 us
  starting transfers between devices: 28.3 us -> 44.1 us
  between operations: 14.5 us -> 1.09 us
    reshape x13 -> x2, local copies, waits for them, and re-layouts: 113 us -> 1.3 us  [the longest x1 0.67 us: local(): short_grad = jnp.swapaxes(short_rows, 0, 1).reshape(3, 3, channels)]
    psum x1 -> x0, waiting for transfers between devices: 75.2 us -> none  [local(): lax.psum(filter_share.astype(jnp.bfloat16), 'dp').astype(jnp.float32)]
    pallas_call x0 -> x10, Pallas kernels: none -> 40.6 us  [the longest x2 10.6 us: local(): pl.pallas_call(functools.partial(backward_kernel, aliased), grid=(steps,)...]
    all_to_all x0 -> x3, blocking collectives: none -> 31.2 us  [the longest x1 12.3 us: local(): lax.all_to_all(output.reshape(owners, rows_here, part), 'tensor', split_a...]
    reduce_sum x5 -> x0, other arithmetic: 28.2 us -> none  [the longest x1 12.5 us: local(): jnp.sum(feature_grad * padded[:, 2 - offset:2 - offset + tokens_here], ax...]
    convert_element_type x6 -> x0, local copies, waits for them, and re-layouts: 23.9 us -> none  [the longest x2 10.6 us: local(): cot_float = cot_cols.astype(jnp.float32)]
    dot_general x3 -> x0, matrix products: 23 us -> none  [the longest x2 13.3 us: apply_band(): jnp.einsum('gij,bjgc->bigc', matrix, window_set, preferred_element_type=j...]
    slice x10 -> x7, local copies, waits for them, and re-layouts: 24 us -> 2.43 us  [the longest x1 1 us: local(): short_filter[1:, 0][:, None, :] * tail[:, 2:]]
  transfers between devices with their start and end apart: 9 -> 15, of which waited for: 2 -> 6; matrix products, arithmetic and copies ran while one was open for 61% -> 2% of each run, Pallas kernels for 0% -> 14%
where the time goes in v1:
time: 172 us; the launch traced here: 171 us
  starting transfers between devices  44.1 us (26%)
  Pallas kernels  40.6 us (24%)
  local copies, waits for them, and re-layouts  33.6 us (20%)
  blocking collectives  31.2 us (18%)
  waiting for transfers between devices  18.1 us (11%)
  other arithmetic  2.5 us (1%)
    unnamed x71, local copies, waits for them, and re-layouts  29.8 us
    ppermute x6, starting transfers between devices, sum_over(): lax.ppermute(value.astype(bf16), axis, [(i, i ^ reach) for i in range(cou...  18.7 us
    ppermute x7, starting transfers between devices, from_behind(): lax.ppermute(value, axis, [(source, source + steps) for source in range(f...  17.2 us
    all_to_all x1, blocking collectives, local(): lax.all_to_all(output.reshape(owners, rows_here, part), 'tensor', split_a...  12.3 us
    all_to_all x1, blocking collectives, local(): lax.all_to_all(piece, 'tensor', split_axis=0, concat_axis=0, tiled=True)  11.9 us
    pallas_call x2, Pallas kernels, local(): pl.pallas_call(functools.partial(backward_kernel, aliased), grid=(steps,)...  10.6 us
    ppermute x6, waiting for transfers between devices, sum_over(): lax.ppermute(value.astype(bf16), axis, [(i, i ^ reach) for i in range(cou...  10.1 us
    pallas_call x1, Pallas kernels, local(): pl.pallas_call(bands_kernel, grid=(groups // PER,), in_specs=[spec((PER,...  9.21 us
  transfers between devices with their start and end apart: 15, of which 6 were waited for; matrix products, arithmetic and copies ran while one was open for 2% of the time, Pallas kernels for 14%

profile of v1, /device:TPU:0, one launch (start us, length us, event | category | flops | bytes accessed | tf_op | source)
XLA Modules:
  0.0 171.2 jit_solution(10325847947363087874)
XLA Ops:
  0.6 1.0 fusion.12
  1.7 1.6 slice_convert_fusion
  4.8 5.0 %collective-permute-start.2 = (bf16[128,1024]{1,0:T(8,128)(2,1)S(1)}, bf16[128,1024]{1,0:T(8,128)(2,1)S(1)}, u32[]{:S(2)}, u32[]{:S(2)}) collective-permute-start(bf16[128,1024]{1,0:T(8,128)(2,1)S(1)} %get-tuple-element.49), channel_id=1, source_target_pairs={{0,4},{4,8},{8,12},{12,16},{16,20},{20,24},{24,28},{1,5},{5,9},{9,... | collective-permute-start | bytes 786440 | tf_op jit(solution)/shard_map/ppermute | solution.py:262
  9.8 3.4 %collective-permute-start = (bf16[3,2,2048]{2,1,0:T(2,128)(2,1)S(1)}, bf16[3,2,2048]{2,1,0:T(2,128)(2,1)S(1)}, u32[]{:S(2)}, u32[]{:S(2)}) collective-permute-start(bf16[3,2,2048]{2,1,0:T(2,128)(2,1)S(1)} %slice.57), channel_id=1, source_target_pairs={{0,4},{4,8},{8,12},{12,16},{16,20},{20,24},{24,28},{1,5},{5,9},{9,... | collective-permute-start | bytes 73736 | tf_op jit(solution)/shard_map/ppermute | solution.py:262
  13.3 9.2 %bands.1 = (bf16[128,128,256]{2,1,0:T(8,128)(2,1)S(1)}, bf16[128,128,256]{2,1,0:T(8,128)(2,1)}) custom-call(f32[128,128]{1,0:T(8,128)S(1)} %copy-done.30), custom_call_target="tpu_custom_call" | custom-call | tf_op jit(solution)/shard_map/bands/pallas_call | solution.py:316
  22.5 2.4 %forward.3 = (bf16[256,1024]{1,0:T(8,128)(2,1)S(1)}, f32[256,1024]{1,0:T(8,128)S(1)}, bf16[256,1024]{1,0:T(8,128)(2,1)S(1)}) custom-call(bf16[3,256,2048]{2,1,0:T(8,128)(2,1)S(1)} %copy-done, bf16[3,2,2048]{2,1,0:T(2,128)(2,1)S(1)} %collective-permute-done.edge_ref, bf16[128,1024]{1,0:T(8,128)(2,1)S(1)} %collective-permute-done.2.before_ref, ...), custom_call_target="tpu_custom_call" | custom-call | tf_op jit(solution)/shard_map/forward/pallas_call | solution.py:328
  25.8 1.0 copy-done.6
  28.4 4.1 %all-to-all-start.1 = ((bf16[4,64,1024]{2,1,0:T(8,128)(2,1)}), bf16[4,64,1024]{2,1,0:T(8,128)(2,1)}, u32[]{:S(2)}, u32[]{:S(2)}) async-start(bf16[4,64,1024]{2,1,0:T(8,128)(2,1)} %bitcast.32), calls=%async_computation.1 | async-start | bytes 1048576 | tf_op jit(solution)/shard_map/all_to_all | solution.py:348
  32.6 3.4 %collective-permute-start.1 = (bf16[128,1024]{1,0:T(8,128)(2,1)}, bf16[128,1024]{1,0:T(8,128)(2,1)S(1)}, u32[]{:S(2)}, u32[]{:S(2)}) collective-permute-start(bf16[128,1024]{1,0:T(8,128)(2,1)} %get-tuple-element.50), channel_id=1, source_target_pairs={{0,4},{4,8},{8,12},{12,16},{16,20},{20,24},{24,28},{1,5},{5,9},{9,... | collective-permute-start | bytes 786440 | tf_op jit(solution)/shard_map/ppermute | solution.py:262
  36.0 6.5 %collective-permute-done.1.before_ref = bf16[128,1024]{1,0:T(8,128)(2,1)S(1)} collective-permute-done((bf16[128,1024]{1,0:T(8,128)(2,1)}, bf16[128,1024]{1,0:T(8,128)(2,1)S(1)}, u32[]{:S(2)}, u32[]{:S(2)}) %collective-permute-start.1) | collective-permute-done | bytes 262176 | tf_op jit(solution)/shard_map/ppermute | solution.py:262
  42.5 3.4 %copy-done.5 = bf16[128,128,256]{2,1,0:T(8,128)(2,1)S(1)} copy-done((bf16[128,128,256]{2,1,0:T(8,128)(2,1)S(1)}, bf16[128,128,256]{2,1,0:T(8,128)(2,1)}, u32[]{:S(2)}) %copy-start.5) | copy-done | bytes 8388632
  45.9 2.4 %forward.2 = (bf16[256,1024]{1,0:T(8,128)(2,1)S(1)}, f32[256,1024]{1,0:T(8,128)S(1)}, bf16[256,1024]{1,0:T(8,128)(2,1)S(1)}) custom-call(bf16[3,256,2048]{2,1,0:T(8,128)(2,1)S(1)} %copy-done, bf16[3,2,2048]{2,1,0:T(2,128)(2,1)S(1)} %collective-permute-done.edge_ref, bf16[128,1024]{1,0:T(8,128)(2,1)S(1)} %collective-permute-done.1.before_ref, ...), custom_call_target="tpu_custom_call" | custom-call | tf_op jit(solution)/shard_map/forward/pallas_call | solution.py:328
  48.3 1.0 copy-done.9
  51.5 12.3 %all_to_all.31.refs_0_ = bf16[4,64,1024]{2,1,0:T(8,128)(2,1)S(1)} all-to-all(bf16[4,64,1024]{2,1,0:T(8,128)(2,1)} %bitcast.33), channel_id=1, replica_groups=mesh['dp'=8,'tensor'=4] {'tensor'}, dimensions={0} | all-to-all | bytes 1048576 | tf_op jit(solution)/shard_map/all_to_all | solution.py:348
  63.8 1.2 copy-done.17
  65.0 1.2 copy-done.18
  67.0 4.3 %norm.1 = (bf16[64,8192]{1,0:T(8,128)(2,1)}, bf16[64,8192]{1,0:T(8,128)(2,1)}, bf16[4,64,1024]{2,1,0:T(8,128)(2,1)S(1)}, bf16[4,64,1024]{2,1,0:T(8,128)(2,1)S(1)}, f32[1,8192]{1,0:T(1,128)S(1)}) custom-call(bf16[4,64,1024]{2,1,0:T(8,128)(2,1)S(1)} %all_to_all.31.refs_0_, bf16[4,64,1024]{2,1,0:T(8,128)(2,1)} %all-to-all-done.1.refs_1_, ...), custom_call_target="tpu_custom_call" | custom-call | tf_op jit(solution)/shard_map/norm/pallas_call | solution.py:355
  71.3 7.0 %all_to_all.32 = f32[4,1,2048]{2,1,0:T(1,128)} all-to-all(f32[4,1,2048]{2,1,0:T(1,128)S(1)} %bitcast.43), channel_id=1, replica_groups=mesh['dp'=8,'tensor'=4] {'tensor'}, dimensions={0} | all-to-all | bytes 65536 | tf_op jit(solution)/shard_map/all_to_all | solution.py:373
  78.3 11.9 %all_to_all.33 = bf16[4,64,1024]{2,1,0:T(8,128)(2,1)} all-to-all(bf16[4,64,1024]{2,1,0:T(8,128)(2,1)S(1)} %get-tuple-element.38), channel_id=1, replica_groups=mesh['dp'=8,'tensor'=4] {'tensor'}, dimensions={0} | all-to-all | bytes 1048576 | tf_op jit(solution)/shard_map/all_to_all | solution.py:370
  90.2 4.1 %all-to-all-start.2 = ((bf16[4,64,1024]{2,1,0:T(8,128)(2,1)}), bf16[4,64,1024]{2,1,0:T(8,128)(2,1)}, u32[]{:S(2)}, u32[]{:S(2)}) async-start(bf16[4,64,1024]{2,1,0:T(8,128)(2,1)} %copy-done.26), calls=%async_computation.2 | async-start | bytes 1048576 | tf_op jit(solution)/shard_map/all_to_all | solution.py:370
  94.4 1.4 copy.27
  95.8 3.4 %copy-done.1 = bf16[128,128,256]{2,1,0:T(8,128)(2,1)S(1)} copy-done((bf16[128,128,256]{2,1,0:T(8,128)(2,1)S(1)}, bf16[128,128,256]{2,1,0:T(8,128)(2,1)}, u32[]{:S(2)}) %copy-start.1) | copy-done | bytes 8388632
  99.1 1.2 copy-done.10
  100.4 1.0 copy-done.12
  101.4 1.0 head.3
  103.9 3.4 %copy-done.2 = bf16[128,128,256]{2,1,0:T(8,128)(2,1)S(1)} copy-done((bf16[128,128,256]{2,1,0:T(8,128)(2,1)S(1)}, bf16[128,128,256]{2,1,0:T(8,128)(2,1)}, u32[]{:S(2)}) %copy-start.2) | copy-done | bytes 8388632
  107.2 1.2 copy-done.7
  108.5 2.0 %head.2 = (bf16[256,1024]{1,0:T(8,128)(2,1)S(1)}, f32[3,2,1024]{2,1,0:T(2,128)S(1)}) custom-call(bf16[3,256,2048]{2,1,0:T(8,128)(2,1)S(1)} %copy-done, bf16[3,2,2048]{2,1,0:T(2,128)(2,1)S(1)} %collective-permute-done.edge_ref, f32[3,3,2048]{2,1,0:T(4,128)S(1)} %copy-done.14, f32[1,2048]{1,0:T(1,128)S(1)} %bitcast.39, bf16[128,128,256]{2,1,0:T(8,128)(2,1)S(1)} %copy-done.2, ...), custom_call_target="tpu_custom_call" | custom-call | tf_op jit(solution)/shard_map/head/pallas_call | solution.py:379
  110.6 3.9 %sums.2 = f32[128,128]{1,0:T(8,128)S(1)} custom-call(bf16[3,256,2048]{2,1,0:T(8,128)(2,1)S(1)} %copy-done, bf16[3,2,2048]{2,1,0:T(2,128)(2,1)S(1)} %collective-permute-done.edge_ref, bf16[256,1024]{1,0:T(8,128)(2,1)S(1)} %copy-done.24, bf16[128,1024]{1,0:T(8,128)(2,1)S(1)} %copy-done.20, bf16[256,1024]{1,0:T(8,128)(2,1)S(1)} %copy-done.16, ...), custom_call_target="tpu_custom_call" | custom-call | tf_op jit(solution)/shard_map/sums/pallas_call | solution.py:407
  114.5 4.7 %sums.3 = f32[128,128]{1,0:T(8,128)S(1)} custom-call(bf16[3,256,2048]{2,1,0:T(8,128)(2,1)S(1)} %copy-done, bf16[3,2,2048]{2,1,0:T(2,128)(2,1)S(1)} %collective-permute-done.edge_ref, bf16[256,1024]{1,0:T(8,128)(2,1)S(1)} %copy-done.22, bf16[128,1024]{1,0:T(8,128)(2,1)S(1)} %collective-permute-done.2.before_ref, ...), custom_call_target="tpu_custom_call" | custom-call | tf_op jit(solution)/shard_map/sums/pallas_call | solution.py:407
  119.2 2.4 %collective-permute-start.7 = (bf16[256,128]{1,0:T(8,128)(2,1)S(1)}, bf16[256,128]{1,0:T(8,128)(2,1)S(1)}, u32[]{:S(2)}, u32[]{:S(2)}) collective-permute-start(bf16[256,128]{1,0:T(8,128)(2,1)S(1)} %fusion.4), channel_id=1, source_target_pairs={{0,4},{4,0},{8,12},{12,8},{16,20},{20,16},{24,28},{28,24},{1,5},{5... | collective-permute-start | bytes 196616 | tf_op jit(solution)/shard_map/ppermute | solution.py:269
  121.7 2.7 %collective-permute-done.7 = bf16[256,128]{1,0:T(8,128)(2,1)S(1)} collective-permute-done((bf16[256,128]{1,0:T(8,128)(2,1)S(1)}, bf16[256,128]{1,0:T(8,128)(2,1)S(1)}, u32[]{:S(2)}, u32[]{:S(2)}) %collective-permute-start.7) | collective-permute-done | bytes 65568 | tf_op jit(solution)/shard_map/ppermute | solution.py:269
  124.4 2.8 %collective-permute-start.8 = (bf16[256,128]{1,0:T(8,128)(2,1)S(1)}, bf16[256,128]{1,0:T(8,128)(2,1)S(1)}, u32[]{:S(2)}, u32[]{:S(2)}) collective-permute-start(bf16[256,128]{1,0:T(8,128)(2,1)S(1)} %fusion.9), channel_id=1, source_target_pairs={{0,8},{4,12},{8,0},{12,4},{16,24},{20,28},{24,16},{28,20},{1,9},{5... | collective-permute-start | bytes 196616 | tf_op jit(solution)/shard_map/ppermute | solution.py:269
  127.2 1.3 collective-permute-start.5
  128.5 1.3 collective-permute-start.3
  129.8 1.3 collective-permute-start.6
  131.1 1.5 collective-permute-start.4
  132.7 8.9 %collective-permute-start.9 = (bf16[256,128]{1,0:T(8,128)(2,1)S(1)}, bf16[256,128]{1,0:T(8,128)(2,1)S(1)}, u32[]{:S(2)}, u32[]{:S(2)}) collective-permute-start(bf16[256,128]{1,0:T(8,128)(2,1)S(1)} %fusion.5), channel_id=1, source_target_pairs={{0,16},{4,20},{8,24},{12,28},{16,0},{20,4},{24,8},{28,12},{1,17},{... | collective-permute-start | bytes 196616 | tf_op jit(solution)/shard_map/ppermute | solution.py:269
  141.6 1.5 collective-permute-done.6.next_ref
  143.1 3.4 %copy-done.3 = bf16[128,128,256]{2,1,0:T(8,128)(2,1)S(1)} copy-done((bf16[128,128,256]{2,1,0:T(8,128)(2,1)S(1)}, bf16[128,128,256]{2,1,0:T(8,128)(2,1)}, u32[]{:S(2)}) %copy-start.3) | copy-done | bytes 8388632
  146.5 4.9 %backward.2 = (bf16[3,256,2048]{2,1,0:T(8,128)(2,1)}, f32[64,128]{1,0:T(8,128)S(1)}) custom-call(bf16[3,256,2048]{2,1,0:T(8,128)(2,1)S(1)} %copy-done, bf16[3,2,2048]{2,1,0:T(2,128)(2,1)S(1)} %collective-permute-done.edge_ref, f32[3,3,2048]{2,1,0:T(4,128)S(1)} %copy-done.14, f32[1,2048]{1,0:T(1,128)S(1)} %bitcast.40, bf16[128,128,256]{2,1,0:T(8,128)(2,1)S(1)} %copy-done.3, ...), custom_call_target="tpu_custom_call" | custom-call | tf_op jit(solution)/shard_map/backward/pallas_call | solution.py:448
  151.4 5.7 %backward.3 = (bf16[3,256,2048]{2,1,0:T(8,128)(2,1)}, f32[64,128]{1,0:T(8,128)S(1)}) custom-call(bf16[3,256,2048]{2,1,0:T(8,128)(2,1)S(1)} %copy-done, bf16[3,2,2048]{2,1,0:T(2,128)(2,1)S(1)} %collective-permute-done.edge_ref, f32[3,3,2048]{2,1,0:T(4,128)S(1)} %copy-done.14, f32[1,2048]{1,0:T(1,128)S(1)} %bitcast.41, ...), custom_call_target="tpu_custom_call", output_to_operand_aliasing={{0}: (10, {})} | custom-call | tf_op jit(solution)/shard_map/backward/pallas_call | solution.py:448
  157.2 2.1 %collective-permute-start.10 = (bf16[128,128]{1,0:T(8,128)(2,1)S(1)}, bf16[128,128]{1,0:T(8,128)(2,1)S(1)}, u32[]{:S(2)}, u32[]{:S(2)}) collective-permute-start(bf16[128,128]{1,0:T(8,128)(2,1)S(1)} %fusion.6), channel_id=1, source_target_pairs={{0,4},{4,0},{8,12},{12,8},{16,20},{20,16},{24,28},{28,24},{1,5},{5... | collective-permute-start | bytes 98312 | tf_op jit(solution)/shard_map/ppermute | solution.py:269
  159.3 1.8 %collective-permute-done.10 = bf16[128,128]{1,0:T(8,128)(2,1)S(1)} collective-permute-done((bf16[128,128]{1,0:T(8,128)(2,1)S(1)}, bf16[128,128]{1,0:T(8,128)(2,1)S(1)}, u32[]{:S(2)}, u32[]{:S(2)}) %collective-permute-start.10) | collective-permute-done | bytes 32800 | tf_op jit(solution)/shard_map/ppermute | solution.py:269
  161.2 1.3 collective-permute-start.11
  163.1 2.4 %collective-permute-done.11 = bf16[128,128]{1,0:T(8,128)(2,1)S(1)} collective-permute-done((bf16[128,128]{1,0:T(8,128)(2,1)S(1)}, bf16[128,128]{1,0:T(8,128)(2,1)S(1)}, u32[]{:S(2)}, u32[]{:S(2)}) %collective-permute-start.11) | collective-permute-done | bytes 32800 | tf_op jit(solution)/shard_map/ppermute | solution.py:269
  165.6 1.1 collective-permute-start.12
  167.3 3.2 %collective-permute-done.12 = bf16[128,128]{1,0:T(8,128)(2,1)S(1)} collective-permute-done((bf16[128,128]{1,0:T(8,128)(2,1)S(1)}, bf16[128,128]{1,0:T(8,128)(2,1)S(1)}, u32[]{:S(2)}, u32[]{:S(2)}) %collective-permute-start.12) | collective-permute-done | bytes 32800 | tf_op jit(solution)/shard_map/ppermute | solution.py:269
  (88 shorter events, 10.7 us)
Async XLA Ops:
  3.9 5.9 %copy-start = (bf16[3,256,2048]{2,1,0:T(8,128)(2,1)S(1)}, bf16[3,256,2048]{2,1,0:T(8,128)(2,1)}, u32[]{:S(2)}) copy-start(bf16[3,256,2048]{2,1,0:T(8,128)(2,1)} %streams_ref.15) | copy-start | bytes 9437188
  3.9 9.4 %copy-start.30 = (f32[128,128]{1,0:T(8,128)S(1)}, f32[128,128]{1,0:T(8,128)}, u32[]{:S(2)}) copy-start(f32[128,128]{1,0:T(8,128)} %filter_ref.1) | copy-start | bytes 196612
  3.9 18.6 %copy-start.14 = (f32[3,3,2048]{2,1,0:T(4,128)S(1)}, f32[3,3,2048]{2,1,0:T(4,128)}, u32[]{:S(2)}) copy-start(f32[3,3,2048]{2,1,0:T(4,128)} %taps_ref.11) | copy-start | bytes 221188
  3.9 18.6 %copy-start.29 = (f32[2048]{0:T(1024)S(1)}, f32[2048]{0:T(1024)}, u32[]{:S(2)}) copy-start(f32[2048]{0:T(1024)} %param.11) | copy-start | bytes 24580
  4.8 17.7 %collective-permute-start.2 = (bf16[128,1024]{1,0:T(8,128)(2,1)S(1)}, bf16[128,1024]{1,0:T(8,128)(2,1)S(1)}, u32[]{:S(2)}, u32[]{:S(2)}) collective-permute-start(bf16[128,1024]{1,0:T(8,128)(2,1)S(1)} %get-tuple-element.49), channel_id=1, source_target_pairs={{0,4},{4,8},{8,12},{12,16},{16,20},{20,24},{24,28},{1,5},{5,9},{9,... | collective-permute-start | bytes 786440 | tf_op jit(solution)/shard_map/ppermute | solution.py:262
  9.8 12.7 %collective-permute-start = (bf16[3,2,2048]{2,1,0:T(2,128)(2,1)S(1)}, bf16[3,2,2048]{2,1,0:T(2,128)(2,1)S(1)}, u32[]{:S(2)}, u32[]{:S(2)}) collective-permute-start(bf16[3,2,2048]{2,1,0:T(2,128)(2,1)S(1)} %slice.57), channel_id=1, source_target_pairs={{0,4},{4,8},{8,12},{12,16},{16,20},{20,24},{24,28},{1,5},{5,9},{9,... | collective-permute-start | bytes 73736 | tf_op jit(solution)/shard_map/ppermute | solution.py:262
  22.5 3.3 %copy-start.4 = (bf16[128,128,256]{2,1,0:T(8,128)(2,1)}, bf16[128,128,256]{2,1,0:T(8,128)(2,1)S(1)}, u32[]{:S(2)}) copy-start(bf16[128,128,256]{2,1,0:T(8,128)(2,1)S(1)} %get-tuple-element.28.ahead_ref) | copy-start | bytes 25165828
  25.8 1.0 copy-start.6
  26.8 0.8 copy-start.21
  27.6 0.8 copy-start.25
  28.4 23.1 %all-to-all-start.1 = ((bf16[4,64,1024]{2,1,0:T(8,128)(2,1)}), bf16[4,64,1024]{2,1,0:T(8,128)(2,1)}, u32[]{:S(2)}, u32[]{:S(2)}) async-start(bf16[4,64,1024]{2,1,0:T(8,128)(2,1)} %bitcast.32), calls=%async_computation.1 | async-start | bytes 1048576 | tf_op jit(solution)/shard_map/all_to_all | solution.py:348
  32.6 9.9 %collective-permute-start.1 = (bf16[128,1024]{1,0:T(8,128)(2,1)}, bf16[128,1024]{1,0:T(8,128)(2,1)S(1)}, u32[]{:S(2)}, u32[]{:S(2)}) collective-permute-start(bf16[128,1024]{1,0:T(8,128)(2,1)} %get-tuple-element.50), channel_id=1, source_target_pairs={{0,4},{4,8},{8,12},{12,16},{16,20},{20,24},{24,28},{1,5},{5,9},{9,... | collective-permute-start | bytes 786440 | tf_op jit(solution)/shard_map/ppermute | solution.py:262
  42.5 3.4 %copy-start.5 = (bf16[128,128,256]{2,1,0:T(8,128)(2,1)S(1)}, bf16[128,128,256]{2,1,0:T(8,128)(2,1)}, u32[]{:S(2)}) copy-start(bf16[128,128,256]{2,1,0:T(8,128)(2,1)} %copy-done.4) | copy-start | bytes 25165828
  48.3 1.0 copy-start.9
  49.2 0.7 copy-start.19
  49.9 0.8 copy-start.23
  50.7 0.8 copy-start.27
  63.8 1.2 copy-start.17
  65.0 1.2 copy-start.18
  66.3 0.8 copy-start.31
  71.3 18.9 %copy-start.26 = (bf16[4,64,1024]{2,1,0:T(8,128)(2,1)}, bf16[4,64,1024]{2,1,0:T(8,128)(2,1)S(1)}, u32[]{:S(2)}) copy-start(bf16[4,64,1024]{2,1,0:T(8,128)(2,1)S(1)} %get-tuple-element.34) | copy-start | bytes 1572868
  90.2 13.6 %all-to-all-start.2 = ((bf16[4,64,1024]{2,1,0:T(8,128)(2,1)}), bf16[4,64,1024]{2,1,0:T(8,128)(2,1)}, u32[]{:S(2)}, u32[]{:S(2)}) async-start(bf16[4,64,1024]{2,1,0:T(8,128)(2,1)} %copy-done.26), calls=%async_computation.2 | async-start | bytes 1048576 | tf_op jit(solution)/shard_map/all_to_all | solution.py:370
  95.8 3.4 %copy-start.1 = (bf16[128,128,256]{2,1,0:T(8,128)(2,1)S(1)}, bf16[128,128,256]{2,1,0:T(8,128)(2,1)}, u32[]{:S(2)}) copy-start(bf16[128,128,256]{2,1,0:T(8,128)(2,1)} %get-tuple-element.33.behind_ref) | copy-start | bytes 25165828
  99.1 1.2 copy-start.10
  100.4 1.0 copy-start.12
  102.4 0.8 copy-start.15
  103.9 3.4 %copy-start.2 = (bf16[128,128,256]{2,1,0:T(8,128)(2,1)S(1)}, bf16[128,128,256]{2,1,0:T(8,128)(2,1)}, u32[]{:S(2)}) copy-start(bf16[128,128,256]{2,1,0:T(8,128)(2,1)} %get-tuple-element.33.behind_ref) | copy-start | bytes 25165828
  107.2 1.2 copy-start.7
  108.5 2.0 %copy-start.11 = (f32[256,1024]{1,0:T(8,128)S(1)}, f32[256,1024]{1,0:T(8,128)}, u32[]{:S(2)}) copy-start(f32[256,1024]{1,0:T(8,128)} %copy-done.9) | copy-start | bytes 3145732
  108.5 2.0 %copy-start.13 = (bf16[4,64,1024]{2,1,0:T(8,128)(2,1)S(1)}, bf16[4,64,1024]{2,1,0:T(8,128)(2,1)}, u32[]{:S(2)}) copy-start(bf16[4,64,1024]{2,1,0:T(8,128)(2,1)} %all_to_all.33) | copy-start | bytes 1572868
  108.5 2.1 %copy-start.16 = (bf16[256,1024]{1,0:T(8,128)(2,1)S(1)}, bf16[256,1024]{1,0:T(8,128)(2,1)}, u32[]{:S(2)}) copy-start(bf16[256,1024]{1,0:T(8,128)(2,1)} %copy-done.15) | copy-start | bytes 1572868
  108.5 2.1 %copy-start.20 = (bf16[128,1024]{1,0:T(8,128)(2,1)S(1)}, bf16[128,1024]{1,0:T(8,128)(2,1)}, u32[]{:S(2)}) copy-start(bf16[128,1024]{1,0:T(8,128)(2,1)} %copy-done.19) | copy-start | bytes 786436
  108.5 2.1 %copy-start.24 = (bf16[256,1024]{1,0:T(8,128)(2,1)S(1)}, bf16[256,1024]{1,0:T(8,128)(2,1)}, u32[]{:S(2)}) copy-start(bf16[256,1024]{1,0:T(8,128)(2,1)} %copy-done.23) | copy-start | bytes 1572868
  108.5 2.1 %copy-start.28 = (f32[4,1,2048]{2,0,1:T(4,128)S(1)}, f32[4,1,2048]{2,0,1:T(4,128)}, u32[]{:S(2)}) copy-start(f32[4,1,2048]{2,0,1:T(4,128)} %copy.27) | copy-start | bytes 98308
  110.6 3.9 %copy-start.22 = (bf16[256,1024]{1,0:T(8,128)(2,1)S(1)}, bf16[256,1024]{1,0:T(8,128)(2,1)}, u32[]{:S(2)}) copy-start(bf16[256,1024]{1,0:T(8,128)(2,1)} %copy-done.21) | copy-start | bytes 1572868
  114.5 15.3 %copy-start.33 = (f32[3,2,1024]{2,1,0:T(2,128)S(1)}, f32[3,2,1024]{2,1,0:T(2,128)}, u32[]{:S(2)}) copy-start(f32[3,2,1024]{2,1,0:T(2,128)} %copy-done.32) | copy-start | bytes 73732
  119.2 5.2 %collective-permute-start.7 = (bf16[256,128]{1,0:T(8,128)(2,1)S(1)}, bf16[256,128]{1,0:T(8,128)(2,1)S(1)}, u32[]{:S(2)}, u32[]{:S(2)}) collective-permute-start(bf16[256,128]{1,0:T(8,128)(2,1)S(1)} %fusion.4), channel_id=1, source_target_pairs={{0,4},{4,0},{8,12},{12,8},{16,20},{20,16},{24,28},{28,24},{1,5},{5... | collective-permute-start | bytes 196616 | tf_op jit(solution)/shard_map/ppermute | solution.py:269
  124.4 8.2 %collective-permute-start.8 = (bf16[256,128]{1,0:T(8,128)(2,1)S(1)}, bf16[256,128]{1,0:T(8,128)(2,1)S(1)}, u32[]{:S(2)}, u32[]{:S(2)}) collective-permute-start(bf16[256,128]{1,0:T(8,128)(2,1)S(1)} %fusion.9), channel_id=1, source_target_pairs={{0,8},{4,12},{8,0},{12,4},{16,24},{20,28},{24,16},{28,20},{1,9},{5... | collective-permute-start | bytes 196616 | tf_op jit(solution)/shard_map/ppermute | solution.py:269
  127.2 15.9 %collective-permute-start.5 = (bf16[128,1024]{1,0:T(8,128)(2,1)S(1)}, bf16[128,1024]{1,0:T(8,128)(2,1)S(1)}, u32[]{:S(2)}, u32[]{:S(2)}) collective-permute-start(bf16[128,1024]{1,0:T(8,128)(2,1)S(1)} %slice.70), channel_id=1, source_target_pairs={{4,0},{8,4},{12,8},{16,12},{20,16},{24,20},{28,24},{5,1},{9,5},{13... | collective-permute-start | bytes 786440 | tf_op jit(solution)/shard_map/ppermute | solution.py:262
  128.5 22.9 %collective-permute-start.3 = (bf16[128,1024]{1,0:T(8,128)(2,1)S(1)}, bf16[128,1024]{1,0:T(8,128)(2,1)S(1)}, u32[]{:S(2)}, u32[]{:S(2)}) collective-permute-start(bf16[128,1024]{1,0:T(8,128)(2,1)S(1)} %slice.69), channel_id=1, source_target_pairs={{4,0},{8,4},{12,8},{16,12},{20,16},{24,20},{28,24},{5,1},{9,5},{13... | collective-permute-start | bytes 786440 | tf_op jit(solution)/shard_map/ppermute | solution.py:262
  129.8 13.3 %collective-permute-start.6 = (f32[3,2,1024]{2,1,0:T(2,128)S(1)}, f32[3,2,1024]{2,1,0:T(2,128)S(1)}, u32[]{:S(2)}, u32[]{:S(2)}) collective-permute-start(f32[3,2,1024]{2,1,0:T(2,128)S(1)} %copy-done.33), channel_id=1, source_target_pairs={{4,0},{8,4},{12,8},{16,12},{20,16},{24,20},{28,24},{5,1},{9,5},{13... | collective-permute-start | bytes 73736 | tf_op jit(solution)/shard_map/ppermute | solution.py:262
  131.1 20.3 %collective-permute-start.4 = (f32[3,2,1024]{2,1,0:T(2,128)S(1)}, f32[3,2,1024]{2,1,0:T(2,128)S(1)}, u32[]{:S(2)}, u32[]{:S(2)}) collective-permute-start(f32[3,2,1024]{2,1,0:T(2,128)S(1)} %get-tuple-element.37), channel_id=1, source_target_pairs={{4,0},{8,4},{12,8},{16,12},{20,16},{24,20},{28,24},{5,1},{9,5},{13... | collective-permute-start | bytes 73736 | tf_op jit(solution)/shard_map/ppermute | solution.py:262
  132.7 26.6 %collective-permute-start.9 = (bf16[256,128]{1,0:T(8,128)(2,1)S(1)}, bf16[256,128]{1,0:T(8,128)(2,1)S(1)}, u32[]{:S(2)}, u32[]{:S(2)}) collective-permute-start(bf16[256,128]{1,0:T(8,128)(2,1)S(1)} %fusion.5), channel_id=1, source_target_pairs={{0,16},{4,20},{8,24},{12,28},{16,0},{20,4},{24,8},{28,12},{1,17},{... | collective-permute-start | bytes 196616 | tf_op jit(solution)/shard_map/ppermute | solution.py:269
  143.1 3.4 %copy-start.3 = (bf16[128,128,256]{2,1,0:T(8,128)(2,1)S(1)}, bf16[128,128,256]{2,1,0:T(8,128)(2,1)}, u32[]{:S(2)}) copy-start(bf16[128,128,256]{2,1,0:T(8,128)(2,1)} %get-tuple-element.33.behind_ref) | copy-start | bytes 25165828
  146.5 4.9 %copy-start.8 = (f32[256,1024]{1,0:T(8,128)S(1)}, f32[256,1024]{1,0:T(8,128)}, u32[]{:S(2)}) copy-start(f32[256,1024]{1,0:T(8,128)} %copy-done.6) | copy-start | bytes 3145732
  157.2 4.0 %collective-permute-start.10 = (bf16[128,128]{1,0:T(8,128)(2,1)S(1)}, bf16[128,128]{1,0:T(8,128)(2,1)S(1)}, u32[]{:S(2)}, u32[]{:S(2)}) collective-permute-start(bf16[128,128]{1,0:T(8,128)(2,1)S(1)} %fusion.6), channel_id=1, source_target_pairs={{0,4},{4,0},{8,12},{12,8},{16,20},{20,16},{24,28},{28,24},{1,5},{5... | collective-permute-start | bytes 98312 | tf_op jit(solution)/shard_map/ppermute | solution.py:269
  161.2 4.3 %collective-permute-start.11 = (bf16[128,128]{1,0:T(8,128)(2,1)S(1)}, bf16[128,128]{1,0:T(8,128)(2,1)S(1)}, u32[]{:S(2)}, u32[]{:S(2)}) collective-permute-start(bf16[128,128]{1,0:T(8,128)(2,1)S(1)} %fusion.8), channel_id=1, source_target_pairs={{0,8},{4,12},{8,0},{12,4},{16,24},{20,28},{24,16},{28,20},{1,9},{5... | collective-permute-start | bytes 98312 | tf_op jit(solution)/shard_map/ppermute | solution.py:269
  165.6 4.9 %collective-permute-start.12 = (bf16[128,128]{1,0:T(8,128)(2,1)S(1)}, bf16[128,128]{1,0:T(8,128)(2,1)S(1)}, u32[]{:S(2)}, u32[]{:S(2)}) collective-permute-start(bf16[128,128]{1,0:T(8,128)(2,1)S(1)} %fusion.7), channel_id=1, source_target_pairs={{0,16},{4,20},{8,24},{12,28},{16,0},{20,4},{24,8},{28,12},{1,17},{... | collective-permute-start | bytes 98312 | tf_op jit(solution)/shard_map/ppermute | solution.py:269
  (1 other events, 0.6 us)

commit v2 on v1

v2 whole, which is shorter than its diff:
```python
import functools

import jax
import jax.numpy as jnp
from jax import lax
from jax.experimental import pallas as pl
from jax.experimental.pallas import tpu as pltpu
from jax.sharding import PartitionSpec as P

norm_eps = 1e-05
LANES = 128
TAPS = 128
WIDTH = 16
PER = LANES // WIDTH
BLOCK = 64
SPAN = 256
VMEM_LIMIT = 56 * 2**20
f32 = jnp.float32
bf16 = jnp.bfloat16


def params():
    return pltpu.CompilerParams(vmem_limit_bytes=VMEM_LIMIT)


def dot(a, b):
    return lax.dot_general(a, b, (((1,), (0,)), ((), ())), preferred_element_type=f32)


def dot_nt(a, b):
    return lax.dot_general(a, b, (((1,), (1,)), ((), ())), preferred_element_type=f32)


def lane_group(shape):
    return lax.broadcasted_iota(jnp.int32, shape, len(shape) - 1) % LANES // WIDTH


def pick_groups(stacked, rows):
    out = stacked[:rows]
    which = lane_group(out.shape)
    for g in range(1, PER):
        out = jnp.where(which == g, stacked[g * rows : (g + 1) * rows], out)
    return out


def shifted(scratch, halo, current):
    length = current.shape[0]
    scratch[6:8, :] = halo
    scratch[8 : 8 + length, :] = current
    return scratch[7 : 7 + length, :], scratch[6 : 6 + length, :]


def band(row, first, rows):
    wide = jnp.concatenate([row, jnp.zeros((1, SPAN - TAPS), f32)], axis=1)
    return pltpu.roll(jnp.broadcast_to(wide, (rows, SPAN)), first, 1, stride=1, stride_axis=0).astype(bf16)


def anti_identity(size):
    total = lax.broadcasted_iota(jnp.int32, (size, size), 0) + lax.broadcasted_iota(jnp.int32, (size, size), 1)
    return jnp.where(total == size - 1, 1.0, 0.0).astype(bf16)


def windows(extended, length):
    return jnp.concatenate([extended[at : at + SPAN] for at in range(0, length, BLOCK)], axis=1)


def convolve(bands, extended, length, rows=BLOCK):
    stacked = dot(bands.reshape(PER * rows, SPAN), windows(extended, length))
    result = pick_groups(stacked, rows)
    return [result[:, at : at + LANES] for at in range(0, result.shape[1], LANES)]


def bands_kernel(filter_ref, ahead_ref, behind_ref):
    half = filter_ref[...].astype(bf16)
    back = dot(half, anti_identity(TAPS))
    fore = half.astype(f32)
    for g in range(half.shape[0]):
        ahead_ref[g] = band(back[g : g + 1], SPAN - TAPS - BLOCK + 1, BLOCK)
        behind_ref[g] = band(fore[g : g + 1], 0, BLOCK)


def open_kernel(
    cot_ref, residual_ref, last0_ref, last1_ref, last2_ref, prior1_ref, prior2_ref, taps_ref, packed_ref, halo_ref, scratch
):
    owners, _, _, channels = packed_ref.shape
    for j in range(owners):
        where = slice(j * channels, (j + 1) * channels)
        packed_ref[j, 0] = cot_ref[:, where]
        packed_ref[j, 1] = residual_ref[:, where]
    for col in range(halo_ref.shape[1] // LANES):
        lanes = slice(col * LANES, (col + 1) * LANES)
        features = []
        for s, last, prior in ((1, last1_ref, prior1_ref), (2, last2_ref, prior2_ref)):
            now = last[0, :, lanes].astype(f32)
            one, two = shifted(scratch.at[s], prior[0, :, lanes].astype(f32)[14:], now)
            taps = taps_ref[s, :, lanes]
            features.append(taps[0:1] * now + taps[1:2] * one + taps[2:3] * two)
        halo_ref[:TAPS, lanes] = (features[0] * features[1]).astype(bf16)
        edges = scratch.at[0]
        edges[0:2, :] = last0_ref[0, :, lanes].astype(f32)[14:]
        edges[2:4, :] = scratch[1, TAPS + 6 : TAPS + 8, :]
        edges[4:6, :] = scratch[2, TAPS + 6 : TAPS + 8, :]
        edges[6:8, :] = jnp.zeros((2, LANES), f32)
        halo_ref[TAPS : TAPS + 8, lanes] = edges[0:8, :].astype(bf16)


def edge(halo_ref, s, lanes):
    return halo_ref[TAPS : TAPS + 8, lanes].astype(f32)[2 * s : 2 * s + 2]


def feature(scratch, halo_ref, streams_ref, taps_ref, s, lanes, index):
    now = streams_ref[index, :, lanes].astype(f32)
    one, two = shifted(scratch, edge(halo_ref, s, lanes), now)
    taps = taps_ref[s, :, lanes]
    return taps[0:1] * now + taps[1:2] * one + taps[2:3] * two


def forward_kernel(streams_ref, halo_ref, taps_ref, skip_ref, ahead_ref, output_ref, mixed_ref, gated_ref, scratch):
    length = streams_ref.shape[1]
    for col in range(streams_ref.shape[2] // LANES):
        lanes = slice(col * LANES, (col + 1) * LANES)
        f0, f1, f2 = (feature(scratch.at[s], halo_ref, streams_ref, taps_ref, s, lanes, s) for s in range(3))
        gated = (f1 * f2).astype(bf16)
        gated_ref[:, lanes] = gated
        zero = jnp.zeros((SPAN - TAPS - BLOCK, LANES), bf16)
        extended = jnp.concatenate([zero, halo_ref[:TAPS, lanes], gated], axis=0)
        skip = skip_ref[:, lanes]
        for b, result in enumerate(convolve(ahead_ref[col * PER : (col + 1) * PER], extended, length)):
            rows = slice(b * BLOCK, (b + 1) * BLOCK)
            mixed = result + skip * gated[rows].astype(f32)
            mixed_ref[rows, lanes] = mixed
            output_ref[rows, lanes] = (f0[rows] * mixed).astype(bf16)


def columns_of(received_ref, which, lanes):
    piece = received_ref[:, which, :, lanes].astype(f32)
    return piece.reshape(piece.shape[0] * piece.shape[1], LANES)


def stats_kernel(received_ref, output_ref, gain_ref, stats_ref, squares_ref, products_ref):
    @pl.when(pl.program_id(0) == 0)
    def _():
        squares_ref[...] = jnp.zeros_like(squares_ref)
        products_ref[...] = jnp.zeros_like(products_ref)

    squares, products = squares_ref[...], products_ref[...]
    for col in range(output_ref.shape[1] // LANES):
        lanes = slice(col * LANES, (col + 1) * LANES)
        summed = columns_of(received_ref, 1, lanes) + output_ref[:, lanes].astype(f32)
        squares = squares + summed * summed
        products = products + columns_of(received_ref, 0, lanes) * gain_ref[:, lanes] * summed
    squares_ref[...] = squares
    products_ref[...] = products

    @pl.when(pl.program_id(0) == pl.num_programs(0) - 1)
    def _():
        for row, sums in ((0, squares), (1, products)):
            stats_ref[row : row + 1, :] = jnp.sum(sums.T, axis=0, keepdims=True)


def norm_kernel(received_ref, residual_ref, cot_ref, gain_ref, normed_ref, grad_ref, summed_ref):
    sources, rows, part = received_ref.shape
    width_all = residual_ref.shape[1]
    squares = jnp.zeros((rows, LANES), f32)
    products = jnp.zeros((rows, LANES), f32)
    for s in range(sources):
        where = slice(s * part, (s + 1) * part)
        summed = residual_ref[:, where].astype(f32) + received_ref[s].astype(f32)
        summed_ref[:, where] = summed
        scaled = cot_ref[:, where].astype(f32) * gain_ref[:, where]
        both = (summed * summed, scaled * summed)
        for col in range(part // LANES):
            lanes = slice(col * LANES, (col + 1) * LANES)
            squares = squares + both[0][:, lanes]
            products = products + both[1][:, lanes]
    inverse = lax.rsqrt(jnp.sum(squares, axis=1, keepdims=True) / width_all + norm_eps)
    along = inverse * jnp.sum(products, axis=1, keepdims=True) / width_all
    for s in range(sources):
        where = slice(s * part, (s + 1) * part)
        unit = summed_ref[:, where] * inverse
        gain = gain_ref[:, where]
        normed_ref[:, where] = (unit * gain).astype(bf16)
        grad_ref[:, where] = (inverse * (cot_ref[:, where].astype(f32) * gain - unit * along)).astype(bf16)


def head_kernel(
    width_all,
    streams_ref,
    first1_ref,
    first2_ref,
    halo_ref,
    taps_ref,
    skip_ref,
    filter_ref,
    stats_ref,
    received_ref,
    output_ref,
    gain_ref,
    mixed_ref,
    grad_ref,
    inner_ref,
    first_ref,
    share_ref,
    scratch,
    inverse_ref,
    along_ref,
):
    @pl.when(pl.program_id(0) == 0)
    def _():
        tokens = stats_ref.shape[1]
        squares = jnp.broadcast_to(stats_ref[0:1, :], (LANES, tokens)).T
        products = jnp.broadcast_to(stats_ref[1:2, :], (LANES, tokens)).T
        inverse = lax.rsqrt(squares / width_all + norm_eps)
        inverse_ref[...] = inverse
        along_ref[...] = inverse * products / width_all

    inverse, along = inverse_ref[...], along_ref[...]
    for col in range(streams_ref.shape[2] // LANES):
        lanes = slice(col * LANES, (col + 1) * LANES)
        cot = columns_of(received_ref, 0, lanes)
        unit = (columns_of(received_ref, 1, lanes) + output_ref[:, lanes].astype(f32)) * inverse
        share_ref[:, lanes] = jnp.sum(cot * unit, axis=0, keepdims=True)
        grad_half = (inverse * (cot * gain_ref[:, lanes] - unit * along)).astype(bf16)
        grad_ref[:, lanes] = grad_half
        grad = grad_half.astype(f32)
        f0 = feature(scratch, halo_ref, streams_ref, taps_ref, 0, lanes, 0)
        inner = (grad * f0).astype(bf16)
        inner_ref[:, lanes] = inner
        first_ref[:TAPS, lanes] = inner[:TAPS]
        features = []
        for s, top in ((1, first1_ref), (2, first2_ref)):
            taps = taps_ref[s, :, lanes]
            now = top[0, :, lanes].astype(f32)
            scratch[6:8, :] = edge(halo_ref, s, lanes)
            scratch[8:24, :] = now
            features.append(taps[0:1] * now[:8] + taps[1:2] * scratch[7:15, :] + taps[2:3] * scratch[6:14, :])
        half = filter_ref[col * PER : (col + 1) * PER].astype(bf16).astype(f32)
        bands = jnp.stack([band(half[g : g + 1], 0, 16) for g in range(PER)])
        conv = convolve(bands, inner, BLOCK, 16)[0][:8]
        grad_gated = conv + skip_ref[:, lanes] * inner[:16].astype(f32)[:8]
        scratch[0:2, :] = (grad[:8] * mixed_ref[0:8, lanes])[:2]
        scratch[2:4, :] = (grad_gated * features[1])[:2]
        scratch[4:6, :] = (grad_gated * features[0])[:2]
        scratch[6:8, :] = jnp.zeros((2, LANES), f32)
        rows = scratch[0:8, :]
        high = rows.astype(bf16)
        first_ref[TAPS : TAPS + 8, lanes] = high
        first_ref[TAPS + 8 : TAPS + 16, lanes] = (rows - high.astype(f32)).astype(bf16)


def sums_kernel(streams_ref, halo_ref, gated_ref, inner_ref, grad_ref, mixed_ref, gain_ref, early_ref, scratch):
    length = streams_ref.shape[1]
    blocks = length // BLOCK
    flip = anti_identity(SPAN)
    which = lane_group((BLOCK, blocks * LANES))
    masks = [jnp.where(which == g, 1.0, 0.0).astype(bf16) for g in range(PER)]
    zero = jnp.zeros((SPAN - TAPS - BLOCK, LANES), bf16)
    for col in range(streams_ref.shape[2] // LANES):
        lanes = slice(col * LANES, (col + 1) * LANES)
        gated = gated_ref[:, lanes]
        inner = inner_ref[:, lanes]
        extended = jnp.concatenate([zero, halo_ref[:TAPS, lanes], gated], axis=0)
        backward = dot(flip, windows(extended, length)).astype(bf16)
        grads = jnp.concatenate([inner[at : at + BLOCK] for at in range(0, length, BLOCK)], axis=1)
        pairs = dot_nt(jnp.concatenate([grads * mask for mask in masks], axis=0), backward)
        base = col * 16
        for g in range(PER):
            skewed = pltpu.roll(pairs[g * BLOCK : (g + 1) * BLOCK], SPAN - BLOCK + 1, 1, stride=1, stride_axis=0)
            early_ref[base + g : base + g + 1, :] = jnp.sum(skewed[:, :TAPS], axis=0, keepdims=True)
        early_ref[base + 8 : base + 9, :] = jnp.sum(inner.astype(f32) * gated.astype(f32), axis=0, keepdims=True)
        early_ref[base + 9 : base + 10, :] = gain_ref[:, lanes]
        grad_query = grad_ref[:, lanes].astype(f32) * mixed_ref[:, lanes]
        now = streams_ref[0, :, lanes].astype(f32)
        one, two = shifted(scratch, edge(halo_ref, 0, lanes), now)
        for j, shift in enumerate((now, one, two)):
            early_ref[base + 10 + j : base + 11 + j, :] = jnp.sum(grad_query * shift, axis=0, keepdims=True)
        early_ref[base + 13 : base + 16, :] = jnp.zeros((3, LANES), f32)


def backward_kernel(
    aliased,
    streams_ref,
    halo_ref,
    taps_ref,
    skip_ref,
    behind_ref,
    grad_ref,
    mixed_ref,
    inner_ref,
    after_ref,
    *refs,
):
    stream_grad_ref, late_ref, scratch, ahead = refs[1:] if aliased else refs
    length = streams_ref.shape[1]
    for col in range(streams_ref.shape[2] // LANES):
        lanes = slice(col * LANES, (col + 1) * LANES)
        inner = inner_ref[:, lanes]
        zero = jnp.zeros((SPAN - TAPS - BLOCK, LANES), bf16)
        extended = jnp.concatenate([inner, after_ref[:TAPS, lanes], zero], axis=0)
        parts = convolve(behind_ref[col * PER : (col + 1) * PER], extended, length)
        grad_gated = jnp.concatenate(parts, axis=0) + skip_ref[:, lanes] * inner.astype(f32)
        shifts, features = {}, {}
        for s in (1, 2):
            now = streams_ref[s, :, lanes].astype(f32)
            one, two = shifted(scratch.at[s], edge(halo_ref, s, lanes), now)
            taps = taps_ref[s, :, lanes]
            shifts[s] = (now, one, two)
            features[s] = taps[0:1] * now + taps[1:2] * one + taps[2:3] * two
        grads = (
            grad_ref[:, lanes].astype(f32) * mixed_ref[:, lanes],
            grad_gated * features[2],
            grad_gated * features[1],
        )
        following = after_ref[TAPS : TAPS + 16, lanes].astype(f32)
        following = following[:8] + following[8:]
        for s in range(3):
            ahead[s, 0:length, :] = grads[s]
            ahead[s, length : length + 2, :] = following[2 * s : 2 * s + 2]
            taps = taps_ref[s, :, lanes]
            stream_grad_ref[s, :, lanes] = (
                taps[0:1] * grads[s] + taps[1:2] * ahead[s, 1 : length + 1, :] + taps[2:3] * ahead[s, 2 : length + 2, :]
            ).astype(bf16)
        for s in (1, 2):
            for j in range(3):
                row = col * 8 + (s - 1) * 3 + j
                late_ref[row : row + 1, :] = jnp.sum(grads[s] * shifts[s][j], axis=0, keepdims=True)
        late_ref[col * 8 + 6 : col * 8 + 8, :] = jnp.zeros((2, LANES), f32)


def from_behind(value, axis, steps):
    count = lax.axis_size(axis)
    first, last = (max(0, -steps), min(count, count - steps))
    return lax.ppermute(value, axis, [(source, source + steps) for source in range(first, last)])


def exchange_sum(value, axis):
    count, reach, other = lax.axis_size(axis), 1, None
    while reach < count:
        if other is not None:
            value = value + other.astype(f32)
        value = lax.reduce_precision(value, 8, 7)
        other = lax.ppermute(value.astype(bf16), axis, [(i, i ^ reach) for i in range(count)])
        reach *= 2
    return value, other


def close_kernel(mine_ref, other_ref, long_ref, short_ref, skip_ref, gain_ref):
    columns = skip_ref.shape[1] // LANES
    total = mine_ref[...] + other_ref[...].astype(f32)
    for col in range(columns):
        lanes = slice(col * LANES, (col + 1) * LANES)
        at, late = col * 16, columns * 16 + col * 8
        long_ref[col * PER : (col + 1) * PER, :] = total[at : at + PER]
        skip_ref[:, lanes] = total[at + 8 : at + 9]
        gain_ref[:, lanes] = total[at + 9 : at + 10]
        for j in range(3):
            short_ref[0, j : j + 1, lanes] = total[at + 10 + j : at + 11 + j]
            for s in (1, 2):
                row = late + (s - 1) * 3 + j
                short_ref[s, j : j + 1, lanes] = total[row : row + 1]


def local(residual, streams, short_filter, long_filter, skip, gain, cotangent):
    tokens_here, channels = streams.shape[1:]
    groups = long_filter.shape[0]
    rows_here, width_all = residual.shape
    owners = lax.axis_size("tensor")
    assert long_filter.shape[1] == TAPS and channels == groups * WIDTH and tokens_here % (2 * TAPS) == 0
    chunks = 2
    part = channels // chunks
    step = min(part, 512)
    steps, all_steps = part // step, channels // step
    cols = step // LANES
    skip_row = skip[None, :]
    gain_row = gain[None, :]
    gain_here = lax.dynamic_slice_in_dim(gain, lax.axis_index("tensor") * channels, channels)[None, :]

    spec = pl.BlockSpec

    def wide(rows, offset=0):
        return spec((rows, step), lambda i: (0, i + offset))

    def deep(first, rows, offset=0):
        return spec((first, rows, step), lambda i: (0, 0, i + offset))

    def bands_of(offset=0):
        return spec((step // WIDTH, BLOCK, SPAN), lambda i: (i + offset, 0, 0))

    def arrived(offset=0):
        return spec((owners, 2, rows_here, step), lambda i: (0, 0, 0, i + offset))

    def padded(count=None):
        shape = (tokens_here + 8, LANES)
        return pltpu.VMEM(shape if count is None else (count,) + shape, f32)

    def kernel(body, name, micros, **how):
        return pl.pallas_call(
            body,
            compiler_params=params(),
            cost_estimate=pl.CostEstimate(flops=0, bytes_accessed=micros * 1000, transcendentals=0),
            name=name,
            **how,
        )

    def last(s):
        return spec((1, TAPS, step), lambda i: (s, tokens_here // TAPS - 1, i))

    def rows16(s, back):
        return spec((1, 16, step), lambda i: (s, tokens_here // 16 - back, i))

    rows_a_step = rows_here // all_steps
    packed, halo = kernel(
        open_kernel,
        "open",
        3,
        grid=(all_steps,),
        in_specs=[
            spec((rows_a_step, width_all), lambda i: (i, 0)),
            spec((rows_a_step, width_all), lambda i: (i, 0)),
            rows16(0, 1),
            last(1),
            last(2),
            rows16(1, TAPS // 16 + 1),
            rows16(2, TAPS // 16 + 1),
            deep(3, 3),
        ],
        out_specs=[
            spec((owners, 2, rows_a_step, channels), lambda i: (0, 0, i, 0)),
            wide(TAPS + 8),
        ],
        out_shape=[
            jax.ShapeDtypeStruct((owners, 2, rows_here, channels), bf16),
            jax.ShapeDtypeStruct((TAPS + 8, channels), bf16),
        ],
        scratch_shapes=[padded(3)],
    )(cotangent, residual, streams, streams, streams, streams, streams, short_filter)
    halo = from_behind(halo, "dp", 1)
    received = lax.all_to_all(packed, "tensor", split_axis=0, concat_axis=0, tiled=True)

    band_shape = jax.ShapeDtypeStruct((groups, BLOCK, SPAN), bf16)
    each = min(groups, 16)
    ahead_bands, behind_bands = kernel(
        bands_kernel,
        "bands",
        5,
        grid=(groups // each,),
        in_specs=[spec((each, TAPS), lambda i: (i, 0))],
        out_specs=[spec((each, BLOCK, SPAN), lambda i: (i, 0, 0))] * 2,
        out_shape=[band_shape] * 2,
    )(long_filter)

    output, mixed, gated = kernel(
        forward_kernel,
        "forward",
        5,
        grid=(all_steps,),
        in_specs=[deep(3, tokens_here), wide(TAPS + 8), deep(3, 3), wide(1), bands_of()],
        out_specs=[wide(tokens_here)] * 3,
        out_shape=[jax.ShapeDtypeStruct((tokens_here, channels), t) for t in (bf16, f32, bf16)],
        scratch_shapes=[padded(3)],
    )(streams, halo, short_filter, skip_row, ahead_bands)
    stats = kernel(
        stats_kernel,
        "stats",
        2,
        grid=(all_steps,),
        in_specs=[arrived(), wide(tokens_here), wide(1)],
        out_specs=spec((2, tokens_here), lambda i: (0, 0)),
        out_shape=jax.ShapeDtypeStruct((2, tokens_here), f32),
        scratch_shapes=[pltpu.VMEM((tokens_here, LANES), f32)] * 2,
    )(received, output, gain_here)
    stats = lax.psum(stats, "tensor")
    stats, leaving = lax.optimization_barrier((stats, output))
    rows_received = lax.all_to_all(
        leaving.reshape(owners, rows_here, channels), "tensor", split_axis=0, concat_axis=0, tiled=True
    )

    grads, inner, after, shares = [], [], [], []
    for k in range(chunks):
        grad_k, inner_k, first_k, share_k = kernel(
            functools.partial(head_kernel, width_all),
            "head",
            2,
            grid=(steps,),
            in_specs=[
                deep(1, tokens_here, k * steps),
                spec((1, 16, step), lambda i, k=k: (1, 0, i + k * steps)),
                spec((1, 16, step), lambda i, k=k: (2, 0, i + k * steps)),
                wide(TAPS + 8, k * steps),
                deep(3, 3, k * steps),
                wide(1, k * steps),
                spec((step // WIDTH, TAPS), lambda i, k=k: (i + k * steps, 0)),
                spec((2, tokens_here), lambda i: (0, 0)),
                arrived(k * steps),
                wide(tokens_here, k * steps),
                wide(1, k * steps),
                spec((16, step), lambda i, k=k: (0, i + k * steps)),
            ],
            out_specs=[wide(tokens_here), wide(tokens_here), wide(TAPS + 16), wide(1)],
            out_shape=[
                jax.ShapeDtypeStruct((tokens_here, part), bf16),
                jax.ShapeDtypeStruct((tokens_here, part), bf16),
                jax.ShapeDtypeStruct((TAPS + 16, part), bf16),
                jax.ShapeDtypeStruct((1, part), f32),
            ],
            scratch_shapes=[padded()] + [pltpu.VMEM((tokens_here, LANES), f32)] * 2,
        )(streams, streams, streams, halo, short_filter, skip_row, long_filter, stats, received, output, gain_here, mixed)
        grads.append(grad_k)
        inner.append(inner_k)
        shares.append(share_k)
        after.append(from_behind(first_k, "dp", -1))

    early = []
    for k in range(chunks):
        early.append(
            kernel(
                sums_kernel,
                "sums",
                4,
                grid=(steps,),
                in_specs=[
                    deep(1, tokens_here, k * steps),
                    wide(TAPS + 8, k * steps),
                    wide(tokens_here, k * steps),
                    wide(tokens_here),
                    wide(tokens_here),
                    wide(tokens_here, k * steps),
                    wide(1),
                ],
                out_specs=spec((cols * 16, LANES), lambda i: (i, 0)),
                out_shape=jax.ShapeDtypeStruct((part // LANES * 16, LANES), f32),
                scratch_shapes=[padded()],
            )(streams, halo, gated, inner[k], grads[k], mixed, shares[k])
        )
    block = min(rows_here, 16)
    by_rows = spec((block, width_all), lambda i: (i, 0))
    normed, grad_residual = kernel(
        norm_kernel,
        "norm",
        4,
        grid=(rows_here // block,),
        in_specs=[
            spec((owners, block, channels), lambda i: (0, i, 0)),
            by_rows,
            by_rows,
            spec((1, width_all), lambda i: (0, 0)),
        ],
        out_specs=[by_rows, by_rows],
        out_shape=[jax.ShapeDtypeStruct(residual.shape, bf16)] * 2,
        scratch_shapes=[pltpu.VMEM((block, width_all), f32)],
    )(rows_received, residual, cotangent, gain_row)

    stream_grad, late = None, []
    for k in range(chunks):
        aliased = stream_grad is not None
        operands = [streams, halo, short_filter, skip_row, behind_bands, grads[k], mixed, inner[k], after[k]]
        in_specs = [
            deep(3, tokens_here, k * steps),
            wide(TAPS + 8, k * steps),
            deep(3, 3, k * steps),
            wide(1, k * steps),
            bands_of(k * steps),
            wide(tokens_here),
            wide(tokens_here, k * steps),
            wide(tokens_here),
            wide(TAPS + 16),
        ]
        if aliased:
            operands.append(stream_grad)
            in_specs.append(spec(memory_space=pl.ANY))
        stream_grad, late_k = kernel(
            functools.partial(backward_kernel, aliased),
            "backward",
            5,
            grid=(steps,),
            in_specs=in_specs,
            out_specs=[
                deep(3, tokens_here, k * steps),
                spec((cols * 8, LANES), lambda i: (i, 0)),
            ],
            out_shape=[
                jax.ShapeDtypeStruct(streams.shape, bf16),
                jax.ShapeDtypeStruct((part // LANES * 8, LANES), f32),
            ],
            scratch_shapes=[padded(3), padded(3)],
            input_output_aliases={len(operands) - 1: 0} if aliased else {},
        )(*operands)
        late.append(late_k)
    mine, other = exchange_sum(jnp.concatenate(early + late, axis=0), "dp")
    long_grad, short_grad, skip_grad, gain_grad = kernel(
        close_kernel,
        "close",
        1,
        out_shape=[
            jax.ShapeDtypeStruct((groups, TAPS), f32),
            jax.ShapeDtypeStruct((3, 3, channels), f32),
            jax.ShapeDtypeStruct((1, channels), f32),
            jax.ShapeDtypeStruct((1, channels), f32),
        ],
    )(mine, other)
    skip_grad, gain_grad = skip_grad.reshape(channels), gain_grad.reshape(channels)
    return (normed, grad_residual, stream_grad, long_grad, short_grad, skip_grad, gain_grad)


def solution(mesh):
    placed = (
        P(("dp", "tensor"), None),
        P(None, "dp", "tensor"),
        P(None, None, "tensor"),
        P("tensor", None),
        P("tensor"),
        P(),
        P(("dp", "tensor"), None),
    )
    return jax.shard_map(
        local,
        mesh=mesh,
        in_specs=placed,
        out_specs=(
            P(("dp", "tensor"), None),
            P(("dp", "tensor"), None),
            P(None, "dp", "tensor"),
            P("tensor", None),
            P(None, None, "tensor"),
            P("tensor"),
            P("tensor"),
        ),
        check_vma=False,
    )
```

time: 172 us -> 118 us (0.69)
  local copies, waits for them, and re-layouts: 33.6 us -> 6.51 us
  blocking collectives: 31.2 us -> 6.33 us
  Pallas kernels: 40.6 us -> 60 us
  starting transfers between devices: 44.1 us -> 26 us
  waiting for transfers between devices: 18.1 us -> 13.9 us
    all_to_all x3 -> x0, blocking collectives: 31.2 us -> none  [the longest x1 12.3 us: local(): lax.all_to_all(output.reshape(owners, rows_here, part), 'tensor', split_a...]
    unnamed x71 -> x20, local copies, waits for them, and re-layouts: 29.8 us -> 5.21 us
    pallas_call x10 -> x12, Pallas kernels: 40.6 us -> 60 us  [the longest x2 13.1 us: local(): kernel(functools.partial(backward_kernel, aliased), 'backward', 5, grid=(...]
    ppermute x7 -> x3, starting transfers between devices: 17.2 us -> 6.91 us  [from_behind(): lax.ppermute(value, axis, [(source, source + steps) for source in range(f...]
    ppermute x6 -> x3, starting transfers between devices: 18.7 us -> 11.2 us  [exchange_sum(): lax.ppermute(value.astype(bf16), axis, [(i, i ^ reach) for i in range(cou...]
    psum x0 -> x1, blocking collectives: none -> 6.33 us  [local(): stats = lax.psum(stats, 'tensor')]
    ppermute x7 -> x3, waiting for transfers between devices: 7.98 us -> 4.44 us  [from_behind(): lax.ppermute(value, axis, [(source, source + steps) for source in range(f...]
    slice x7 -> x0, local copies, waits for them, and re-layouts: 2.43 us -> none  [the longest x1 1 us: local(): short_filter[1:, 0][:, None, :] * tail[:, 2:]]
  transfers between devices with their start and end apart: 15 -> 8, of which waited for: 6 -> 5; matrix products, arithmetic and copies ran while one was open for 2% -> 4% of each run, Pallas kernels for 14% -> 37%
where the time goes in v2:
time: 118 us; the launch traced here: 117 us
  Pallas kernels  60 us (51%)
  starting transfers between devices  26 us (22%)
  waiting for transfers between devices  13.9 us (12%)
  local copies, waits for them, and re-layouts  6.51 us (6%)
  blocking collectives  6.33 us (5%)
  other arithmetic  3.06 us (3%)
    pallas_call x2, Pallas kernels, local(): kernel(functools.partial(backward_kernel, aliased), 'backward', 5, grid=(...  13.1 us
    ppermute x3, starting transfers between devices, exchange_sum(): lax.ppermute(value.astype(bf16), axis, [(i, i ^ reach) for i in range(cou...  11.2 us
    pallas_call x2, Pallas kernels, local(): kernel(sums_kernel, 'sums', 4, grid=(steps,), in_specs=[deep(1, tokens_he...  10 us
    ppermute x3, waiting for transfers between devices, exchange_sum(): lax.ppermute(value.astype(bf16), axis, [(i, i ^ reach) for i in range(cou...  8.84 us
    pallas_call x2, Pallas kernels, local(): kernel(functools.partial(head_kernel, width_all), 'head', 2, grid=(steps,...  8.39 us
    pallas_call x1, Pallas kernels, local(): kernel(forward_kernel, 'forward', 5, grid=(all_steps,), in_specs=[deep(3,...  7.5 us
    ppermute x3, starting transfers between devices, from_behind(): lax.ppermute(value, axis, [(source, source + steps) for source in range(f...  6.91 us
    pallas_call x1, Pallas kernels, local(): kernel(bands_kernel, 'bands', 5, grid=(groups // each,), in_specs=[spec((...  6.71 us
  transfers between devices with their start and end apart: 8, of which 5 were waited for; matrix products, arithmetic and copies ran while one was open for 4% of the time, Pallas kernels for 37%

profile of v2, /device:TPU:0, one launch (start us, length us, event | category | flops | bytes accessed | tf_op | source)
XLA Modules:
  0.0 116.6 jit_solution(10826049197335250267)
XLA Ops:
  0.6 4.5 %open.1 = (bf16[4,2,64,2048]{3,2,1,0:T(8,128)(2,1)}, bf16[136,2048]{1,0:T(8,128)(2,1)}) custom-call(bf16[64,8192]{1,0:T(8,128)(2,1)} %cot_ref.3, bf16[64,8192]{1,0:T(8,128)(2,1)} %residual_ref.3, bf16[3,256,2048]{2,1,0:T(8,128)(2,1)} %streams_ref.13, bf16[3,256,2048]{2,1,0:T(8,128)(2,1)} %streams_ref.13, bf16[3,256,2048]{2,1,0:T(8,128)(2,1)} %streams_ref.13, ...), custom_call_target="tpu_custom_call" | custom-call | bytes 3000 | tf_op jit(solution)/shard_map/open/pallas_call | solution.py:412
  5.1 0.0 copy-start.9
  5.1 4.4 %all-to-all-start = ((bf16[4,2,64,2048]{3,2,1,0:T(8,128)(2,1)}), bf16[4,2,64,2048]{3,2,1,0:T(8,128)(2,1)S(1)}, u32[]{:S(2)}, u32[]{:S(2)}) async-start(bf16[4,2,64,2048]{3,2,1,0:T(8,128)(2,1)} %get-tuple-element.34), calls=%async_computation | async-start | bytes 4194304 | tf_op jit(solution)/shard_map/all_to_all | solution.py:438
  9.4 0.0 copy-done.9
  9.4 4.3 %collective-permute-start = (bf16[136,2048]{1,0:T(8,128)(2,1)S(1)}, bf16[136,2048]{1,0:T(8,128)(2,1)S(1)}, u32[]{:S(2)}, u32[]{:S(2)}) collective-permute-start(bf16[136,2048]{1,0:T(8,128)(2,1)S(1)} %copy-done.9), channel_id=1, source_target_pairs={{0,4},{4,8},{8,12},{12,16},{16,20},{20,24},{24,28},{1,5},{5,9},{9,... | collective-permute-start | bytes 1671176 | tf_op jit(solution)/shard_map/ppermute | solution.py:333
  13.8 6.7 %bands.1 = (bf16[128,64,256]{2,1,0:T(8,128)(2,1)}, bf16[128,64,256]{2,1,0:T(8,128)(2,1)}) custom-call(f32[128,128]{1,0:T(8,128)} %filter_ref.5), custom_call_target="tpu_custom_call" | custom-call | bytes 5000 | tf_op jit(solution)/shard_map/bands/pallas_call | solution.py:442
  20.5 1.3 %dynamic_slice.3 = f32[2048]{0:T(1024)} dynamic-slice(f32[8192]{0:T(1024)} %param.12, s32[]{:T(128)S(6)} %select_n.3), dynamic_slice_sizes={2048} | dynamic-slice | bytes 16388 | tf_op jit(solution)/shard_map/dynamic_slice | solution.py:376
  21.8 4.4 %collective-permute-done.halo_ref = bf16[136,2048]{1,0:T(8,128)(2,1)S(1)} collective-permute-done((bf16[136,2048]{1,0:T(8,128)(2,1)S(1)}, bf16[136,2048]{1,0:T(8,128)(2,1)S(1)}, u32[]{:S(2)}, u32[]{:S(2)}) %collective-permute-start) | collective-permute-done | bytes 557088 | tf_op jit(solution)/shard_map/ppermute | solution.py:333
  26.2 0.0 copy-start.1
  26.2 0.8 copy-done.1
  27.0 7.5 %forward.1 = (bf16[256,2048]{1,0:T(8,128)(2,1)}, f32[256,2048]{1,0:T(8,128)}, bf16[256,2048]{1,0:T(8,128)(2,1)}) custom-call(bf16[3,256,2048]{2,1,0:T(8,128)(2,1)} %streams_ref.13, bf16[136,2048]{1,0:T(8,128)(2,1)} %copy-done.1, f32[3,3,2048]{2,1,0:T(4,128)} %taps_ref.11, f32[1,2048]{1,0:T(1,128)} %bitcast.6, bf16[128,64,256]{2,1,0:T(8,128)(2,1)} %get-tuple-element.36.ahead_ref), custom_call_target="tpu_custom_call" | custom-call | bytes 5000 | tf_op jit(solution)/shard_map/forward/pallas_call | solution.py:452
  34.5 0.6 all-to-all-done.received_ref
  35.1 0.0 copy-start
  35.1 1.3 %copy-done = bf16[4,2,64,2048]{3,2,1,0:T(8,128)(2,1)} copy-done((bf16[4,2,64,2048]{3,2,1,0:T(8,128)(2,1)}, bf16[4,2,64,2048]{3,2,1,0:T(8,128)(2,1)S(1)}, u32[]{:S(2)}) %copy-start) | copy-done | bytes 2097176
  36.5 3.6 %stats.1 = f32[2,256]{1,0:T(2,128)} custom-call(bf16[4,2,64,2048]{3,2,1,0:T(8,128)(2,1)} %copy-done, bf16[256,2048]{1,0:T(8,128)(2,1)} %get-tuple-element.38.output_ref, f32[1,2048]{1,0:T(1,128)} %bitcast.11), custom_call_target="tpu_custom_call" | custom-call | bytes 2000 | tf_op jit(solution)/shard_map/stats/pallas_call | solution.py:462
  40.1 6.3 %psum.7.stats_ref = f32[2,256]{1,0:T(2,128)} all-reduce(f32[2,256]{1,0:T(2,128)} %stats.1), channel_id=1, replica_groups=mesh['dp'=8,'tensor'=4] {'tensor'}, use_global_device_ids=true, to_apply=%region_0.0 | all-reduce | flops 512 | bytes 4096 | tf_op jit(solution)/shard_map/psum | solution.py:472
  46.4 4.2 %head.3 = (bf16[256,1024]{1,0:T(8,128)(2,1)}, bf16[256,1024]{1,0:T(8,128)(2,1)}, bf16[144,1024]{1,0:T(8,128)(2,1)}, f32[1,1024]{1,0:T(1,128)}) custom-call(bf16[3,256,2048]{2,1,0:T(8,128)(2,1)} %streams_ref.13, bf16[3,256,2048]{2,1,0:T(8,128)(2,1)} %streams_ref.13, bf16[3,256,2048]{2,1,0:T(8,128)(2,1)} %streams_ref.13, bf16[136,2048]{1,0:T(8,128)(2,1)} %copy-done.1, ...), custom_call_target="tpu_custom_call" | custom-call | bytes 2000 | tf_op jit(solution)/shard_map/head/pallas_call | solution.py:480
  50.6 1.3 %collective-permute-start.2 = (bf16[144,1024]{1,0:T(8,128)(2,1)}, bf16[144,1024]{1,0:T(8,128)(2,1)S(1)}, u32[]{:S(2)}, u32[]{:S(2)}) collective-permute-start(bf16[144,1024]{1,0:T(8,128)(2,1)} %get-tuple-element.49), channel_id=1, source_target_pairs={{4,0},{8,4},{12,8},{16,12},{20,16},{24,20},{28,24},{5,1},{9,5},{13... | collective-permute-start | bytes 884744 | tf_op jit(solution)/shard_map/ppermute | solution.py:333
  51.9 4.2 %head.2 = (bf16[256,1024]{1,0:T(8,128)(2,1)}, bf16[256,1024]{1,0:T(8,128)(2,1)}, bf16[144,1024]{1,0:T(8,128)(2,1)}, f32[1,1024]{1,0:T(1,128)}) custom-call(bf16[3,256,2048]{2,1,0:T(8,128)(2,1)} %streams_ref.13, bf16[3,256,2048]{2,1,0:T(8,128)(2,1)} %streams_ref.13, bf16[3,256,2048]{2,1,0:T(8,128)(2,1)} %streams_ref.13, bf16[136,2048]{1,0:T(8,128)(2,1)} %copy-done.1, ...), custom_call_target="tpu_custom_call" | custom-call | bytes 2000 | tf_op jit(solution)/shard_map/head/pallas_call | solution.py:480
  56.1 1.3 %collective-permute-start.1 = (bf16[144,1024]{1,0:T(8,128)(2,1)}, bf16[144,1024]{1,0:T(8,128)(2,1)S(1)}, u32[]{:S(2)}, u32[]{:S(2)}) collective-permute-start(bf16[144,1024]{1,0:T(8,128)(2,1)} %get-tuple-element.46), channel_id=1, source_target_pairs={{4,0},{8,4},{12,8},{16,12},{20,16},{24,20},{28,24},{5,1},{9,5},{13... | collective-permute-start | bytes 884744 | tf_op jit(solution)/shard_map/ppermute | solution.py:333
  57.4 3.5 %all-to-all-start.1 = ((bf16[4,64,2048]{2,1,0:T(8,128)(2,1)}), bf16[4,64,2048]{2,1,0:T(8,128)(2,1)S(1)}, u32[]{:S(2)}, u32[]{:S(2)}) async-start(bf16[4,64,2048]{2,1,0:T(8,128)(2,1)} %bitcast.2), calls=%async_computation.1 | async-start | bytes 2097152 | tf_op jit(solution)/shard_map/all_to_all | solution.py:474
  61.0 5.0 %sums.2 = f32[128,128]{1,0:T(8,128)} custom-call(bf16[3,256,2048]{2,1,0:T(8,128)(2,1)} %streams_ref.13, bf16[136,2048]{1,0:T(8,128)(2,1)} %copy-done.1, bf16[256,2048]{1,0:T(8,128)(2,1)} %get-tuple-element.52.gated_ref, bf16[256,1024]{1,0:T(8,128)(2,1)} %get-tuple-element.48.inner_ref, bf16[256,1024]{1,0:T(8,128)(2,1)} %get-tuple-element.47.grad_ref, ...), custom_call_target="tpu_custom_call" | custom-call | bytes 4000 | tf_op jit(solution)/shard_map/sums/pallas_call | solution.py:516
  66.0 5.0 %sums.3 = f32[128,128]{1,0:T(8,128)} custom-call(bf16[3,256,2048]{2,1,0:T(8,128)(2,1)} %streams_ref.13, bf16[136,2048]{1,0:T(8,128)(2,1)} %copy-done.1, bf16[256,2048]{1,0:T(8,128)(2,1)} %get-tuple-element.52.gated_ref, bf16[256,1024]{1,0:T(8,128)(2,1)} %get-tuple-element.45.inner_ref, bf16[256,1024]{1,0:T(8,128)(2,1)} %get-tuple-element.44.grad_ref, ...), custom_call_target="tpu_custom_call" | custom-call | bytes 4000 | tf_op jit(solution)/shard_map/sums/pallas_call | solution.py:516
  71.0 0.0 collective-permute-done.2.after_ref
  71.0 0.0 copy-start.5
  71.0 0.7 copy-done.5
  71.7 6.5 %backward.2 = (bf16[3,256,2048]{2,1,0:T(8,128)(2,1)}, f32[64,128]{1,0:T(8,128)}) custom-call(bf16[3,256,2048]{2,1,0:T(8,128)(2,1)} %streams_ref.13, bf16[136,2048]{1,0:T(8,128)(2,1)} %copy-done.1, f32[3,3,2048]{2,1,0:T(4,128)} %taps_ref.11, f32[1,2048]{1,0:T(1,128)} %bitcast.9, bf16[128,64,256]{2,1,0:T(8,128)(2,1)} %get-tuple-element.41.behind_ref, ...), custom_call_target="tpu_custom_call" | custom-call | bytes 5000 | tf_op jit(solution)/shard_map/backward/pallas_call | solution.py:571
  78.2 0.0 collective-permute-done.1.after_ref
  78.2 0.0 copy-start.7
  78.2 0.7 copy-done.7
  79.0 6.6 %backward.3 = (bf16[3,256,2048]{2,1,0:T(8,128)(2,1)}, f32[64,128]{1,0:T(8,128)}) custom-call(bf16[3,256,2048]{2,1,0:T(8,128)(2,1)} %streams_ref.13, bf16[136,2048]{1,0:T(8,128)(2,1)} %copy-done.1, f32[3,3,2048]{2,1,0:T(4,128)} %taps_ref.11, f32[1,2048]{1,0:T(1,128)} %bitcast.10, ...), custom_call_target="tpu_custom_call", output_to_operand_aliasing={{0}: (9, {})} | custom-call | bytes 5000 | tf_op jit(solution)/shard_map/backward/pallas_call | solution.py:571
  85.5 0.0 copy-done.3
  85.5 0.0 copy-done.4
  85.6 0.0 copy-done.6
  85.6 0.8 fusion.1
  86.3 3.8 %collective-permute-start.3 = (bf16[384,128]{1,0:T(8,128)(2,1)S(1)}, bf16[384,128]{1,0:T(8,128)(2,1)S(1)}, u32[]{:S(2)}, u32[]{:S(2)}) collective-permute-start(bf16[384,128]{1,0:T(8,128)(2,1)S(1)} %fusion.1), channel_id=1, source_target_pairs={{0,4},{4,0},{8,12},{12,8},{16,20},{20,16},{24,28},{28,24},{1,5},{5... | collective-permute-start | bytes 294920 | tf_op jit(solution)/shard_map/ppermute | solution.py:342
  90.1 3.4 %collective-permute-done.3 = bf16[384,128]{1,0:T(8,128)(2,1)S(1)} collective-permute-done((bf16[384,128]{1,0:T(8,128)(2,1)S(1)}, bf16[384,128]{1,0:T(8,128)(2,1)S(1)}, u32[]{:S(2)}, u32[]{:S(2)}) %collective-permute-start.3) | collective-permute-done | bytes 98336 | tf_op jit(solution)/shard_map/ppermute | solution.py:342
  93.5 0.8 fusion
  94.3 3.5 %collective-permute-start.4 = (bf16[384,128]{1,0:T(8,128)(2,1)S(1)}, bf16[384,128]{1,0:T(8,128)(2,1)S(1)}, u32[]{:S(2)}, u32[]{:S(2)}) collective-permute-start(bf16[384,128]{1,0:T(8,128)(2,1)S(1)} %fusion), channel_id=1, source_target_pairs={{0,8},{4,12},{8,0},{12,4},{16,24},{20,28},{24,16},{28,20},{1,9},{5... | collective-permute-start | bytes 294920 | tf_op jit(solution)/shard_map/ppermute | solution.py:342
  97.9 2.8 %collective-permute-done.4 = bf16[384,128]{1,0:T(8,128)(2,1)S(1)} collective-permute-done((bf16[384,128]{1,0:T(8,128)(2,1)S(1)}, bf16[384,128]{1,0:T(8,128)(2,1)S(1)}, u32[]{:S(2)}, u32[]{:S(2)}) %collective-permute-start.4) | collective-permute-done | bytes 98336 | tf_op jit(solution)/shard_map/ppermute | solution.py:342
  100.7 1.5 %fusion.2 = (bf16[384,128]{1,0:T(8,128)(2,1)S(1)}, f32[384,128]{1,0:T(8,128)}) fusion(bf16[384,128]{1,0:T(8,128)(2,1)S(1)} %collective-permute-done.4, bf16[384,128]{1,0:T(8,128)(2,1)S(1)} %collective-permute-done.3, f32[64,128]{1,0:T(8,128)} %get-tuple-element.56, f32[64,128]{1,0:T(8,128)S(1)} %copy-done.6, f32[128,128]{1,0:T(8,128)S(1)} %copy-done.4, ...), kind=kLoop, calls=%fused_computation.5 | loop fusion | flops 540672 | bytes 688128 | tf_op jit(solution)/shard_map/convert_element_type | solution.py:342
  102.2 3.9 %collective-permute-start.5 = (bf16[384,128]{1,0:T(8,128)(2,1)S(1)}, bf16[384,128]{1,0:T(8,128)(2,1)S(1)}, u32[]{:S(2)}, u32[]{:S(2)}) collective-permute-start(bf16[384,128]{1,0:T(8,128)(2,1)S(1)} %get-tuple-element.61), channel_id=1, source_target_pairs={{0,16},{4,20},{8,24},{12,28},{16,0},{20,4},{24,8},{28,12},{1,17},{... | collective-permute-start | bytes 294920 | tf_op jit(solution)/shard_map/ppermute | solution.py:342
  106.1 2.6 %collective-permute-done.5.other_ref = bf16[384,128]{1,0:T(8,128)(2,1)S(1)} collective-permute-done((bf16[384,128]{1,0:T(8,128)(2,1)S(1)}, bf16[384,128]{1,0:T(8,128)(2,1)S(1)}, u32[]{:S(2)}, u32[]{:S(2)}) %collective-permute-start.5) | collective-permute-done | bytes 98336 | tf_op jit(solution)/shard_map/ppermute | solution.py:342
  108.7 0.6 copy-done.8
  109.3 1.7 %close.1 = (f32[128,128]{1,0:T(8,128)}, f32[3,3,2048]{2,1,0:T(4,128)}, f32[1,2048]{1,0:T(1,128)}, f32[1,2048]{1,0:T(1,128)}) custom-call(f32[384,128]{1,0:T(8,128)} %get-tuple-element.62.mine_ref, bf16[384,128]{1,0:T(8,128)(2,1)} %copy-done.8), custom_call_target="tpu_custom_call" | custom-call | bytes 1000 | tf_op jit(solution)/shard_map/close/pallas_call | solution.py:590
  111.0 0.0 all-to-all-done.1.received_ref
  111.1 1.0 copy-done.2
  112.1 4.5 %norm.1 = (bf16[64,8192]{1,0:T(8,128)(2,1)}, bf16[64,8192]{1,0:T(8,128)(2,1)}) custom-call(bf16[4,64,2048]{2,1,0:T(8,128)(2,1)} %copy-done.2, bf16[64,8192]{1,0:T(8,128)(2,1)} %residual_ref.3, bf16[64,8192]{1,0:T(8,128)(2,1)} %cot_ref.3, f32[1,8192]{1,0:T(1,128)} %bitcast.14), custom_call_target="tpu_custom_call" | custom-call | bytes 4000 | tf_op jit(solution)/shard_map/norm/pallas_call | solution.py:537
  (5 shorter events, 0.0 us)
Async XLA Ops:
  5.1 4.4 %copy-start.9 = (bf16[136,2048]{1,0:T(8,128)(2,1)S(1)}, bf16[136,2048]{1,0:T(8,128)(2,1)}, u32[]{:S(2)}) copy-start(bf16[136,2048]{1,0:T(8,128)(2,1)} %get-tuple-element.35) | copy-start | bytes 1671172
  5.1 30.1 %all-to-all-start = ((bf16[4,2,64,2048]{3,2,1,0:T(8,128)(2,1)}), bf16[4,2,64,2048]{3,2,1,0:T(8,128)(2,1)S(1)}, u32[]{:S(2)}, u32[]{:S(2)}) async-start(bf16[4,2,64,2048]{3,2,1,0:T(8,128)(2,1)} %get-tuple-element.34), calls=%async_computation | async-start | bytes 4194304 | tf_op jit(solution)/shard_map/all_to_all | solution.py:438
  9.4 16.8 %collective-permute-start = (bf16[136,2048]{1,0:T(8,128)(2,1)S(1)}, bf16[136,2048]{1,0:T(8,128)(2,1)S(1)}, u32[]{:S(2)}, u32[]{:S(2)}) collective-permute-start(bf16[136,2048]{1,0:T(8,128)(2,1)S(1)} %copy-done.9), channel_id=1, source_target_pairs={{0,4},{4,8},{8,12},{12,16},{16,20},{20,24},{24,28},{1,5},{5,9},{9,... | collective-permute-start | bytes 1671176 | tf_op jit(solution)/shard_map/ppermute | solution.py:333
  26.2 0.8 copy-start.1
  35.1 1.3 %copy-start = (bf16[4,2,64,2048]{3,2,1,0:T(8,128)(2,1)}, bf16[4,2,64,2048]{3,2,1,0:T(8,128)(2,1)S(1)}, u32[]{:S(2)}) copy-start(bf16[4,2,64,2048]{3,2,1,0:T(8,128)(2,1)S(1)} %all-to-all-done.received_ref) | copy-start | bytes 6291460
  50.6 20.3 %collective-permute-start.2 = (bf16[144,1024]{1,0:T(8,128)(2,1)}, bf16[144,1024]{1,0:T(8,128)(2,1)S(1)}, u32[]{:S(2)}, u32[]{:S(2)}) collective-permute-start(bf16[144,1024]{1,0:T(8,128)(2,1)} %get-tuple-element.49), channel_id=1, source_target_pairs={{4,0},{8,4},{12,8},{16,12},{20,16},{24,20},{28,24},{5,1},{9,5},{13... | collective-permute-start | bytes 884744 | tf_op jit(solution)/shard_map/ppermute | solution.py:333
  56.1 22.1 %collective-permute-start.1 = (bf16[144,1024]{1,0:T(8,128)(2,1)}, bf16[144,1024]{1,0:T(8,128)(2,1)S(1)}, u32[]{:S(2)}, u32[]{:S(2)}) collective-permute-start(bf16[144,1024]{1,0:T(8,128)(2,1)} %get-tuple-element.46), channel_id=1, source_target_pairs={{4,0},{8,4},{12,8},{16,12},{20,16},{24,20},{28,24},{5,1},{9,5},{13... | collective-permute-start | bytes 884744 | tf_op jit(solution)/shard_map/ppermute | solution.py:333
  57.4 53.6 %all-to-all-start.1 = ((bf16[4,64,2048]{2,1,0:T(8,128)(2,1)}), bf16[4,64,2048]{2,1,0:T(8,128)(2,1)S(1)}, u32[]{:S(2)}, u32[]{:S(2)}) async-start(bf16[4,64,2048]{2,1,0:T(8,128)(2,1)} %bitcast.2), calls=%async_computation.1 | async-start | bytes 2097152 | tf_op jit(solution)/shard_map/all_to_all | solution.py:474
  71.0 0.7 copy-start.5
  78.2 0.7 copy-start.7
  78.9 6.6 %copy-start.3 = (f32[128,128]{1,0:T(8,128)S(1)}, f32[128,128]{1,0:T(8,128)}, u32[]{:S(2)}) copy-start(f32[128,128]{1,0:T(8,128)} %sums.2) | copy-start | bytes 196612
  79.0 6.6 %copy-start.4 = (f32[128,128]{1,0:T(8,128)S(1)}, f32[128,128]{1,0:T(8,128)}, u32[]{:S(2)}) copy-start(f32[128,128]{1,0:T(8,128)} %sums.3) | copy-start | bytes 196612
  79.0 6.6 %copy-start.6 = (f32[64,128]{1,0:T(8,128)S(1)}, f32[64,128]{1,0:T(8,128)}, u32[]{:S(2)}) copy-start(f32[64,128]{1,0:T(8,128)} %get-tuple-element.55) | copy-start | bytes 98308
  86.3 7.2 %collective-permute-start.3 = (bf16[384,128]{1,0:T(8,128)(2,1)S(1)}, bf16[384,128]{1,0:T(8,128)(2,1)S(1)}, u32[]{:S(2)}, u32[]{:S(2)}) collective-permute-start(bf16[384,128]{1,0:T(8,128)(2,1)S(1)} %fusion.1), channel_id=1, source_target_pairs={{0,4},{4,0},{8,12},{12,8},{16,20},{20,16},{24,28},{28,24},{1,5},{5... | collective-permute-start | bytes 294920 | tf_op jit(solution)/shard_map/ppermute | solution.py:342
  94.3 6.4 %collective-permute-start.4 = (bf16[384,128]{1,0:T(8,128)(2,1)S(1)}, bf16[384,128]{1,0:T(8,128)(2,1)S(1)}, u32[]{:S(2)}, u32[]{:S(2)}) collective-permute-start(bf16[384,128]{1,0:T(8,128)(2,1)S(1)} %fusion), channel_id=1, source_target_pairs={{0,8},{4,12},{8,0},{12,4},{16,24},{20,28},{24,16},{28,20},{1,9},{5... | collective-permute-start | bytes 294920 | tf_op jit(solution)/shard_map/ppermute | solution.py:342
  102.2 6.5 %collective-permute-start.5 = (bf16[384,128]{1,0:T(8,128)(2,1)S(1)}, bf16[384,128]{1,0:T(8,128)(2,1)S(1)}, u32[]{:S(2)}, u32[]{:S(2)}) collective-permute-start(bf16[384,128]{1,0:T(8,128)(2,1)S(1)} %get-tuple-element.61), channel_id=1, source_target_pairs={{0,16},{4,20},{8,24},{12,28},{16,0},{20,4},{24,8},{28,12},{1,17},{... | collective-permute-start | bytes 294920 | tf_op jit(solution)/shard_map/ppermute | solution.py:342
  108.7 0.6 copy-start.8
  111.1 1.0 copy-start.2

commit v3 on v2

--- a/solution.py
+++ b/solution.py
@@ -14,13 +14,14 @@
 PER = LANES // WIDTH
 BLOCK = 64
 SPAN = 256
-VMEM_LIMIT = 56 * 2**20
+VMEM_LIMIT = 62
+SMALL_LIMIT = 8
 f32 = jnp.float32
 bf16 = jnp.bfloat16
 
 
-def params():
-    return pltpu.CompilerParams(vmem_limit_bytes=VMEM_LIMIT)
+def params(limit):
+    return pltpu.CompilerParams(vmem_limit_bytes=limit * 2**20)
 
 
 def dot(a, b):
@@ -80,28 +81,50 @@
 
 
 def open_kernel(
-    cot_ref, residual_ref, last0_ref, last1_ref, last2_ref, prior1_ref, prior2_ref, taps_ref, packed_ref, halo_ref, scratch
+    cot_ref, residual_ref, streams_ref, taps_ref, packed_ref, halo_ref, pieces, ends, rows, scratch, in_sem, out_sem, end_sem
 ):
     owners, _, _, channels = packed_ref.shape
-    for j in range(owners):
-        where = slice(j * channels, (j + 1) * channels)
-        packed_ref[j, 0] = cot_ref[:, where]
-        packed_ref[j, 1] = residual_ref[:, where]
-    for col in range(halo_ref.shape[1] // LANES):
+    length = streams_ref.shape[1]
+    back = ends.shape[1]
+    ending = pltpu.make_async_copy(streams_ref.at[:, pl.ds(length - back, back), :], ends, end_sem.at[0])
+    ending.start()
+    places = [(j, which) for j in range(owners) for which in range(2)]
+    arriving = [
+        pltpu.make_async_copy(
+            (cot_ref, residual_ref)[which].at[:, pl.ds(j * channels, channels)], pieces.at[j, which], in_sem.at[j, which]
+        )
+        for j, which in places
+    ]
+    leaving = [
+        pltpu.make_async_copy(pieces.at[j, which], packed_ref.at[j, which], out_sem.at[j, which]) for j, which in places
+    ]
+    for copy in arriving:
+        copy.start()
+    ending.wait()
+    for col in range(channels // LANES):
         lanes = slice(col * LANES, (col + 1) * LANES)
         features = []
-        for s, last, prior in ((1, last1_ref, prior1_ref), (2, last2_ref, prior2_ref)):
-            now = last[0, :, lanes].astype(f32)
-            one, two = shifted(scratch.at[s], prior[0, :, lanes].astype(f32)[14:], now)
+        for s in (1, 2):
+            scratch[s, 0:back, :] = ends[s, :, lanes].astype(f32)
             taps = taps_ref[s, :, lanes]
+            now, one, two = (scratch[s, back - TAPS - n : back - n, :] for n in range(3))
             features.append(taps[0:1] * now + taps[1:2] * one + taps[2:3] * two)
-        halo_ref[:TAPS, lanes] = (features[0] * features[1]).astype(bf16)
+        rows[:TAPS, lanes] = (features[0] * features[1]).astype(bf16)
         edges = scratch.at[0]
-        edges[0:2, :] = last0_ref[0, :, lanes].astype(f32)[14:]
-        edges[2:4, :] = scratch[1, TAPS + 6 : TAPS + 8, :]
-        edges[4:6, :] = scratch[2, TAPS + 6 : TAPS + 8, :]
+        edges[0:2, :] = ends[0, back - 16 : back, lanes].astype(f32)[14:]
+        edges[2:4, :] = scratch[1, back - 2 : back, :]
+        edges[4:6, :] = scratch[2, back - 2 : back, :]
         edges[6:8, :] = jnp.zeros((2, LANES), f32)
-        halo_ref[TAPS : TAPS + 8, lanes] = edges[0:8, :].astype(bf16)
+        rows[TAPS : TAPS + 8, lanes] = edges[0:8, :].astype(bf16)
+        if col == 0:
+            for copy, onward in zip(arriving, leaving):
+                copy.wait()
+                onward.start()
+    ending = pltpu.make_async_copy(rows, halo_ref, end_sem.at[1])
+    ending.start()
+    for copy in leaving:
+        copy.wait()
+    ending.wait()
 
 
 def edge(halo_ref, s, lanes):
@@ -185,6 +208,7 @@
 
 def head_kernel(
     width_all,
+    aliased,
     streams_ref,
     first1_ref,
     first2_ref,
@@ -197,14 +221,10 @@
     output_ref,
     gain_ref,
     mixed_ref,
-    grad_ref,
-    inner_ref,
-    first_ref,
-    share_ref,
-    scratch,
-    inverse_ref,
-    along_ref,
+    *refs,
 ):
+    grad_ref, inner_ref, share_ref, first_ref, scratch, inverse_ref, along_ref = refs[3:] if aliased else refs
+
     @pl.when(pl.program_id(0) == 0)
     def _():
         tokens = stats_ref.shape[1]
@@ -290,7 +310,7 @@
     after_ref,
     *refs,
 ):
-    stream_grad_ref, late_ref, scratch, ahead = refs[1:] if aliased else refs
+    stream_grad_ref, late_ref, scratch, ahead = refs[2:] if aliased else refs
     length = streams_ref.shape[1]
     for col in range(streams_ref.shape[2] // LANES):
         lanes = slice(col * LANES, (col + 1) * LANES)
@@ -333,31 +353,30 @@
     return lax.ppermute(value, axis, [(source, source + steps) for source in range(first, last)])
 
 
-def exchange_sum(value, axis):
-    count, reach, other = lax.axis_size(axis), 1, None
-    while reach < count:
-        if other is not None:
-            value = value + other.astype(f32)
-        value = lax.reduce_precision(value, 8, 7)
-        other = lax.ppermute(value.astype(bf16), axis, [(i, i ^ reach) for i in range(count)])
-        reach *= 2
-    return value, other
-
-
-def close_kernel(mine_ref, other_ref, long_ref, short_ref, skip_ref, gain_ref):
-    columns = skip_ref.shape[1] // LANES
-    total = mine_ref[...] + other_ref[...].astype(f32)
-    for col in range(columns):
+def exchange(value, other, axis, reach):
+    if other is not None:
+        value = value + other.astype(f32)
+    value = lax.reduce_precision(value, 8, 7)
+    count = lax.axis_size(axis)
+    return value, lax.ppermute(value.astype(bf16), axis, [(i, i ^ reach) for i in range(count)])
+
+
+def close_kernel(
+    early_ref, early_other_ref, late_ref, late_other_ref, long_ref, short_ref, skip_ref, gain_ref
+):
+    early = early_ref[...] + early_other_ref[...].astype(f32)
+    late = late_ref[...] + late_other_ref[...].astype(f32)
+    for col in range(skip_ref.shape[1] // LANES):
         lanes = slice(col * LANES, (col + 1) * LANES)
-        at, late = col * 16, columns * 16 + col * 8
-        long_ref[col * PER : (col + 1) * PER, :] = total[at : at + PER]
-        skip_ref[:, lanes] = total[at + 8 : at + 9]
-        gain_ref[:, lanes] = total[at + 9 : at + 10]
+        at = col * 16
+        long_ref[col * PER : (col + 1) * PER, :] = early[at : at + PER]
+        skip_ref[:, lanes] = early[at + 8 : at + 9]
+        gain_ref[:, lanes] = early[at + 9 : at + 10]
         for j in range(3):
-            short_ref[0, j : j + 1, lanes] = total[at + 10 + j : at + 11 + j]
+            short_ref[0, j : j + 1, lanes] = early[at + 10 + j : at + 11 + j]
             for s in (1, 2):
-                row = late + (s - 1) * 3 + j
-                short_ref[s, j : j + 1, lanes] = total[row : row + 1]
+                row = col * 8 + (s - 1) * 3 + j
+                short_ref[s, j : j + 1, lanes] = late[row : row + 1]
 
 
 def local(residual, streams, short_filter, long_filter, skip, gain, cotangent):
@@ -366,7 +385,7 @@
     rows_here, width_all = residual.shape
     owners = lax.axis_size("tensor")
     assert long_filter.shape[1] == TAPS and channels == groups * WIDTH and tokens_here % (2 * TAPS) == 0
-    chunks = 2
+    chunks = 1
     part = channels // chunks
     step = min(part, 512)
     steps, all_steps = part // step, channels // step
@@ -393,47 +412,35 @@
         shape = (tokens_here + 8, LANES)
         return pltpu.VMEM(shape if count is None else (count,) + shape, f32)
 
-    def kernel(body, name, micros, **how):
+    def kernel(body, name, micros, limit=VMEM_LIMIT, **how):
         return pl.pallas_call(
             body,
-            compiler_params=params(),
+            compiler_params=params(limit),
             cost_estimate=pl.CostEstimate(flops=0, bytes_accessed=micros * 1000, transcendentals=0),
             name=name,
             **how,
         )
 
-    def last(s):
-        return spec((1, TAPS, step), lambda i: (s, tokens_here // TAPS - 1, i))
-
-    def rows16(s, back):
-        return spec((1, 16, step), lambda i: (s, tokens_here // 16 - back, i))
-
-    rows_a_step = rows_here // all_steps
     packed, halo = kernel(
         open_kernel,
         "open",
         3,
-        grid=(all_steps,),
-        in_specs=[
-            spec((rows_a_step, width_all), lambda i: (i, 0)),
-            spec((rows_a_step, width_all), lambda i: (i, 0)),
-            rows16(0, 1),
-            last(1),
-            last(2),
-            rows16(1, TAPS // 16 + 1),
-            rows16(2, TAPS // 16 + 1),
-            deep(3, 3),
-        ],
-        out_specs=[
-            spec((owners, 2, rows_a_step, channels), lambda i: (0, 0, i, 0)),
-            wide(TAPS + 8),
-        ],
+        in_specs=[spec(memory_space=pl.ANY)] * 3 + [spec(memory_space=pltpu.VMEM)],
+        out_specs=[spec(memory_space=pl.ANY)] * 2,
         out_shape=[
             jax.ShapeDtypeStruct((owners, 2, rows_here, channels), bf16),
             jax.ShapeDtypeStruct((TAPS + 8, channels), bf16),
         ],
-        scratch_shapes=[padded(3)],
-    )(cotangent, residual, streams, streams, streams, streams, streams, short_filter)
+        scratch_shapes=[
+            pltpu.VMEM((owners, 2, rows_here, channels), bf16),
+            pltpu.VMEM((3, TAPS + 16, channels), bf16),
+            pltpu.VMEM((TAPS + 8, channels), bf16),
+            pltpu.VMEM((3, TAPS + 16, LANES), f32),
+            pltpu.SemaphoreType.DMA((owners, 2)),
+            pltpu.SemaphoreType.DMA((owners, 2)),
+            pltpu.SemaphoreType.DMA((2,)),
+        ],
+    )(cotangent, residual, streams, short_filter)
     halo = from_behind(halo, "dp", 1)
     received = lax.all_to_all(packed, "tensor", split_axis=0, concat_axis=0, tiled=True)
 
@@ -475,10 +482,10 @@
         leaving.reshape(owners, rows_here, channels), "tensor", split_axis=0, concat_axis=0, tiled=True
     )
 
-    grads, inner, after, shares = [], [], [], []
+    after, filled = [], []
     for k in range(chunks):
-        grad_k, inner_k, first_k, share_k = kernel(
-            functools.partial(head_kernel, width_all),
+        grads, inner, shares, first = kernel(
+            functools.partial(head_kernel, width_all, bool(filled)),
             "head",
             2,
             grid=(steps,),
@@ -495,43 +502,48 @@
                 wide(tokens_here, k * steps),
                 wide(1, k * steps),
                 spec((16, step), lambda i, k=k: (0, i + k * steps)),
+            ]
+            + [spec(memory_space=pl.ANY)] * len(filled),
+            out_specs=[
+                wide(tokens_here, k * steps),
+                wide(tokens_here, k * steps),
+                wide(1, k * steps),
+                wide(TAPS + 16),
             ],
-            out_specs=[wide(tokens_here), wide(tokens_here), wide(TAPS + 16), wide(1)],
             out_shape=[
-                jax.ShapeDtypeStruct((tokens_here, part), bf16),
-                jax.ShapeDtypeStruct((tokens_here, part), bf16),
+                jax.ShapeDtypeStruct((tokens_here, channels), bf16),
+                jax.ShapeDtypeStruct((tokens_here, channels), bf16),
+                jax.ShapeDtypeStruct((1, channels), f32),
                 jax.ShapeDtypeStruct((TAPS + 16, part), bf16),
-                jax.ShapeDtypeStruct((1, part), f32),
             ],
             scratch_shapes=[padded()] + [pltpu.VMEM((tokens_here, LANES), f32)] * 2,
-        )(streams, streams, streams, halo, short_filter, skip_row, long_filter, stats, received, output, gain_here, mixed)
-        grads.append(grad_k)
-        inner.append(inner_k)
-        shares.append(share_k)
-        after.append(from_behind(first_k, "dp", -1))
-
-    early = []
-    for k in range(chunks):
-        early.append(
-            kernel(
-                sums_kernel,
-                "sums",
-                4,
-                grid=(steps,),
-                in_specs=[
-                    deep(1, tokens_here, k * steps),
-                    wide(TAPS + 8, k * steps),
-                    wide(tokens_here, k * steps),
-                    wide(tokens_here),
-                    wide(tokens_here),
-                    wide(tokens_here, k * steps),
-                    wide(1),
-                ],
-                out_specs=spec((cols * 16, LANES), lambda i: (i, 0)),
-                out_shape=jax.ShapeDtypeStruct((part // LANES * 16, LANES), f32),
-                scratch_shapes=[padded()],
-            )(streams, halo, gated, inner[k], grads[k], mixed, shares[k])
+            input_output_aliases={12 + n: n for n in range(len(filled))},
+        )(
+            *(streams, streams, streams, halo, short_filter, skip_row, long_filter, stats, received, output),
+            *(gain_here, mixed, *filled),
         )
+        filled = [grads, inner, shares]
+        after.append(from_behind(first, "dp", -1))
+
+    early = kernel(
+        sums_kernel,
+        "sums",
+        8,
+        grid=(all_steps,),
+        in_specs=[
+            deep(1, tokens_here),
+            wide(TAPS + 8),
+            wide(tokens_here),
+            wide(tokens_here),
+            wide(tokens_here),
+            wide(tokens_here),
+            wide(1),
+        ],
+        out_specs=spec((cols * 16, LANES), lambda i: (i, 0)),
+        out_shape=jax.ShapeDtypeStruct((channels // LANES * 16, LANES), f32),
+        scratch_shapes=[padded()],
+    )(streams, halo, gated, inner, grads, mixed, shares)
+
     block = min(rows_here, 16)
     by_rows = spec((block, width_all), lambda i: (i, 0))
     normed, grad_residual = kernel(
@@ -550,54 +562,61 @@
         scratch_shapes=[pltpu.VMEM((block, width_all), f32)],
     )(rows_received, residual, cotangent, gain_row)
 
-    stream_grad, late = None, []
+    reaches = [1 << n for n in range((lax.axis_size("dp") - 1).bit_length())]
+    waiting = list(reaches)
+    early_other, filled = None, []
     for k in range(chunks):
-        aliased = stream_grad is not None
-        operands = [streams, halo, short_filter, skip_row, behind_bands, grads[k], mixed, inner[k], after[k]]
-        in_specs = [
-            deep(3, tokens_here, k * steps),
-            wide(TAPS + 8, k * steps),
-            deep(3, 3, k * steps),
-            wide(1, k * steps),
-            bands_of(k * steps),
-            wide(tokens_here),
-            wide(tokens_here, k * steps),
-            wide(tokens_here),
-            wide(TAPS + 16),
-        ]
-        if aliased:
-            operands.append(stream_grad)
-            in_specs.append(spec(memory_space=pl.ANY))
-        stream_grad, late_k = kernel(
-            functools.partial(backward_kernel, aliased),
+        if waiting:
+            early = early if early_other is None else early + early_other.astype(f32)
+            early, after[k] = lax.optimization_barrier((early, after[k]))
+            early, early_other = exchange(early, None, "dp", waiting.pop(0))
+        stream_grad, late = kernel(
+            functools.partial(backward_kernel, bool(filled)),
             "backward",
             5,
             grid=(steps,),
-            in_specs=in_specs,
+            in_specs=[
+                deep(3, tokens_here, k * steps),
+                wide(TAPS + 8, k * steps),
+                deep(3, 3, k * steps),
+                wide(1, k * steps),
+                bands_of(k * steps),
+                wide(tokens_here, k * steps),
+                wide(tokens_here, k * steps),
+                wide(tokens_here, k * steps),
+                wide(TAPS + 16),
+            ]
+            + [spec(memory_space=pl.ANY)] * len(filled),
             out_specs=[
                 deep(3, tokens_here, k * steps),
-                spec((cols * 8, LANES), lambda i: (i, 0)),
+                spec((cols * 8, LANES), lambda i, k=k: (i + k * steps, 0)),
             ],
             out_shape=[
                 jax.ShapeDtypeStruct(streams.shape, bf16),
-                jax.ShapeDtypeStruct((part // LANES * 8, LANES), f32),
+                jax.ShapeDtypeStruct((channels // LANES * 8, LANES), f32),
             ],
             scratch_shapes=[padded(3), padded(3)],
-            input_output_aliases={len(operands) - 1: 0} if aliased else {},
-        )(*operands)
-        late.append(late_k)
-    mine, other = exchange_sum(jnp.concatenate(early + late, axis=0), "dp")
+            input_output_aliases={9 + n: n for n in range(len(filled))},
+        )(streams, halo, short_filter, skip_row, behind_bands, grads, mixed, inner, after[k], *filled)
+        filled = [stream_grad, late]
+    for reach in waiting:
+        early, early_other = exchange(early, early_other, "dp", reach)
+    late_other = None
+    for reach in reaches:
+        late, late_other = exchange(late, late_other, "dp", reach)
+    late, normed, grad_residual = lax.optimization_barrier((late, normed, grad_residual))
     long_grad, short_grad, skip_grad, gain_grad = kernel(
         close_kernel,
         "close",
         1,
+        SMALL_LIMIT,
         out_shape=[
             jax.ShapeDtypeStruct((groups, TAPS), f32),
             jax.ShapeDtypeStruct((3, 3, channels), f32),
             jax.ShapeDtypeStruct((1, channels), f32),
             jax.ShapeDtypeStruct((1, channels), f32),
         ],
-    )(mine, other)
+    )(early, early_other, late, late_other)
     skip_grad, gain_grad = skip_grad.reshape(channels), gain_grad.reshape(channels)
     return (normed, grad_residual, stream_grad, long_grad, short_grad, skip_grad, gain_grad)
 

time: 118 us -> 106 us (0.90)
  Pallas kernels: 60 us -> 53 us
  local copies, waits for them, and re-layouts: 6.51 us -> 3.17 us
  starting transfers between devices: 26 us -> 24.3 us
    pallas_call x8 -> x5, Pallas kernels: 37.7 us -> 30.7 us  [the longest x1 10.6 us: local(): kernel(functools.partial(backward_kernel, bool(filled)), 'backward', 5, g...]
    ppermute x3 -> x6, waiting for transfers between devices: 8.84 us -> 3.47 us  [exchange(): lax.ppermute(value.astype(bf16), axis, [(i, i ^ reach) for i in range(cou...]
    ppermute x3 -> x2, waiting for transfers between devices: 4.44 us -> 9.47 us  [from_behind(): lax.ppermute(value, axis, [(source, source + steps) for source in range(f...]
    unnamed x20 -> x10, local copies, waits for them, and re-layouts: 5.21 us -> 1.88 us
    ppermute x3 -> x6, starting transfers between devices: 11.2 us -> 9.93 us  [exchange(): lax.ppermute(value.astype(bf16), axis, [(i, i ^ reach) for i in range(cou...]
    ppermute x3 -> x2, starting transfers between devices: 6.91 us -> 6.2 us  [from_behind(): lax.ppermute(value, axis, [(source, source + steps) for source in range(f...]
    convert_element_type x3 -> x6, other arithmetic: 3.06 us -> 3.65 us  [exchange(): value.astype(bf16)]
  transfers between devices with their start and end apart: 8 -> 10, of which waited for: 5 -> 5; matrix products, arithmetic and copies ran while one was open for 4% -> 5% of each run, Pallas kernels for 37% -> 36%
where the time goes in v3:
time: 106 us; the launch traced here: 105 us
  Pallas kernels  53 us (50%)
  starting transfers between devices  24.3 us (23%)
  waiting for transfers between devices  13.5 us (13%)
  blocking collectives  6.33 us (6%)
  other arithmetic  3.65 us (3%)
  local copies, waits for them, and re-layouts  3.17 us (3%)
    pallas_call x1, Pallas kernels, local(): kernel(functools.partial(backward_kernel, bool(filled)), 'backward', 5, g...  10.6 us
    ppermute x6, starting transfers between devices, exchange(): lax.ppermute(value.astype(bf16), axis, [(i, i ^ reach) for i in range(cou...  9.93 us
    ppermute x2, waiting for transfers between devices, from_behind(): lax.ppermute(value, axis, [(source, source + steps) for source in range(f...  9.47 us
    pallas_call x1, Pallas kernels, local(): kernel(sums_kernel, 'sums', 8, grid=(all_steps,), in_specs=[deep(1, token...  7.98 us
    pallas_call x1, Pallas kernels, local(): kernel(forward_kernel, 'forward', 5, grid=(all_steps,), in_specs=[deep(3,...  7.5 us
    pallas_call x1, Pallas kernels, local(): kernel(bands_kernel, 'bands', 5, grid=(groups // each,), in_specs=[spec((...  6.7 us
    pallas_call x1, Pallas kernels, local(): kernel(functools.partial(head_kernel, width_all, bool(filled)), 'head', 2...  6.67 us
    psum x1, blocking collectives, local(): stats = lax.psum(stats, 'tensor')  6.33 us
  transfers between devices with their start and end apart: 10, of which 5 were waited for; matrix products, arithmetic and copies ran while one was open for 5% of the time, Pallas kernels for 36%

profile of v3, /device:TPU:0, one launch (start us, length us, event | category | flops | bytes accessed | tf_op | source)
XLA Modules:
  0.0 104.8 jit_solution(8928941782592262978)
XLA Ops:
  0.6 4.7 %open.1 = (bf16[4,2,64,2048]{3,2,1,0:T(8,128)(2,1)}, bf16[136,2048]{1,0:T(8,128)(2,1)}) custom-call(bf16[64,8192]{1,0:T(8,128)(2,1)} %cot_ref.3, bf16[64,8192]{1,0:T(8,128)(2,1)} %residual_ref.3, bf16[3,256,2048]{2,1,0:T(8,128)(2,1)} %streams_ref.9, f32[3,3,2048]{2,1,0:T(4,128)} %taps_ref.7), custom_call_target="tpu_custom_call" | custom-call | bytes 3000 | tf_op jit(solution)/shard_map/open/pallas_call | solution.py:424
  5.3 0.0 copy-start.4
  5.3 4.6 %all-to-all-start = ((bf16[4,2,64,2048]{3,2,1,0:T(8,128)(2,1)}), bf16[4,2,64,2048]{3,2,1,0:T(8,128)(2,1)}, u32[]{:S(2)}, u32[]{:S(2)}) async-start(bf16[4,2,64,2048]{3,2,1,0:T(8,128)(2,1)} %get-tuple-element.35), calls=%async_computation | async-start | bytes 4194304 | tf_op jit(solution)/shard_map/all_to_all | solution.py:445
  10.0 0.0 copy-done.4
  10.0 4.9 %collective-permute-start = (bf16[136,2048]{1,0:T(8,128)(2,1)S(1)}, bf16[136,2048]{1,0:T(8,128)(2,1)S(1)}, u32[]{:S(2)}, u32[]{:S(2)}) collective-permute-start(bf16[136,2048]{1,0:T(8,128)(2,1)S(1)} %copy-done.4), channel_id=1, source_target_pairs={{0,4},{4,8},{8,12},{12,16},{16,20},{20,24},{24,28},{1,5},{5,9},{9,... | collective-permute-start | bytes 1671176 | tf_op jit(solution)/shard_map/ppermute | solution.py:353
  14.9 6.7 %bands.1 = (bf16[128,64,256]{2,1,0:T(8,128)(2,1)}, bf16[128,64,256]{2,1,0:T(8,128)(2,1)}) custom-call(f32[128,128]{1,0:T(8,128)} %filter_ref.3), custom_call_target="tpu_custom_call" | custom-call | bytes 5000 | tf_op jit(solution)/shard_map/bands/pallas_call | solution.py:449
  21.6 1.3 %dynamic_slice.3 = f32[2048]{0:T(1024)} dynamic-slice(f32[8192]{0:T(1024)} %param.12, s32[]{:T(128)S(6)} %select_n.3), dynamic_slice_sizes={2048} | dynamic-slice | bytes 16388 | tf_op jit(solution)/shard_map/dynamic_slice | solution.py:395
  22.9 4.4 %collective-permute-done.halo_ref = bf16[136,2048]{1,0:T(8,128)(2,1)S(1)} collective-permute-done((bf16[136,2048]{1,0:T(8,128)(2,1)S(1)}, bf16[136,2048]{1,0:T(8,128)(2,1)S(1)}, u32[]{:S(2)}, u32[]{:S(2)}) %collective-permute-start) | collective-permute-done | bytes 557088 | tf_op jit(solution)/shard_map/ppermute | solution.py:353
  27.3 0.0 copy-start
  27.3 0.9 copy-done
  28.2 7.5 %forward.1 = (bf16[256,2048]{1,0:T(8,128)(2,1)}, f32[256,2048]{1,0:T(8,128)}, bf16[256,2048]{1,0:T(8,128)(2,1)}) custom-call(bf16[3,256,2048]{2,1,0:T(8,128)(2,1)} %streams_ref.9, bf16[136,2048]{1,0:T(8,128)(2,1)} %copy-done, f32[3,3,2048]{2,1,0:T(4,128)} %taps_ref.7, f32[1,2048]{1,0:T(1,128)} %bitcast.8, bf16[128,64,256]{2,1,0:T(8,128)(2,1)} %get-tuple-element.36.ahead_ref), custom_call_target="tpu_custom_call" | custom-call | bytes 5000 | tf_op jit(solution)/shard_map/forward/pallas_call | solution.py:459
  35.7 0.6 all-to-all-done.received_ref
  36.3 3.6 %stats.1 = f32[2,256]{1,0:T(2,128)} custom-call(bf16[4,2,64,2048]{3,2,1,0:T(8,128)(2,1)} %all-to-all-done.received_ref, bf16[256,2048]{1,0:T(8,128)(2,1)} %get-tuple-element.47.output_ref, f32[1,2048]{1,0:T(1,128)} %bitcast.6), custom_call_target="tpu_custom_call" | custom-call | bytes 2000 | tf_op jit(solution)/shard_map/stats/pallas_call | solution.py:469
  39.9 6.3 %psum.7.stats_ref = f32[2,256]{1,0:T(2,128)} all-reduce(f32[2,256]{1,0:T(2,128)} %stats.1), channel_id=1, replica_groups=mesh['dp'=8,'tensor'=4] {'tensor'}, use_global_device_ids=true, to_apply=%region_0.0 | all-reduce | flops 512 | bytes 4096 | tf_op jit(solution)/shard_map/psum | solution.py:479
  46.3 6.7 %head.1 = (bf16[256,2048]{1,0:T(8,128)(2,1)}, bf16[256,2048]{1,0:T(8,128)(2,1)}, f32[1,2048]{1,0:T(1,128)}, bf16[144,2048]{1,0:T(8,128)(2,1)}) custom-call(bf16[3,256,2048]{2,1,0:T(8,128)(2,1)} %streams_ref.9, bf16[3,256,2048]{2,1,0:T(8,128)(2,1)} %streams_ref.9, bf16[3,256,2048]{2,1,0:T(8,128)(2,1)} %streams_ref.9, bf16[136,2048]{1,0:T(8,128)(2,1)} %copy-done, ...), custom_call_target="tpu_custom_call" | custom-call | bytes 2000 | tf_op jit(solution)/shard_map/head/pallas_call | solution.py:487
  52.9 1.3 %collective-permute-start.1 = (bf16[144,2048]{1,0:T(8,128)(2,1)}, bf16[144,2048]{1,0:T(8,128)(2,1)S(1)}, u32[]{:S(2)}, u32[]{:S(2)}) collective-permute-start(bf16[144,2048]{1,0:T(8,128)(2,1)} %get-tuple-element.44), channel_id=1, source_target_pairs={{4,0},{8,4},{12,8},{16,12},{20,16},{24,20},{28,24},{5,1},{9,5},{13... | collective-permute-start | bytes 1769480 | tf_op jit(solution)/shard_map/ppermute | solution.py:353
  54.2 3.5 %all-to-all-start.1 = ((bf16[4,64,2048]{2,1,0:T(8,128)(2,1)}), bf16[4,64,2048]{2,1,0:T(8,128)(2,1)S(1)}, u32[]{:S(2)}, u32[]{:S(2)}) async-start(bf16[4,64,2048]{2,1,0:T(8,128)(2,1)} %bitcast.2), calls=%async_computation.1 | async-start | bytes 2097152 | tf_op jit(solution)/shard_map/all_to_all | solution.py:481
  57.8 8.0 %sums.1 = f32[256,128]{1,0:T(8,128)} custom-call(bf16[3,256,2048]{2,1,0:T(8,128)(2,1)} %streams_ref.9, bf16[136,2048]{1,0:T(8,128)(2,1)} %copy-done, bf16[256,2048]{1,0:T(8,128)(2,1)} %get-tuple-element.42.gated_ref, bf16[256,2048]{1,0:T(8,128)(2,1)} %get-tuple-element.41.inner_ref, bf16[256,2048]{1,0:T(8,128)(2,1)} %get-tuple-element.40.grad_ref, ...), custom_call_target="tpu_custom_call" | custom-call | bytes 8000 | tf_op jit(solution)/shard_map/sums/pallas_call | solution.py:528
  65.8 5.0 %collective-permute-done.1.after_ref = bf16[144,2048]{1,0:T(8,128)(2,1)S(1)} collective-permute-done((bf16[144,2048]{1,0:T(8,128)(2,1)}, bf16[144,2048]{1,0:T(8,128)(2,1)S(1)}, u32[]{:S(2)}, u32[]{:S(2)}) %collective-permute-start.1) | collective-permute-done | bytes 589856 | tf_op jit(solution)/shard_map/ppermute | solution.py:353
  70.8 0.0 copy-start.3
  70.8 1.0 reduce-precision_convert_fusion
  71.8 2.6 %collective-permute-start.4 = (bf16[256,128]{1,0:T(8,128)(2,1)S(1)}, bf16[256,128]{1,0:T(8,128)(2,1)S(1)}, u32[]{:S(2)}, u32[]{:S(2)}) collective-permute-start(bf16[256,128]{1,0:T(8,128)(2,1)S(1)} %reduce-precision_convert_fusion), channel_id=1, source_target_pairs={{0,4},{4,0},{8,12},{12,8},{16,20},{20,16},{24,28},{28,24},{1,5},{5... | collective-permute-start | bytes 196616 | tf_op jit(solution)/shard_map/ppermute | solution.py:361
  74.5 0.0 copy-done.3
  74.5 0.0 copy-start.2
  74.5 10.6 %backward.1 = (bf16[3,256,2048]{2,1,0:T(8,128)(2,1)}, f32[128,128]{1,0:T(8,128)}) custom-call(bf16[3,256,2048]{2,1,0:T(8,128)(2,1)} %streams_ref.9, bf16[136,2048]{1,0:T(8,128)(2,1)} %copy-done, f32[3,3,2048]{2,1,0:T(4,128)} %taps_ref.7, f32[1,2048]{1,0:T(1,128)} %bitcast.10, bf16[128,64,256]{2,1,0:T(8,128)(2,1)} %get-tuple-element.34.behind_ref, ...), custom_call_target="tpu_custom_call" | custom-call | bytes 5000 | tf_op jit(solution)/shard_map/backward/pallas_call | solution.py:573
  85.1 0.8 reduce-precision_convert_fusion.1
  86.0 0.0 collective-permute-start.2
  86.0 0.0 collective-permute-done.4
  86.0 0.0 copy-done.2
  86.0 1.7 %collective-permute-start.5 = (bf16[256,128]{1,0:T(8,128)(2,1)S(1)}, bf16[256,128]{1,0:T(8,128)(2,1)S(1)}, u32[]{:S(2)}, u32[]{:S(2)}) collective-permute-start(bf16[256,128]{1,0:T(8,128)(2,1)S(1)} %fusion), channel_id=1, source_target_pairs={{0,8},{4,12},{8,0},{12,4},{16,24},{20,28},{24,16},{28,20},{1,9},{5... | collective-permute-start | bytes 196616 | tf_op jit(solution)/shard_map/ppermute | solution.py:361
  87.7 2.2 %collective-permute-done.2 = bf16[128,128]{1,0:T(8,128)(2,1)S(1)} collective-permute-done((bf16[128,128]{1,0:T(8,128)(2,1)S(1)}, bf16[128,128]{1,0:T(8,128)(2,1)S(1)}, u32[]{:S(2)}, u32[]{:S(2)}) %collective-permute-start.2) | collective-permute-done | bytes 32800 | tf_op jit(solution)/shard_map/ppermute | solution.py:361
  89.9 0.9 fusion.1
  90.7 1.6 %collective-permute-start.3 = (bf16[128,128]{1,0:T(8,128)(2,1)S(1)}, bf16[128,128]{1,0:T(8,128)(2,1)S(1)}, u32[]{:S(2)}, u32[]{:S(2)}) collective-permute-start(bf16[128,128]{1,0:T(8,128)(2,1)S(1)} %fusion.1), channel_id=1, source_target_pairs={{0,8},{4,12},{8,0},{12,4},{16,24},{20,28},{24,16},{28,20},{1,9},{5... | collective-permute-start | bytes 98312 | tf_op jit(solution)/shard_map/ppermute | solution.py:361
  92.4 0.0 collective-permute-done.5
  92.4 1.1 %collective-permute-start.6 = (bf16[256,128]{1,0:T(8,128)(2,1)S(1)}, bf16[256,128]{1,0:T(8,128)(2,1)S(1)}, u32[]{:S(2)}, u32[]{:S(2)}) collective-permute-start(bf16[256,128]{1,0:T(8,128)(2,1)S(1)} %get-tuple-element.61), channel_id=1, source_target_pairs={{0,16},{4,20},{8,24},{12,28},{16,0},{20,4},{24,8},{28,12},{1,17},{... | collective-permute-start | bytes 196616 | tf_op jit(solution)/shard_map/ppermute | solution.py:361
  93.5 1.3 %collective-permute-done.3 = bf16[128,128]{1,0:T(8,128)(2,1)S(1)} collective-permute-done((bf16[128,128]{1,0:T(8,128)(2,1)S(1)}, bf16[128,128]{1,0:T(8,128)(2,1)S(1)}, u32[]{:S(2)}, u32[]{:S(2)}) %collective-permute-start.3) | collective-permute-done | bytes 32800 | tf_op jit(solution)/shard_map/ppermute | solution.py:361
  94.8 0.9 fusion.2
  95.6 2.9 %collective-permute-start.7 = (bf16[128,128]{1,0:T(8,128)(2,1)S(1)}, bf16[128,128]{1,0:T(8,128)(2,1)S(1)}, u32[]{:S(2)}, u32[]{:S(2)}) collective-permute-start(bf16[128,128]{1,0:T(8,128)(2,1)S(1)} %get-tuple-element.59), channel_id=1, source_target_pairs={{0,16},{4,20},{8,24},{12,28},{16,0},{20,4},{24,8},{28,12},{1,17},{... | collective-permute-start | bytes 98312 | tf_op jit(solution)/shard_map/ppermute | solution.py:361
  98.5 0.0 all-to-all-done.1.received_ref
  98.5 0.0 copy-start.1
  98.5 1.0 copy-done.1
  99.5 4.5 %norm.1 = (bf16[64,8192]{1,0:T(8,128)(2,1)}, bf16[64,8192]{1,0:T(8,128)(2,1)}) custom-call(bf16[4,64,2048]{2,1,0:T(8,128)(2,1)} %copy-done.1, bf16[64,8192]{1,0:T(8,128)(2,1)} %residual_ref.3, bf16[64,8192]{1,0:T(8,128)(2,1)} %cot_ref.3, f32[1,8192]{1,0:T(1,128)} %bitcast.11), custom_call_target="tpu_custom_call" | custom-call | bytes 4000 | tf_op jit(solution)/shard_map/norm/pallas_call | solution.py:549
  104.0 0.0 collective-permute-done.7.late_other_ref
  104.0 0.0 collective-permute-done.6.early_other_ref
  104.0 0.7 close.1
  (2 shorter events, 0.1 us)
Async XLA Ops:
  5.3 4.7 %copy-start.4 = (bf16[136,2048]{1,0:T(8,128)(2,1)S(1)}, bf16[136,2048]{1,0:T(8,128)(2,1)}, u32[]{:S(2)}) copy-start(bf16[136,2048]{1,0:T(8,128)(2,1)} %get-tuple-element.33) | copy-start | bytes 1671172
  5.3 31.0 %all-to-all-start = ((bf16[4,2,64,2048]{3,2,1,0:T(8,128)(2,1)}), bf16[4,2,64,2048]{3,2,1,0:T(8,128)(2,1)}, u32[]{:S(2)}, u32[]{:S(2)}) async-start(bf16[4,2,64,2048]{3,2,1,0:T(8,128)(2,1)} %get-tuple-element.35), calls=%async_computation | async-start | bytes 4194304 | tf_op jit(solution)/shard_map/all_to_all | solution.py:445
  10.0 17.4 %collective-permute-start = (bf16[136,2048]{1,0:T(8,128)(2,1)S(1)}, bf16[136,2048]{1,0:T(8,128)(2,1)S(1)}, u32[]{:S(2)}, u32[]{:S(2)}) collective-permute-start(bf16[136,2048]{1,0:T(8,128)(2,1)S(1)} %copy-done.4), channel_id=1, source_target_pairs={{0,4},{4,8},{8,12},{12,16},{16,20},{20,24},{24,28},{1,5},{5,9},{9,... | collective-permute-start | bytes 1671176 | tf_op jit(solution)/shard_map/ppermute | solution.py:353
  27.3 0.9 copy-start
  52.9 17.9 %collective-permute-start.1 = (bf16[144,2048]{1,0:T(8,128)(2,1)}, bf16[144,2048]{1,0:T(8,128)(2,1)S(1)}, u32[]{:S(2)}, u32[]{:S(2)}) collective-permute-start(bf16[144,2048]{1,0:T(8,128)(2,1)} %get-tuple-element.44), channel_id=1, source_target_pairs={{4,0},{8,4},{12,8},{16,12},{20,16},{24,20},{28,24},{5,1},{9,5},{13... | collective-permute-start | bytes 1769480 | tf_op jit(solution)/shard_map/ppermute | solution.py:353
  54.2 44.3 %all-to-all-start.1 = ((bf16[4,64,2048]{2,1,0:T(8,128)(2,1)}), bf16[4,64,2048]{2,1,0:T(8,128)(2,1)S(1)}, u32[]{:S(2)}, u32[]{:S(2)}) async-start(bf16[4,64,2048]{2,1,0:T(8,128)(2,1)} %bitcast.2), calls=%async_computation.1 | async-start | bytes 2097152 | tf_op jit(solution)/shard_map/all_to_all | solution.py:481
  70.8 3.7 %copy-start.3 = (bf16[144,2048]{1,0:T(8,128)(2,1)}, bf16[144,2048]{1,0:T(8,128)(2,1)S(1)}, u32[]{:S(2)}) copy-start(bf16[144,2048]{1,0:T(8,128)(2,1)S(1)} %collective-permute-done.1.after_ref) | copy-start | bytes 1769476
  71.8 14.2 %collective-permute-start.4 = (bf16[256,128]{1,0:T(8,128)(2,1)S(1)}, bf16[256,128]{1,0:T(8,128)(2,1)S(1)}, u32[]{:S(2)}, u32[]{:S(2)}) collective-permute-start(bf16[256,128]{1,0:T(8,128)(2,1)S(1)} %reduce-precision_convert_fusion), channel_id=1, source_target_pairs={{0,4},{4,0},{8,12},{12,8},{16,20},{20,16},{24,28},{28,24},{1,5},{5... | collective-permute-start | bytes 196616 | tf_op jit(solution)/shard_map/ppermute | solution.py:361
  74.5 11.5 %copy-start.2 = (f32[256,128]{1,0:T(8,128)S(1)}, f32[256,128]{1,0:T(8,128)}, u32[]{:S(2)}) copy-start(f32[256,128]{1,0:T(8,128)} %sums.1) | copy-start | bytes 393220
  86.0 3.9 %collective-permute-start.2 = (bf16[128,128]{1,0:T(8,128)(2,1)S(1)}, bf16[128,128]{1,0:T(8,128)(2,1)S(1)}, u32[]{:S(2)}, u32[]{:S(2)}) collective-permute-start(bf16[128,128]{1,0:T(8,128)(2,1)S(1)} %reduce-precision_convert_fusion.1), channel_id=1, source_target_pairs={{0,4},{4,0},{8,12},{12,8},{16,20},{20,16},{24,28},{28,24},{1,5},{5... | collective-permute-start | bytes 98312 | tf_op jit(solution)/shard_map/ppermute | solution.py:361
  86.0 6.3 %collective-permute-start.5 = (bf16[256,128]{1,0:T(8,128)(2,1)S(1)}, bf16[256,128]{1,0:T(8,128)(2,1)S(1)}, u32[]{:S(2)}, u32[]{:S(2)}) collective-permute-start(bf16[256,128]{1,0:T(8,128)(2,1)S(1)} %fusion), channel_id=1, source_target_pairs={{0,8},{4,12},{8,0},{12,4},{16,24},{20,28},{24,16},{28,20},{1,9},{5... | collective-permute-start | bytes 196616 | tf_op jit(solution)/shard_map/ppermute | solution.py:361
  90.7 4.1 %collective-permute-start.3 = (bf16[128,128]{1,0:T(8,128)(2,1)S(1)}, bf16[128,128]{1,0:T(8,128)(2,1)S(1)}, u32[]{:S(2)}, u32[]{:S(2)}) collective-permute-start(bf16[128,128]{1,0:T(8,128)(2,1)S(1)} %fusion.1), channel_id=1, source_target_pairs={{0,8},{4,12},{8,0},{12,4},{16,24},{20,28},{24,16},{28,20},{1,9},{5... | collective-permute-start | bytes 98312 | tf_op jit(solution)/shard_map/ppermute | solution.py:361
  92.4 11.6 %collective-permute-start.6 = (bf16[256,128]{1,0:T(8,128)(2,1)S(1)}, bf16[256,128]{1,0:T(8,128)(2,1)S(1)}, u32[]{:S(2)}, u32[]{:S(2)}) collective-permute-start(bf16[256,128]{1,0:T(8,128)(2,1)S(1)} %get-tuple-element.61), channel_id=1, source_target_pairs={{0,16},{4,20},{8,24},{12,28},{16,0},{20,4},{24,8},{28,12},{1,17},{... | collective-permute-start | bytes 196616 | tf_op jit(solution)/shard_map/ppermute | solution.py:361
  95.6 8.4 %collective-permute-start.7 = (bf16[128,128]{1,0:T(8,128)(2,1)S(1)}, bf16[128,128]{1,0:T(8,128)(2,1)S(1)}, u32[]{:S(2)}, u32[]{:S(2)}) collective-permute-start(bf16[128,128]{1,0:T(8,128)(2,1)S(1)} %get-tuple-element.59), channel_id=1, source_target_pairs={{0,16},{4,20},{8,24},{12,28},{16,0},{20,4},{24,8},{28,12},{1,17},{... | collective-permute-start | bytes 98312 | tf_op jit(solution)/shard_map/ppermute | solution.py:361
  98.5 1.0 copy-start.1

commit v4 on v3

--- a/solution.py
+++ b/solution.py
@@ -16,6 +16,8 @@
 SPAN = 256
 VMEM_LIMIT = 62
 SMALL_LIMIT = 8
+NORM_LIMIT = 24
+STEP = 512
 f32 = jnp.float32
 bf16 = jnp.bfloat16
 
@@ -138,7 +140,7 @@
     return taps[0:1] * now + taps[1:2] * one + taps[2:3] * two
 
 
-def forward_kernel(streams_ref, halo_ref, taps_ref, skip_ref, ahead_ref, output_ref, mixed_ref, gated_ref, scratch):
+def forward_kernel(index, streams_ref, halo_ref, taps_ref, skip_ref, ahead_ref, output_ref, mixed_ref, gated_ref, scratch):
     length = streams_ref.shape[1]
     for col in range(streams_ref.shape[2] // LANES):
         lanes = slice(col * LANES, (col + 1) * LANES)
@@ -160,8 +162,8 @@
     return piece.reshape(piece.shape[0] * piece.shape[1], LANES)
 
 
-def stats_kernel(received_ref, output_ref, gain_ref, stats_ref, squares_ref, products_ref):
-    @pl.when(pl.program_id(0) == 0)
+def stats_kernel(count, index, received_ref, output_ref, gain_ref, stats_ref, squares_ref, products_ref):
+    @pl.when(index == 0)
     def _():
         squares_ref[...] = jnp.zeros_like(squares_ref)
         products_ref[...] = jnp.zeros_like(products_ref)
@@ -175,7 +177,7 @@
     squares_ref[...] = squares
     products_ref[...] = products
 
-    @pl.when(pl.program_id(0) == pl.num_programs(0) - 1)
+    @pl.when(index == count - 1)
     def _():
         for row, sums in ((0, squares), (1, products)):
             stats_ref[row : row + 1, :] = jnp.sum(sums.T, axis=0, keepdims=True)
@@ -208,7 +210,7 @@
 
 def head_kernel(
     width_all,
-    aliased,
+    index,
     streams_ref,
     first1_ref,
     first2_ref,
@@ -221,11 +223,15 @@
     output_ref,
     gain_ref,
     mixed_ref,
-    *refs,
+    grad_ref,
+    inner_ref,
+    share_ref,
+    first_ref,
+    scratch,
+    inverse_ref,
+    along_ref,
 ):
-    grad_ref, inner_ref, share_ref, first_ref, scratch, inverse_ref, along_ref = refs[3:] if aliased else refs
-
-    @pl.when(pl.program_id(0) == 0)
+    @pl.when(index == 0)
     def _():
         tokens = stats_ref.shape[1]
         squares = jnp.broadcast_to(stats_ref[0:1, :], (LANES, tokens)).T
@@ -268,7 +274,7 @@
         first_ref[TAPS + 8 : TAPS + 16, lanes] = (rows - high.astype(f32)).astype(bf16)
 
 
-def sums_kernel(streams_ref, halo_ref, gated_ref, inner_ref, grad_ref, mixed_ref, gain_ref, early_ref, scratch):
+def sums_kernel(index, streams_ref, halo_ref, gated_ref, inner_ref, grad_ref, mixed_ref, gain_ref, early_ref, scratch):
     length = streams_ref.shape[1]
     blocks = length // BLOCK
     flip = anti_identity(SPAN)
@@ -298,7 +304,7 @@
 
 
 def backward_kernel(
-    aliased,
+    index,
     streams_ref,
     halo_ref,
     taps_ref,
@@ -308,9 +314,11 @@
     mixed_ref,
     inner_ref,
     after_ref,
-    *refs,
+    stream_grad_ref,
+    late_ref,
+    scratch,
+    ahead,
 ):
-    stream_grad_ref, late_ref, scratch, ahead = refs[2:] if aliased else refs
     length = streams_ref.shape[1]
     for col in range(streams_ref.shape[2] // LANES):
         lanes = slice(col * LANES, (col + 1) * LANES)
@@ -353,19 +361,23 @@
     return lax.ppermute(value, axis, [(source, source + steps) for source in range(first, last)])
 
 
-def exchange(value, other, axis, reach):
-    if other is not None:
-        value = value + other.astype(f32)
+def sent_to(value, axis, distances):
     value = lax.reduce_precision(value, 8, 7)
     count = lax.axis_size(axis)
-    return value, lax.ppermute(value.astype(bf16), axis, [(i, i ^ reach) for i in range(count)])
-
-
-def close_kernel(
-    early_ref, early_other_ref, late_ref, late_other_ref, long_ref, short_ref, skip_ref, gain_ref
-):
-    early = early_ref[...] + early_other_ref[...].astype(f32)
-    late = late_ref[...] + late_other_ref[...].astype(f32)
+    half = value.astype(bf16)
+    return value, [lax.ppermute(half, axis, [(i, i ^ d) for i in range(count)]) for d in distances]
+
+
+def added(value, others):
+    terms = [value] + [other.astype(f32) for other in others]
+    while len(terms) > 1:
+        terms = [terms[i] + terms[i + 1] for i in range(0, len(terms), 2)]
+    return terms[0]
+
+
+def close_kernel(mine_ref, other_ref, long_ref, short_ref, skip_ref, gain_ref):
+    total = mine_ref[...] + other_ref[...].astype(f32)
+    early, late = total[: skip_ref.shape[1] // LANES * 16], total[skip_ref.shape[1] // LANES * 16 :]
     for col in range(skip_ref.shape[1] // LANES):
         lanes = slice(col * LANES, (col + 1) * LANES)
         at = col * 16
@@ -379,34 +391,114 @@
                 short_ref[s, j : j + 1, lanes] = late[row : row + 1]
 
 
+def streamed(body, name, count, inputs, outputs, scratch_shapes=()):
+    inputs = [(array if isinstance(array, tuple) else (array,), picks, split) for array, picks, split in inputs]
+    firsts = [sum(len(arrays) for arrays, _, _ in inputs[:at]) for at in range(len(inputs) + 1)]
+
+    def piece(ref, split, i, count=count):
+        size = ref.shape[split] // count
+        start = i * size
+        if not isinstance(start, int):
+            start = pl.multiple_of(start, size)
+        return ref.at[tuple(pl.ds(start, size) if d == split else slice(None) for d in range(len(ref.shape)))]
+
+    def kernel(*refs):
+        n, m = len(inputs), len(outputs)
+        sources, refs = refs[: firsts[-1]], refs[firsts[-1] :]
+        targets, held, made = refs[:m], refs[m : m + n], refs[m + n : 2 * m + n]
+        in_sem, out_sem = refs[2 * m + n : 2 * m + n + 2]
+        own = refs[2 * m + n + 2 :]
+
+        def fetch(at, i, array=0):
+            arrays, picks, split = inputs[at]
+            source, target = sources[firsts[at] + array], held[at]
+            if picks:
+                source = source.at[tuple(pl.ds(*picks[d]) if d in picks else slice(None) for d in range(arrays[0].ndim))]
+            if isinstance(split, int):
+                share = count // len(arrays)
+                source, target = piece(source, split, i - array * share, share), piece(target, split, i)
+            elif len(arrays) > 1:
+                target = piece(target, split[0], array, len(arrays))
+            return pltpu.make_async_copy(source, target, in_sem.at[at, array if isinstance(split, tuple) else i])
+
+        def send(at, i):
+            split = outputs[at][2]
+            source, target = made[at], targets[at]
+            if isinstance(split, int):
+                source, target = piece(source, split, i), piece(target, split, i)
+            return pltpu.make_async_copy(source, target, out_sem.at[at, i])
+
+        whole_in = [at for at in range(n) if not isinstance(inputs[at][2], int)]
+        split_in = [at for at in range(n) if isinstance(inputs[at][2], int)]
+        whole_out = [at for at in range(m) if not isinstance(outputs[at][2], int)]
+        split_out = [at for at in range(m) if isinstance(outputs[at][2], int)]
+        whole_parts = [(at, array) for at in whole_in for array in range(len(inputs[at][0]))]
+        for at, array in whole_parts:
+            fetch(at, 0, array).start()
+        for i in range(count):
+            for at in split_in:
+                fetch(at, i, i * len(inputs[at][0]) // count).start()
+        for at, array in whole_parts:
+            fetch(at, 0, array).wait()
+
+        def step(i, carry):
+            for at in split_in:
+                target = piece(held[at], inputs[at][2], i)
+                pltpu.make_async_copy(target, target, in_sem.at[at, i]).wait()
+            views = [
+                ref if split is None else piece(ref, split if isinstance(split, int) else split[0], i)
+                for ref, split in zip((*held, *made), [x[2] for x in (*inputs, *outputs)])
+            ]
+            body(i, *views, *own)
+            for at in split_out:
+                send(at, i).start()
+            return carry
+
+        lax.fori_loop(0, count, step, 0)
+        for at in whole_out:
+            send(at, 0).start()
+        for at in whole_out:
+            send(at, 0).wait()
+        for i in range(count):
+            for at in split_out:
+                send(at, i).wait()
+
+    def held_shape(arrays, picks, split):
+        shape = [picks[d][1] if d in picks else arrays[0].shape[d] for d in range(arrays[0].ndim)]
+        if len(arrays) > 1:
+            shape[split if isinstance(split, int) else split[0]] *= len(arrays)
+        return tuple(shape)
+
+    return pl.pallas_call(
+        kernel,
+        in_specs=[pl.BlockSpec(memory_space=pl.ANY)] * firsts[-1],
+        out_specs=[pl.BlockSpec(memory_space=pl.ANY)] * len(outputs),
+        out_shape=[jax.ShapeDtypeStruct(shape, dtype) for shape, dtype, _ in outputs],
+        scratch_shapes=[pltpu.VMEM(held_shape(*each), each[0][0].dtype) for each in inputs]
+        + [pltpu.VMEM(shape, dtype) for shape, dtype, _ in outputs]
+        + [pltpu.SemaphoreType.DMA((len(inputs), count)), pltpu.SemaphoreType.DMA((len(outputs), count))]
+        + list(scratch_shapes),
+        compiler_params=params(VMEM_LIMIT),
+        cost_estimate=pl.CostEstimate(flops=0, bytes_accessed=8000, transcendentals=0),
+        name=name,
+    )(*(array for arrays, _, _ in inputs for array in arrays))
+
+
 def local(residual, streams, short_filter, long_filter, skip, gain, cotangent):
     tokens_here, channels = streams.shape[1:]
     groups = long_filter.shape[0]
     rows_here, width_all = residual.shape
     owners = lax.axis_size("tensor")
     assert long_filter.shape[1] == TAPS and channels == groups * WIDTH and tokens_here % (2 * TAPS) == 0
-    chunks = 1
-    part = channels // chunks
-    step = min(part, 512)
-    steps, all_steps = part // step, channels // step
-    cols = step // LANES
+    columns = channels // LANES
+    halves = 1
+    part = channels // halves
+    count = max(halves, channels // STEP)
     skip_row = skip[None, :]
     gain_row = gain[None, :]
     gain_here = lax.dynamic_slice_in_dim(gain, lax.axis_index("tensor") * channels, channels)[None, :]
 
     spec = pl.BlockSpec
-
-    def wide(rows, offset=0):
-        return spec((rows, step), lambda i: (0, i + offset))
-
-    def deep(first, rows, offset=0):
-        return spec((first, rows, step), lambda i: (0, 0, i + offset))
-
-    def bands_of(offset=0):
-        return spec((step // WIDTH, BLOCK, SPAN), lambda i: (i + offset, 0, 0))
-
-    def arrived(offset=0):
-        return spec((owners, 2, rows_here, step), lambda i: (0, 0, 0, i + offset))
 
     def padded(count=None):
         shape = (tokens_here + 8, LANES)
@@ -456,100 +548,110 @@
         out_shape=[band_shape] * 2,
     )(long_filter)
 
-    output, mixed, gated = kernel(
+    output, mixed, gated = streamed(
         forward_kernel,
         "forward",
-        5,
-        grid=(all_steps,),
-        in_specs=[deep(3, tokens_here), wide(TAPS + 8), deep(3, 3), wide(1), bands_of()],
-        out_specs=[wide(tokens_here)] * 3,
-        out_shape=[jax.ShapeDtypeStruct((tokens_here, channels), t) for t in (bf16, f32, bf16)],
-        scratch_shapes=[padded(3)],
-    )(streams, halo, short_filter, skip_row, ahead_bands)
-    stats = kernel(
-        stats_kernel,
+        count,
+        [(streams, {}, 2), (halo, {}, 1), (short_filter, {}, (2,)), (skip_row, {}, (1,)), (ahead_bands, {}, 0)],
+        [((tokens_here, channels), t, 1) for t in (bf16, f32, bf16)],
+        [padded(3)],
+    )
+
+    (stats,) = streamed(
+        functools.partial(stats_kernel, count),
         "stats",
-        2,
-        grid=(all_steps,),
-        in_specs=[arrived(), wide(tokens_here), wide(1)],
-        out_specs=spec((2, tokens_here), lambda i: (0, 0)),
-        out_shape=jax.ShapeDtypeStruct((2, tokens_here), f32),
-        scratch_shapes=[pltpu.VMEM((tokens_here, LANES), f32)] * 2,
-    )(received, output, gain_here)
+        count,
+        [(received, {}, 3), (output, {}, 1), (gain_here, {}, (1,))],
+        [((2, tokens_here), f32, None)],
+        [pltpu.VMEM((tokens_here, LANES), f32)] * 2,
+    )
     stats = lax.psum(stats, "tensor")
-    stats, leaving = lax.optimization_barrier((stats, output))
+    heads = []
+    for k in range(halves):
+        here = (k * part, part)
+        heads.append(
+            streamed(
+                functools.partial(head_kernel, width_all),
+                "head",
+                count // halves,
+                [
+                    (streams, {0: (0, 1), 2: here}, 2),
+                    (streams, {0: (1, 1), 1: (0, 16), 2: here}, 2),
+                    (streams, {0: (2, 1), 1: (0, 16), 2: here}, 2),
+                    (halo, {1: here}, 1),
+                    (short_filter, {2: here}, (2,)),
+                    (skip_row, {1: here}, (1,)),
+                    (long_filter, {0: (k * groups // halves, groups // halves)}, 0),
+                    (stats, {}, None),
+                    (received, {3: here}, 3),
+                    (output, {1: here}, 1),
+                    (gain_here, {1: here}, (1,)),
+                    (mixed, {0: (0, 16), 1: here}, 1),
+                ],
+                [
+                    ((tokens_here, part), bf16, 1),
+                    ((tokens_here, part), bf16, 1),
+                    ((1, part), f32, (1,)),
+                    ((TAPS + 16, part), bf16, 1),
+                ],
+                [padded()] + [pltpu.VMEM((tokens_here, LANES), f32)] * 2,
+            )
+        )
+    grads, inner, shares, first = (tuple(column) for column in zip(*heads))
+    after = [from_behind(piece, "dp", -1) for piece in first]
+    leaving, inner = lax.optimization_barrier((output, inner))
     rows_received = lax.all_to_all(
         leaving.reshape(owners, rows_here, channels), "tensor", split_axis=0, concat_axis=0, tiled=True
     )
 
-    after, filled = [], []
-    for k in range(chunks):
-        grads, inner, shares, first = kernel(
-            functools.partial(head_kernel, width_all, bool(filled)),
-            "head",
-            2,
-            grid=(steps,),
-            in_specs=[
-                deep(1, tokens_here, k * steps),
-                spec((1, 16, step), lambda i, k=k: (1, 0, i + k * steps)),
-                spec((1, 16, step), lambda i, k=k: (2, 0, i + k * steps)),
-                wide(TAPS + 8, k * steps),
-                deep(3, 3, k * steps),
-                wide(1, k * steps),
-                spec((step // WIDTH, TAPS), lambda i, k=k: (i + k * steps, 0)),
-                spec((2, tokens_here), lambda i: (0, 0)),
-                arrived(k * steps),
-                wide(tokens_here, k * steps),
-                wide(1, k * steps),
-                spec((16, step), lambda i, k=k: (0, i + k * steps)),
-            ]
-            + [spec(memory_space=pl.ANY)] * len(filled),
-            out_specs=[
-                wide(tokens_here, k * steps),
-                wide(tokens_here, k * steps),
-                wide(1, k * steps),
-                wide(TAPS + 16),
-            ],
-            out_shape=[
-                jax.ShapeDtypeStruct((tokens_here, channels), bf16),
-                jax.ShapeDtypeStruct((tokens_here, channels), bf16),
-                jax.ShapeDtypeStruct((1, channels), f32),
-                jax.ShapeDtypeStruct((TAPS + 16, part), bf16),
-            ],
-            scratch_shapes=[padded()] + [pltpu.VMEM((tokens_here, LANES), f32)] * 2,
-            input_output_aliases={12 + n: n for n in range(len(filled))},
-        )(
-            *(streams, streams, streams, halo, short_filter, skip_row, long_filter, stats, received, output),
-            *(gain_here, mixed, *filled),
-        )
-        filled = [grads, inner, shares]
-        after.append(from_behind(first, "dp", -1))
-
-    early = kernel(
+    (early,) = streamed(
         sums_kernel,
         "sums",
-        8,
-        grid=(all_steps,),
-        in_specs=[
-            deep(1, tokens_here),
-            wide(TAPS + 8),
-            wide(tokens_here),
-            wide(tokens_here),
-            wide(tokens_here),
-            wide(tokens_here),
-            wide(1),
+        count,
+        [
+            (streams, {0: (0, 1)}, 2),
+            (halo, {}, 1),
+            (gated, {}, 1),
+            (inner, {}, 1),
+            (grads, {}, 1),
+            (mixed, {}, 1),
+            (shares, {}, (1,)),
         ],
-        out_specs=spec((cols * 16, LANES), lambda i: (i, 0)),
-        out_shape=jax.ShapeDtypeStruct((channels // LANES * 16, LANES), f32),
-        scratch_shapes=[padded()],
-    )(streams, halo, gated, inner, grads, mixed, shares)
-
+        [((columns * 16, LANES), f32, 0)],
+        [padded()],
+    )
+
+    stream_grad, late = streamed(
+        backward_kernel,
+        "backward",
+        count,
+        [
+            (streams, {}, 2),
+            (halo, {}, 1),
+            (short_filter, {}, (2,)),
+            (skip_row, {}, (1,)),
+            (behind_bands, {}, 0),
+            (grads, {}, 1),
+            (mixed, {}, 1),
+            (inner, {}, 1),
+            (tuple(after), {}, 1),
+        ],
+        [(streams.shape, bf16, 2), ((columns * 8, LANES), f32, 0)],
+        [padded(3), padded(3)],
+    )
+    bits = (lax.axis_size("dp") - 1).bit_length()
+    stages = [[1 << n] if n + 1 == bits else [1 << n, 2 << n, 3 << n] for n in range(0, bits, 2)]
+    total = jnp.concatenate([early, late], axis=0)
+    for stage in stages[:-1]:
+        mine, others = sent_to(total, "dp", stage)
+        total = added(mine, others)
     block = min(rows_here, 16)
     by_rows = spec((block, width_all), lambda i: (i, 0))
     normed, grad_residual = kernel(
         norm_kernel,
         "norm",
         4,
+        NORM_LIMIT,
         grid=(rows_here // block,),
         in_specs=[
             spec((owners, block, channels), lambda i: (0, i, 0)),
@@ -562,49 +664,9 @@
         scratch_shapes=[pltpu.VMEM((block, width_all), f32)],
     )(rows_received, residual, cotangent, gain_row)
 
-    reaches = [1 << n for n in range((lax.axis_size("dp") - 1).bit_length())]
-    waiting = list(reaches)
-    early_other, filled = None, []
-    for k in range(chunks):
-        if waiting:
-            early = early if early_other is None else early + early_other.astype(f32)
-            early, after[k] = lax.optimization_barrier((early, after[k]))
-            early, early_other = exchange(early, None, "dp", waiting.pop(0))
-        stream_grad, late = kernel(
-            functools.partial(backward_kernel, bool(filled)),
-            "backward",
-            5,
-            grid=(steps,),
-            in_specs=[
-                deep(3, tokens_here, k * steps),
-                wide(TAPS + 8, k * steps),
-                deep(3, 3, k * steps),
-                wide(1, k * steps),
-                bands_of(k * steps),
-                wide(tokens_here, k * steps),
-                wide(tokens_here, k * steps),
-                wide(tokens_here, k * steps),
-                wide(TAPS + 16),
-            ]
-            + [spec(memory_space=pl.ANY)] * len(filled),
-            out_specs=[
-                deep(3, tokens_here, k * steps),
-                spec((cols * 8, LANES), lambda i, k=k: (i + k * steps, 0)),
-            ],
-            out_shape=[
-                jax.ShapeDtypeStruct(streams.shape, bf16),
-                jax.ShapeDtypeStruct((channels // LANES * 8, LANES), f32),
-            ],
-            scratch_shapes=[padded(3), padded(3)],
-            input_output_aliases={9 + n: n for n in range(len(filled))},
-        )(streams, halo, short_filter, skip_row, behind_bands, grads, mixed, inner, after[k], *filled)
-        filled = [stream_grad, late]
-    for reach in waiting:
-        early, early_other = exchange(early, early_other, "dp", reach)
-    late_other = None
-    for reach in reaches:
-        late, late_other = exchange(late, late_other, "dp", reach)
-    late, normed, grad_residual = lax.optimization_barrier((late, normed, grad_residual))
+    mine, others = sent_to(total, "dp", stages[-1])
+    mine, normed, grad_residual = lax.optimization_barrier((mine, normed, grad_residual))
+    mine, other = (mine, others[0]) if len(others) == 1 else (added(mine, others[:1]), added(others[1], others[2:]))
     long_grad, short_grad, skip_grad, gain_grad = kernel(
         close_kernel,
         "close",
@@ -616,7 +678,7 @@
             jax.ShapeDtypeStruct((1, channels), f32),
             jax.ShapeDtypeStruct((1, channels), f32),
         ],
-    )(early, early_other, late, late_other)
+    )(mine, other)
     skip_grad, gain_grad = skip_grad.reshape(channels), gain_grad.reshape(channels)
     return (normed, grad_residual, stream_grad, long_grad, short_grad, skip_grad, gain_grad)
 

time: 106 us -> 102 us (0.962)
  starting transfers between devices: 24.3 us -> 21.4 us
  Pallas kernels: 53 us -> 50.4 us
  other arithmetic: 3.65 us -> 1.76 us
  waiting for transfers between devices: 13.5 us -> 15.3 us
  local copies, waits for them, and re-layouts: 3.17 us -> 4.73 us
    ppermute x6 -> x4, starting transfers between devices: 9.93 us -> 7 us  [sent_to(): lax.ppermute(half, axis, [(i, i ^ d) for i in range(count)])]
    pallas_call x6, Pallas kernels: 40.9 us -> 38.3 us  [the longest x5 35.6 us: streamed(): pl.pallas_call(kernel, in_specs=[pl.BlockSpec(memory_space=pl.ANY)] * fir...]
    unnamed x10 -> x14, local copies, waits for them, and re-layouts: 1.88 us -> 4.13 us
    convert_element_type x6 -> x2, other arithmetic: 3.65 us -> 1.76 us  [sent_to(): half = value.astype(bf16)]
    ppermute x6 -> x4, waiting for transfers between devices: 3.47 us -> 4.43 us  [sent_to(): lax.ppermute(half, axis, [(i, i ^ d) for i in range(count)])]
  transfers between devices with their start and end apart: 10 -> 8, of which waited for: 5 -> 6; matrix products, arithmetic and copies ran while one was open for 5% -> 2% of each run, Pallas kernels for 36% -> 35%
where the time goes in v4:
time: 102 us; the launch traced here: 101 us
  Pallas kernels  50.4 us (49%)
  starting transfers between devices  21.4 us (21%)
  waiting for transfers between devices  15.3 us (15%)
  blocking collectives  6.52 us (6%)
  local copies, waits for them, and re-layouts  4.73 us (5%)
  other arithmetic  1.76 us (2%)
    pallas_call x5, Pallas kernels, streamed(): pl.pallas_call(kernel, in_specs=[pl.BlockSpec(memory_space=pl.ANY)] * fir...  35.6 us
    ppermute x2, waiting for transfers between devices, from_behind(): lax.ppermute(value, axis, [(source, source + steps) for source in range(f...  9.61 us
    ppermute x4, starting transfers between devices, sent_to(): lax.ppermute(half, axis, [(i, i ^ d) for i in range(count)])  7 us
    pallas_call x1, Pallas kernels, local(): kernel(bands_kernel, 'bands', 5, grid=(groups // each,), in_specs=[spec((...  6.71 us
    psum x1, blocking collectives, local(): stats = lax.psum(stats, 'tensor')  6.52 us
    ppermute x2, starting transfers between devices, from_behind(): lax.ppermute(value, axis, [(source, source + steps) for source in range(f...  6.2 us
    pallas_call x1, Pallas kernels, local(): kernel(open_kernel, 'open', 3, in_specs=[spec(memory_space=pl.ANY)] * 3 +...  4.66 us
    all_to_all x1, starting transfers between devices, local(): lax.all_to_all(packed, 'tensor', split_axis=0, concat_axis=0, tiled=True)  4.65 us
  transfers between devices with their start and end apart: 8, of which 6 were waited for; matrix products, arithmetic and copies ran while one was open for 2% of the time, Pallas kernels for 35%

profile of v4, /device:TPU:0, one launch (start us, length us, event | category | flops | bytes accessed | tf_op | source)
XLA Modules:
  0.0 100.8 jit_solution(14972317357875113465)
XLA Ops:
  0.6 4.7 %open.1 = (bf16[4,2,64,2048]{3,2,1,0:T(8,128)(2,1)}, bf16[136,2048]{1,0:T(8,128)(2,1)}) custom-call(bf16[64,8192]{1,0:T(8,128)(2,1)} %cot_ref.3, bf16[64,8192]{1,0:T(8,128)(2,1)} %residual_ref.3, bf16[3,256,2048]{2,1,0:T(8,128)(2,1)} %refs_0_.7, f32[3,3,2048]{2,1,0:T(4,128)} %refs_2_.5), custom_call_target="tpu_custom_call" | custom-call | bytes 3000 | tf_op jit(solution)/shard_map/open/pallas_call | solution.py:516
  5.3 0.0 copy-start.6
  5.3 0.0 copy-start.2
  5.3 4.7 %all-to-all-start = ((bf16[4,2,64,2048]{3,2,1,0:T(8,128)(2,1)}), bf16[4,2,64,2048]{3,2,1,0:T(8,128)(2,1)}, u32[]{:S(2)}, u32[]{:S(2)}) async-start(bf16[4,2,64,2048]{3,2,1,0:T(8,128)(2,1)} %get-tuple-element.35), calls=%async_computation | async-start | bytes 4194304 | tf_op jit(solution)/shard_map/all_to_all | solution.py:537
  10.0 0.0 copy-done.6
  10.0 4.9 %collective-permute-start = (bf16[136,2048]{1,0:T(8,128)(2,1)S(1)}, bf16[136,2048]{1,0:T(8,128)(2,1)S(1)}, u32[]{:S(2)}, u32[]{:S(2)}) collective-permute-start(bf16[136,2048]{1,0:T(8,128)(2,1)S(1)} %copy-done.6), channel_id=1, source_target_pairs={{0,4},{4,8},{8,12},{12,16},{16,20},{20,24},{24,28},{1,5},{5,9},{9,... | collective-permute-start | bytes 1671176 | tf_op jit(solution)/shard_map/ppermute | solution.py:361
  14.9 6.7 %bands.1 = (bf16[128,64,256]{2,1,0:T(8,128)(2,1)}, bf16[128,64,256]{2,1,0:T(8,128)(2,1)}) custom-call(f32[128,128]{1,0:T(8,128)} %refs_6_.1), custom_call_target="tpu_custom_call" | custom-call | bytes 5000 | tf_op jit(solution)/shard_map/bands/pallas_call | solution.py:541
  21.6 0.0 copy-done.2
  21.6 0.6 dynamic_slice.3
  22.2 5.1 %collective-permute-done.refs_1_.refs_3_ = bf16[136,2048]{1,0:T(8,128)(2,1)S(1)} collective-permute-done((bf16[136,2048]{1,0:T(8,128)(2,1)S(1)}, bf16[136,2048]{1,0:T(8,128)(2,1)S(1)}, u32[]{:S(2)}, u32[]{:S(2)}) %collective-permute-start) | collective-permute-done | bytes 557088 | tf_op jit(solution)/shard_map/ppermute | solution.py:361
  27.3 0.0 copy-start.3
  27.3 0.8 copy-done.3
  28.2 6.9 %forward.1 = (bf16[256,2048]{1,0:T(8,128)(2,1)}, f32[256,2048]{1,0:T(8,128)}, bf16[256,2048]{1,0:T(8,128)(2,1)}) custom-call(bf16[3,256,2048]{2,1,0:T(8,128)(2,1)} %refs_0_.7, bf16[136,2048]{1,0:T(8,128)(2,1)} %copy-done.3, f32[3,3,2048]{2,1,0:T(4,128)} %refs_2_.5, f32[1,2048]{1,0:T(1,128)} %bitcast.10, bf16[128,64,256]{2,1,0:T(8,128)(2,1)} %get-tuple-element.32.refs_4_), custom_call_target="tpu_custom_call" | custom-call | bytes 8000 | tf_op jit(solution)/shard_map/forward/pallas_call | solution.py:472
  35.1 1.2 %all-to-all-done.refs_0_.refs_8_ = bf16[4,2,64,2048]{3,2,1,0:T(8,128)(2,1)} async-done(((bf16[4,2,64,2048]{3,2,1,0:T(8,128)(2,1)}), bf16[4,2,64,2048]{3,2,1,0:T(8,128)(2,1)}, u32[]{:S(2)}, u32[]{:S(2)}) %all-to-all-start) | async-done | bytes 2097184 | tf_op jit(solution)/shard_map/all_to_all | solution.py:537
  36.3 2.9 %stats.1 = f32[2,256]{1,0:T(2,128)} custom-call(bf16[4,2,64,2048]{3,2,1,0:T(8,128)(2,1)} %all-to-all-done.refs_0_.refs_8_, bf16[256,2048]{1,0:T(8,128)(2,1)} %get-tuple-element.44.refs_1_.refs_9_, f32[1,2048]{1,0:T(1,128)} %bitcast.8), custom_call_target="tpu_custom_call" | custom-call | bytes 8000 | tf_op jit(solution)/shard_map/stats/pallas_call | solution.py:472
  39.2 6.5 %psum.7.refs_7_ = f32[2,256]{1,0:T(2,128)} all-reduce(f32[2,256]{1,0:T(2,128)} %stats.1), channel_id=1, replica_groups=mesh['dp'=8,'tensor'=4] {'tensor'}, use_global_device_ids=true, to_apply=%region_0.0 | all-reduce | flops 512 | bytes 4096 | tf_op jit(solution)/shard_map/psum | solution.py:568
  45.7 6.6 %head.1 = (bf16[256,2048]{1,0:T(8,128)(2,1)}, bf16[256,2048]{1,0:T(8,128)(2,1)}, f32[1,2048]{1,0:T(1,128)}, bf16[144,2048]{1,0:T(8,128)(2,1)}) custom-call(bf16[3,256,2048]{2,1,0:T(8,128)(2,1)} %refs_0_.7, bf16[3,256,2048]{2,1,0:T(8,128)(2,1)} %refs_0_.7, bf16[3,256,2048]{2,1,0:T(8,128)(2,1)} %refs_0_.7, bf16[136,2048]{1,0:T(8,128)(2,1)} %copy-done.3, ...), custom_call_target="tpu_custom_call" | custom-call | bytes 8000 | tf_op jit(solution)/shard_map/head/pallas_call | solution.py:472
  52.3 1.3 %collective-permute-start.1 = (bf16[144,2048]{1,0:T(8,128)(2,1)}, bf16[144,2048]{1,0:T(8,128)(2,1)S(1)}, u32[]{:S(2)}, u32[]{:S(2)}) collective-permute-start(bf16[144,2048]{1,0:T(8,128)(2,1)} %get-tuple-element.42), channel_id=1, source_target_pairs={{4,0},{8,4},{12,8},{16,12},{20,16},{24,20},{28,24},{5,1},{9,5},{13... | collective-permute-start | bytes 1769480 | tf_op jit(solution)/shard_map/ppermute | solution.py:361
  53.6 3.5 %all-to-all-start.1 = ((bf16[4,64,2048]{2,1,0:T(8,128)(2,1)}), bf16[4,64,2048]{2,1,0:T(8,128)(2,1)S(1)}, u32[]{:S(2)}, u32[]{:S(2)}) async-start(bf16[4,64,2048]{2,1,0:T(8,128)(2,1)} %bitcast.7), calls=%async_computation.1 | async-start | bytes 2097152 | tf_op jit(solution)/shard_map/all_to_all | solution.py:603
  57.2 8.4 %sums.1 = f32[256,128]{1,0:T(8,128)} custom-call(bf16[3,256,2048]{2,1,0:T(8,128)(2,1)} %refs_0_.7, bf16[136,2048]{1,0:T(8,128)(2,1)} %copy-done.3, bf16[256,2048]{1,0:T(8,128)(2,1)} %get-tuple-element.33.refs_2_, bf16[256,2048]{1,0:T(8,128)(2,1)} %get-tuple-element.38.refs_3_.refs_7_, bf16[256,2048]{1,0:T(8,128)(2,1)} %get-tuple-element.39.refs_4_.refs_5_, ...), custom_call_target="tpu_custom_call" | custom-call | bytes 8000 | tf_op jit(solution)/shard_map/sums/pallas_call | solution.py:472
  65.5 4.5 %collective-permute-done.1.refs_8_ = bf16[144,2048]{1,0:T(8,128)(2,1)S(1)} collective-permute-done((bf16[144,2048]{1,0:T(8,128)(2,1)}, bf16[144,2048]{1,0:T(8,128)(2,1)S(1)}, u32[]{:S(2)}, u32[]{:S(2)}) %collective-permute-start.1) | collective-permute-done | bytes 589856 | tf_op jit(solution)/shard_map/ppermute | solution.py:361
  70.0 0.0 copy-start.5
  70.0 0.8 copy-done.5
  70.8 0.0 copy-start.4
  70.8 10.9 %backward.1 = (bf16[3,256,2048]{2,1,0:T(8,128)(2,1)}, f32[128,128]{1,0:T(8,128)}) custom-call(bf16[3,256,2048]{2,1,0:T(8,128)(2,1)} %refs_0_.7, bf16[136,2048]{1,0:T(8,128)(2,1)} %copy-done.3, f32[3,3,2048]{2,1,0:T(4,128)} %refs_2_.5, f32[1,2048]{1,0:T(1,128)} %bitcast.12, bf16[128,64,256]{2,1,0:T(8,128)(2,1)} %get-tuple-element.41.refs_4_, ...), custom_call_target="tpu_custom_call" | custom-call | bytes 8000 | tf_op jit(solution)/shard_map/backward/pallas_call | solution.py:472
  81.7 0.0 copy-done.4
  81.7 0.9 fusion
  82.6 3.7 %collective-permute-start.4 = (bf16[384,128]{1,0:T(8,128)(2,1)S(1)}, bf16[384,128]{1,0:T(8,128)(2,1)S(1)}, u32[]{:S(2)}, u32[]{:S(2)}) collective-permute-start(bf16[384,128]{1,0:T(8,128)(2,1)S(1)} %fusion), channel_id=1, source_target_pairs={{0,12},{4,8},{8,4},{12,0},{16,28},{20,24},{24,20},{28,16},{1,13},{... | collective-permute-start | bytes 294920 | tf_op jit(solution)/shard_map/ppermute | solution.py:368
  86.3 0.5 collective-permute-start.3
  86.8 0.2 collective-permute-start.2
  87.0 2.2 %collective-permute-done.4 = bf16[384,128]{1,0:T(8,128)(2,1)S(1)} collective-permute-done((bf16[384,128]{1,0:T(8,128)(2,1)S(1)}, bf16[384,128]{1,0:T(8,128)(2,1)S(1)}, u32[]{:S(2)}, u32[]{:S(2)}) %collective-permute-start.4) | collective-permute-done | bytes 98336 | tf_op jit(solution)/shard_map/ppermute | solution.py:368
  89.2 1.8 %collective-permute-done.3 = bf16[384,128]{1,0:T(8,128)(2,1)S(1)} collective-permute-done((bf16[384,128]{1,0:T(8,128)(2,1)S(1)}, bf16[384,128]{1,0:T(8,128)(2,1)S(1)}, u32[]{:S(2)}, u32[]{:S(2)}) %collective-permute-start.3) | collective-permute-done | bytes 98336 | tf_op jit(solution)/shard_map/ppermute | solution.py:368
  90.9 0.5 collective-permute-done.2
  91.4 0.9 fusion.1
  92.3 2.6 %collective-permute-start.5 = (bf16[384,128]{1,0:T(8,128)(2,1)S(1)}, bf16[384,128]{1,0:T(8,128)(2,1)S(1)}, u32[]{:S(2)}, u32[]{:S(2)}) collective-permute-start(bf16[384,128]{1,0:T(8,128)(2,1)S(1)} %get-tuple-element.55), channel_id=1, source_target_pairs={{0,16},{4,20},{8,24},{12,28},{16,0},{20,4},{24,8},{28,12},{1,17},{... | collective-permute-start | bytes 294920 | tf_op jit(solution)/shard_map/ppermute | solution.py:368
  94.9 0.0 all-to-all-done.1.received_ref
  94.9 0.0 copy-start
  94.9 1.2 %copy-done = bf16[64,8192]{1,0:T(8,128)(2,1)S(1)} copy-done((bf16[64,8192]{1,0:T(8,128)(2,1)S(1)}, bf16[64,8192]{1,0:T(8,128)(2,1)}, u32[]{:S(2)}) %copy-start) | copy-done | bytes 1048600
  96.2 0.0 copy-start.1
  96.2 1.2 %copy-done.1 = bf16[64,8192]{1,0:T(8,128)(2,1)S(1)} copy-done((bf16[64,8192]{1,0:T(8,128)(2,1)S(1)}, bf16[64,8192]{1,0:T(8,128)(2,1)}, u32[]{:S(2)}) %copy-start.1) | copy-done | bytes 1048600
  97.4 2.7 %norm.1 = (bf16[64,8192]{1,0:T(8,128)(2,1)}, bf16[64,8192]{1,0:T(8,128)(2,1)}) custom-call(bf16[4,64,2048]{2,1,0:T(8,128)(2,1)S(1)} %all-to-all-done.1.received_ref, bf16[64,8192]{1,0:T(8,128)(2,1)S(1)} %copy-done.1, bf16[64,8192]{1,0:T(8,128)(2,1)S(1)} %copy-done, f32[1,8192]{1,0:T(1,128)S(1)} %bitcast.6), custom_call_target="tpu_custom_call" | custom-call | bytes 4000 | tf_op jit(solution)/shard_map/norm/pallas_call | solution.py:650
  100.1 0.0 collective-permute-done.5.other_ref
  100.1 0.7 close.1
Async XLA Ops:
  5.3 4.7 %copy-start.6 = (bf16[136,2048]{1,0:T(8,128)(2,1)S(1)}, bf16[136,2048]{1,0:T(8,128)(2,1)}, u32[]{:S(2)}) copy-start(bf16[136,2048]{1,0:T(8,128)(2,1)} %get-tuple-element.31) | copy-start | bytes 1671172
  5.3 16.3 %copy-start.2 = (f32[8192]{0:T(1024)S(1)}, f32[8192]{0:T(1024)}, u32[]{:S(2)}) copy-start(f32[8192]{0:T(1024)} %param.12) | copy-start | bytes 98308
  5.3 31.0 %all-to-all-start = ((bf16[4,2,64,2048]{3,2,1,0:T(8,128)(2,1)}), bf16[4,2,64,2048]{3,2,1,0:T(8,128)(2,1)}, u32[]{:S(2)}, u32[]{:S(2)}) async-start(bf16[4,2,64,2048]{3,2,1,0:T(8,128)(2,1)} %get-tuple-element.35), calls=%async_computation | async-start | bytes 4194304 | tf_op jit(solution)/shard_map/all_to_all | solution.py:537
  10.0 17.4 %collective-permute-start = (bf16[136,2048]{1,0:T(8,128)(2,1)S(1)}, bf16[136,2048]{1,0:T(8,128)(2,1)S(1)}, u32[]{:S(2)}, u32[]{:S(2)}) collective-permute-start(bf16[136,2048]{1,0:T(8,128)(2,1)S(1)} %copy-done.6), channel_id=1, source_target_pairs={{0,4},{4,8},{8,12},{12,16},{16,20},{20,24},{24,28},{1,5},{5,9},{9,... | collective-permute-start | bytes 1671176 | tf_op jit(solution)/shard_map/ppermute | solution.py:361
  27.3 0.9 copy-start.3
  52.3 17.7 %collective-permute-start.1 = (bf16[144,2048]{1,0:T(8,128)(2,1)}, bf16[144,2048]{1,0:T(8,128)(2,1)S(1)}, u32[]{:S(2)}, u32[]{:S(2)}) collective-permute-start(bf16[144,2048]{1,0:T(8,128)(2,1)} %get-tuple-element.42), channel_id=1, source_target_pairs={{4,0},{8,4},{12,8},{16,12},{20,16},{24,20},{28,24},{5,1},{9,5},{13... | collective-permute-start | bytes 1769480 | tf_op jit(solution)/shard_map/ppermute | solution.py:361
  53.6 41.3 %all-to-all-start.1 = ((bf16[4,64,2048]{2,1,0:T(8,128)(2,1)}), bf16[4,64,2048]{2,1,0:T(8,128)(2,1)S(1)}, u32[]{:S(2)}, u32[]{:S(2)}) async-start(bf16[4,64,2048]{2,1,0:T(8,128)(2,1)} %bitcast.7), calls=%async_computation.1 | async-start | bytes 2097152 | tf_op jit(solution)/shard_map/all_to_all | solution.py:603
  70.0 0.8 copy-start.5
  70.8 10.9 %copy-start.4 = (f32[256,128]{1,0:T(8,128)S(1)}, f32[256,128]{1,0:T(8,128)}, u32[]{:S(2)}) copy-start(f32[256,128]{1,0:T(8,128)} %sums.1) | copy-start | bytes 393220
  82.6 6.6 %collective-permute-start.4 = (bf16[384,128]{1,0:T(8,128)(2,1)S(1)}, bf16[384,128]{1,0:T(8,128)(2,1)S(1)}, u32[]{:S(2)}, u32[]{:S(2)}) collective-permute-start(bf16[384,128]{1,0:T(8,128)(2,1)S(1)} %fusion), channel_id=1, source_target_pairs={{0,12},{4,8},{8,4},{12,0},{16,28},{20,24},{24,20},{28,16},{1,13},{... | collective-permute-start | bytes 294920 | tf_op jit(solution)/shard_map/ppermute | solution.py:368
  86.3 4.6 %collective-permute-start.3 = (bf16[384,128]{1,0:T(8,128)(2,1)S(1)}, bf16[384,128]{1,0:T(8,128)(2,1)S(1)}, u32[]{:S(2)}, u32[]{:S(2)}) collective-permute-start(bf16[384,128]{1,0:T(8,128)(2,1)S(1)} %fusion), channel_id=1, source_target_pairs={{0,8},{4,12},{8,0},{12,4},{16,24},{20,28},{24,16},{28,20},{1,9},{5... | collective-permute-start | bytes 294920 | tf_op jit(solution)/shard_map/ppermute | solution.py:368
  86.8 4.6 %collective-permute-start.2 = (bf16[384,128]{1,0:T(8,128)(2,1)S(1)}, bf16[384,128]{1,0:T(8,128)(2,1)S(1)}, u32[]{:S(2)}, u32[]{:S(2)}) collective-permute-start(bf16[384,128]{1,0:T(8,128)(2,1)S(1)} %fusion), channel_id=1, source_target_pairs={{0,4},{4,0},{8,12},{12,8},{16,20},{20,16},{24,28},{28,24},{1,5},{5... | collective-permute-start | bytes 294920 | tf_op jit(solution)/shard_map/ppermute | solution.py:368
  92.3 7.8 %collective-permute-start.5 = (bf16[384,128]{1,0:T(8,128)(2,1)S(1)}, bf16[384,128]{1,0:T(8,128)(2,1)S(1)}, u32[]{:S(2)}, u32[]{:S(2)}) collective-permute-start(bf16[384,128]{1,0:T(8,128)(2,1)S(1)} %get-tuple-element.55), channel_id=1, source_target_pairs={{0,16},{4,20},{8,24},{12,28},{16,0},{20,4},{24,8},{28,12},{1,17},{... | collective-permute-start | bytes 294920 | tf_op jit(solution)/shard_map/ppermute | solution.py:368
  94.9 1.2 %copy-start = (bf16[64,8192]{1,0:T(8,128)(2,1)S(1)}, bf16[64,8192]{1,0:T(8,128)(2,1)}, u32[]{:S(2)}) copy-start(bf16[64,8192]{1,0:T(8,128)(2,1)} %cot_ref.3) | copy-start | bytes 3145732
  96.2 1.2 %copy-start.1 = (bf16[64,8192]{1,0:T(8,128)(2,1)S(1)}, bf16[64,8192]{1,0:T(8,128)(2,1)}, u32[]{:S(2)}) copy-start(bf16[64,8192]{1,0:T(8,128)(2,1)} %residual_ref.3) | copy-start | bytes 3145732

commit v5 on v4

--- a/solution.py
+++ b/solution.py
@@ -14,16 +14,16 @@
 PER = LANES // WIDTH
 BLOCK = 64
 SPAN = 256
-VMEM_LIMIT = 62
+VMEM_LIMIT = 63.5
 SMALL_LIMIT = 8
-NORM_LIMIT = 24
+NORM_LIMIT = 63.5
 STEP = 512
 f32 = jnp.float32
 bf16 = jnp.bfloat16
 
 
 def params(limit):
-    return pltpu.CompilerParams(vmem_limit_bytes=limit * 2**20)
+    return pltpu.CompilerParams(vmem_limit_bytes=int(limit * 2**20))
 
 
 def dot(a, b):
@@ -83,13 +83,17 @@
 
 
 def open_kernel(
-    cot_ref, residual_ref, streams_ref, taps_ref, packed_ref, halo_ref, pieces, ends, rows, scratch, in_sem, out_sem, end_sem
+    cot_ref, residual_ref, streams_ref, taps_ref, packed_ref, halo_ref, pieces, ends, last, rows, scratch, in_sem, out_sem, end_sem
 ):
     owners, _, _, channels = packed_ref.shape
     length = streams_ref.shape[1]
     back = ends.shape[1]
-    ending = pltpu.make_async_copy(streams_ref.at[:, pl.ds(length - back, back), :], ends, end_sem.at[0])
-    ending.start()
+    ending = [
+        pltpu.make_async_copy(streams_ref.at[pl.ds(1, 2), pl.ds(length - back, back), :], ends, end_sem.at[0]),
+        pltpu.make_async_copy(streams_ref.at[0, pl.ds(length - 16, 16), :], last, end_sem.at[1]),
+    ]
+    for copy in ending:
+        copy.start()
     places = [(j, which) for j in range(owners) for which in range(2)]
     arriving = [
         pltpu.make_async_copy(
@@ -102,18 +106,19 @@
     ]
     for copy in arriving:
         copy.start()
-    ending.wait()
+    for copy in ending:
+        copy.wait()
     for col in range(channels // LANES):
         lanes = slice(col * LANES, (col + 1) * LANES)
         features = []
         for s in (1, 2):
-            scratch[s, 0:back, :] = ends[s, :, lanes].astype(f32)
+            scratch[s, 0:back, :] = ends[s - 1, :, lanes].astype(f32)
             taps = taps_ref[s, :, lanes]
             now, one, two = (scratch[s, back - TAPS - n : back - n, :] for n in range(3))
             features.append(taps[0:1] * now + taps[1:2] * one + taps[2:3] * two)
         rows[:TAPS, lanes] = (features[0] * features[1]).astype(bf16)
         edges = scratch.at[0]
-        edges[0:2, :] = ends[0, back - 16 : back, lanes].astype(f32)[14:]
+        edges[0:2, :] = last[:, lanes].astype(f32)[14:]
         edges[2:4, :] = scratch[1, back - 2 : back, :]
         edges[4:6, :] = scratch[2, back - 2 : back, :]
         edges[6:8, :] = jnp.zeros((2, LANES), f32)
@@ -122,7 +127,7 @@
             for copy, onward in zip(arriving, leaving):
                 copy.wait()
                 onward.start()
-    ending = pltpu.make_async_copy(rows, halo_ref, end_sem.at[1])
+    ending = pltpu.make_async_copy(rows, halo_ref, end_sem.at[2])
     ending.start()
     for copy in leaving:
         copy.wait()
@@ -314,12 +319,15 @@
     mixed_ref,
     inner_ref,
     after_ref,
+    early_ref,
     stream_grad_ref,
-    late_ref,
+    bundle_ref,
     scratch,
     ahead,
 ):
     length = streams_ref.shape[1]
+    late = scratch.at[0]
+    late[0:8, :] = jnp.zeros((8, LANES), f32)
     for col in range(streams_ref.shape[2] // LANES):
         lanes = slice(col * LANES, (col + 1) * LANES)
         inner = inner_ref[:, lanes]
@@ -329,7 +337,7 @@
         grad_gated = jnp.concatenate(parts, axis=0) + skip_ref[:, lanes] * inner.astype(f32)
         shifts, features = {}, {}
         for s in (1, 2):
-            now = streams_ref[s, :, lanes].astype(f32)
+            now = streams_ref[s - 1, :, lanes].astype(f32)
             one, two = shifted(scratch.at[s], edge(halo_ref, s, lanes), now)
             taps = taps_ref[s, :, lanes]
             shifts[s] = (now, one, two)
@@ -350,9 +358,11 @@
             ).astype(bf16)
         for s in (1, 2):
             for j in range(3):
-                row = col * 8 + (s - 1) * 3 + j
-                late_ref[row : row + 1, :] = jnp.sum(grads[s] * shifts[s][j], axis=0, keepdims=True)
-        late_ref[col * 8 + 6 : col * 8 + 8, :] = jnp.zeros((2, LANES), f32)
+                row = (s - 1) * 3 + j
+                late[row : row + 1, :] = jnp.sum(grads[s] * shifts[s][j], axis=0, keepdims=True)
+        base = col * 24
+        bundle_ref[base : base + 16, :] = early_ref[col * 16 : (col + 1) * 16, :].astype(bf16)
+        bundle_ref[base + 16 : base + 24, :] = late[0:8, :].astype(bf16)
 
 
 def from_behind(value, axis, steps):
@@ -362,33 +372,34 @@
 
 
 def sent_to(value, axis, distances):
-    value = lax.reduce_precision(value, 8, 7)
+    half = value
+    if value.dtype != bf16:
+        value = lax.reduce_precision(value, 8, 7)
+        half = value.astype(bf16)
     count = lax.axis_size(axis)
-    half = value.astype(bf16)
     return value, [lax.ppermute(half, axis, [(i, i ^ d) for i in range(count)]) for d in distances]
 
 
 def added(value, others):
-    terms = [value] + [other.astype(f32) for other in others]
+    terms = [term.astype(f32) for term in (value, *others)]
     while len(terms) > 1:
         terms = [terms[i] + terms[i + 1] for i in range(0, len(terms), 2)]
     return terms[0]
 
 
 def close_kernel(mine_ref, other_ref, long_ref, short_ref, skip_ref, gain_ref):
-    total = mine_ref[...] + other_ref[...].astype(f32)
-    early, late = total[: skip_ref.shape[1] // LANES * 16], total[skip_ref.shape[1] // LANES * 16 :]
+    total = mine_ref[...].astype(f32) + other_ref[...].astype(f32)
     for col in range(skip_ref.shape[1] // LANES):
         lanes = slice(col * LANES, (col + 1) * LANES)
-        at = col * 16
-        long_ref[col * PER : (col + 1) * PER, :] = early[at : at + PER]
-        skip_ref[:, lanes] = early[at + 8 : at + 9]
-        gain_ref[:, lanes] = early[at + 9 : at + 10]
+        at = col * 24
+        long_ref[col * PER : (col + 1) * PER, :] = total[at : at + PER]
+        skip_ref[:, lanes] = total[at + 8 : at + 9]
+        gain_ref[:, lanes] = total[at + 9 : at + 10]
         for j in range(3):
-            short_ref[0, j : j + 1, lanes] = early[at + 10 + j : at + 11 + j]
+            short_ref[0, j : j + 1, lanes] = total[at + 10 + j : at + 11 + j]
             for s in (1, 2):
-                row = col * 8 + (s - 1) * 3 + j
-                short_ref[s, j : j + 1, lanes] = late[row : row + 1]
+                row = at + 16 + (s - 1) * 3 + j
+                short_ref[s, j : j + 1, lanes] = total[row : row + 1]
 
 
 def streamed(body, name, count, inputs, outputs, scratch_shapes=()):
@@ -525,12 +536,13 @@
         ],
         scratch_shapes=[
             pltpu.VMEM((owners, 2, rows_here, channels), bf16),
-            pltpu.VMEM((3, TAPS + 16, channels), bf16),
+            pltpu.VMEM((2, TAPS + 16, channels), bf16),
+            pltpu.VMEM((16, channels), bf16),
             pltpu.VMEM((TAPS + 8, channels), bf16),
             pltpu.VMEM((3, TAPS + 16, LANES), f32),
             pltpu.SemaphoreType.DMA((owners, 2)),
             pltpu.SemaphoreType.DMA((owners, 2)),
-            pltpu.SemaphoreType.DMA((2,)),
+            pltpu.SemaphoreType.DMA((3,)),
         ],
     )(cotangent, residual, streams, short_filter)
     halo = from_behind(halo, "dp", 1)
@@ -621,12 +633,12 @@
         [padded()],
     )
 
-    stream_grad, late = streamed(
+    stream_grad, bundle = streamed(
         backward_kernel,
         "backward",
         count,
         [
-            (streams, {}, 2),
+            (streams, {0: (1, 2)}, 2),
             (halo, {}, 1),
             (short_filter, {}, (2,)),
             (skip_row, {}, (1,)),
@@ -635,17 +647,18 @@
             (mixed, {}, 1),
             (inner, {}, 1),
             (tuple(after), {}, 1),
+            (early, {}, 0),
         ],
-        [(streams.shape, bf16, 2), ((columns * 8, LANES), f32, 0)],
+        [(streams.shape, bf16, 2), ((columns * 24, LANES), bf16, 0)],
         [padded(3), padded(3)],
     )
     bits = (lax.axis_size("dp") - 1).bit_length()
     stages = [[1 << n] if n + 1 == bits else [1 << n, 2 << n, 3 << n] for n in range(0, bits, 2)]
-    total = jnp.concatenate([early, late], axis=0)
+    total = bundle
     for stage in stages[:-1]:
         mine, others = sent_to(total, "dp", stage)
         total = added(mine, others)
-    block = min(rows_here, 16)
+    block = min(rows_here, 32)
     by_rows = spec((block, width_all), lambda i: (i, 0))
     normed, grad_residual = kernel(
         norm_kernel,

time: 102 us -> 98.4 us (0.965)
  local copies, waits for them, and re-layouts: 4.73 us -> 1.29 us
  starting transfers between devices: 21.4 us -> 22.8 us
    unnamed x14 -> x0, local copies, waits for them, and re-layouts: 4.13 us -> none
    ppermute x2, waiting for transfers between devices: 9.61 us -> 7.9 us  [from_behind(): lax.ppermute(value, axis, [(source, source + steps) for source in range(f...]
    pallas_call x1, Pallas kernels: 2.69 us -> 3.85 us  [local(): kernel(norm_kernel, 'norm', 4, NORM_LIMIT, grid=(rows_here // block,), in...]
  transfers between devices with their start and end apart: 8 -> 8, of which waited for: 6 -> 6; matrix products, arithmetic and copies ran while one was open for 2% -> 2% of each run, Pallas kernels for 35% -> 37%
where the time goes in v5:
time: 98.4 us; the launch traced here: 97.7 us
  Pallas kernels  51.2 us (52%)
  starting transfers between devices  22.8 us (23%)
  waiting for transfers between devices  14.3 us (15%)
  blocking collectives  6.47 us (7%)
  local copies, waits for them, and re-layouts  1.29 us (1%)
    pallas_call x5, Pallas kernels, streamed(): pl.pallas_call(kernel, in_specs=[pl.BlockSpec(memory_space=pl.ANY)] * fir...  35.5 us
    ppermute x2, waiting for transfers between devices, from_behind(): lax.ppermute(value, axis, [(source, source + steps) for source in range(f...  7.9 us
    ppermute x4, starting transfers between devices, sent_to(): lax.ppermute(half, axis, [(i, i ^ d) for i in range(count)])  7.03 us
    ppermute x2, starting transfers between devices, from_behind(): lax.ppermute(value, axis, [(source, source + steps) for source in range(f...  7.02 us
    pallas_call x1, Pallas kernels, local(): kernel(bands_kernel, 'bands', 5, grid=(groups // each,), in_specs=[spec((...  6.66 us
    psum x1, blocking collectives, local(): stats = lax.psum(stats, 'tensor')  6.47 us
    ppermute x4, waiting for transfers between devices, sent_to(): lax.ppermute(half, axis, [(i, i ^ d) for i in range(count)])  4.62 us
    all_to_all x1, starting transfers between devices, local(): lax.all_to_all(packed, 'tensor', split_axis=0, concat_axis=0, tiled=True)  4.46 us
  transfers between devices with their start and end apart: 8, of which 6 were waited for; matrix products, arithmetic and copies ran while one was open for 2% of the time, Pallas kernels for 37%

profile of v5, /device:TPU:0, one launch (start us, length us, event | category | flops | bytes accessed | tf_op | source)
XLA Modules:
  0.0 97.7 jit_solution(13532071886545213887)
XLA Ops:
  0.6 4.4 %open.1 = (bf16[4,2,64,2048]{3,2,1,0:T(8,128)(2,1)}, bf16[136,2048]{1,0:T(8,128)(2,1)}) custom-call(bf16[64,8192]{1,0:T(8,128)(2,1)} %cot_ref.3, bf16[64,8192]{1,0:T(8,128)(2,1)} %residual_ref.3, bf16[3,256,2048]{2,1,0:T(8,128)(2,1)} %refs_0_.7, f32[3,3,2048]{2,1,0:T(4,128)} %refs_2_.5), custom_call_target="tpu_custom_call" | custom-call | bytes 3000 | tf_op jit(solution)/shard_map/open/pallas_call | solution.py:527
  5.1 4.5 %all-to-all-start = ((bf16[4,2,64,2048]{3,2,1,0:T(8,128)(2,1)}), bf16[4,2,64,2048]{3,2,1,0:T(8,128)(2,1)}, u32[]{:S(2)}, u32[]{:S(2)}) async-start(bf16[4,2,64,2048]{3,2,1,0:T(8,128)(2,1)} %get-tuple-element.33), calls=%async_computation | async-start | bytes 4194304 | tf_op jit(solution)/shard_map/all_to_all | solution.py:549
  9.5 5.7 %collective-permute-start = (bf16[136,2048]{1,0:T(8,128)(2,1)}, bf16[136,2048]{1,0:T(8,128)(2,1)}, u32[]{:S(2)}, u32[]{:S(2)}) collective-permute-start(bf16[136,2048]{1,0:T(8,128)(2,1)} %get-tuple-element.31), channel_id=1, source_target_pairs={{0,4},{4,8},{8,12},{12,16},{16,20},{20,24},{24,28},{1,5},{5,9},{9,... | collective-permute-start | bytes 1671176 | tf_op jit(solution)/shard_map/ppermute | solution.py:371
  15.3 6.7 %bands.1 = (bf16[128,64,256]{2,1,0:T(8,128)(2,1)}, bf16[128,64,256]{2,1,0:T(8,128)(2,1)}) custom-call(f32[128,128]{1,0:T(8,128)} %refs_6_.1), custom_call_target="tpu_custom_call" | custom-call | bytes 5000 | tf_op jit(solution)/shard_map/bands/pallas_call | solution.py:553
  21.9 1.3 %dynamic_slice.3 = f32[2048]{0:T(1024)} dynamic-slice(f32[8192]{0:T(1024)} %param.12, s32[]{:T(128)S(6)} %select_n.3), dynamic_slice_sizes={2048} | dynamic-slice | bytes 16388 | tf_op jit(solution)/shard_map/dynamic_slice | solution.py:510
  23.2 4.0 %collective-permute-done.refs_1_.refs_3_ = bf16[136,2048]{1,0:T(8,128)(2,1)} collective-permute-done((bf16[136,2048]{1,0:T(8,128)(2,1)}, bf16[136,2048]{1,0:T(8,128)(2,1)}, u32[]{:S(2)}, u32[]{:S(2)}) %collective-permute-start) | collective-permute-done | bytes 557088 | tf_op jit(solution)/shard_map/ppermute | solution.py:371
  27.2 6.9 %forward.1 = (bf16[256,2048]{1,0:T(8,128)(2,1)}, f32[256,2048]{1,0:T(8,128)}, bf16[256,2048]{1,0:T(8,128)(2,1)}) custom-call(bf16[3,256,2048]{2,1,0:T(8,128)(2,1)} %refs_0_.7, bf16[136,2048]{1,0:T(8,128)(2,1)} %collective-permute-done.refs_1_.refs_3_, f32[3,3,2048]{2,1,0:T(4,128)} %refs_2_.5, f32[1,2048]{1,0:T(1,128)} %bitcast.9, ...), custom_call_target="tpu_custom_call" | custom-call | bytes 8000 | tf_op jit(solution)/shard_map/forward/pallas_call | solution.py:483
  34.1 1.8 %all-to-all-done.refs_0_.refs_8_ = bf16[4,2,64,2048]{3,2,1,0:T(8,128)(2,1)} async-done(((bf16[4,2,64,2048]{3,2,1,0:T(8,128)(2,1)}), bf16[4,2,64,2048]{3,2,1,0:T(8,128)(2,1)}, u32[]{:S(2)}, u32[]{:S(2)}) %all-to-all-start) | async-done | bytes 2097184 | tf_op jit(solution)/shard_map/all_to_all | solution.py:549
  35.9 2.9 %stats.1 = f32[2,256]{1,0:T(2,128)} custom-call(bf16[4,2,64,2048]{3,2,1,0:T(8,128)(2,1)} %all-to-all-done.refs_0_.refs_8_, bf16[256,2048]{1,0:T(8,128)(2,1)} %get-tuple-element.44.refs_1_.refs_9_, f32[1,2048]{1,0:T(1,128)} %bitcast.7), custom_call_target="tpu_custom_call" | custom-call | bytes 8000 | tf_op jit(solution)/shard_map/stats/pallas_call | solution.py:483
  38.8 6.5 %psum.7.refs_7_ = f32[2,256]{1,0:T(2,128)} all-reduce(f32[2,256]{1,0:T(2,128)} %stats.1), channel_id=1, replica_groups=mesh['dp'=8,'tensor'=4] {'tensor'}, use_global_device_ids=true, to_apply=%region_0.0 | all-reduce | flops 512 | bytes 4096 | tf_op jit(solution)/shard_map/psum | solution.py:580
  45.3 6.6 %head.1 = (bf16[256,2048]{1,0:T(8,128)(2,1)}, bf16[256,2048]{1,0:T(8,128)(2,1)}, f32[1,2048]{1,0:T(1,128)}, bf16[144,2048]{1,0:T(8,128)(2,1)}) custom-call(bf16[3,256,2048]{2,1,0:T(8,128)(2,1)} %refs_0_.7, bf16[3,256,2048]{2,1,0:T(8,128)(2,1)} %refs_0_.7, bf16[3,256,2048]{2,1,0:T(8,128)(2,1)} %refs_0_.7, ...), custom_call_target="tpu_custom_call" | custom-call | bytes 8000 | tf_op jit(solution)/shard_map/head/pallas_call | solution.py:483
  51.9 1.3 %collective-permute-start.1 = (bf16[144,2048]{1,0:T(8,128)(2,1)}, bf16[144,2048]{1,0:T(8,128)(2,1)}, u32[]{:S(2)}, u32[]{:S(2)}) collective-permute-start(bf16[144,2048]{1,0:T(8,128)(2,1)} %get-tuple-element.40), channel_id=1, source_target_pairs={{4,0},{8,4},{12,8},{16,12},{20,16},{24,20},{28,24},{5,1},{9,5},{13... | collective-permute-start | bytes 1769480 | tf_op jit(solution)/shard_map/ppermute | solution.py:371
  53.2 4.3 %all-to-all-start.1 = ((bf16[4,64,2048]{2,1,0:T(8,128)(2,1)}), bf16[4,64,2048]{2,1,0:T(8,128)(2,1)}, u32[]{:S(2)}, u32[]{:S(2)}) async-start(bf16[4,64,2048]{2,1,0:T(8,128)(2,1)} %bitcast.6), calls=%async_computation.1 | async-start | bytes 2097152 | tf_op jit(solution)/shard_map/all_to_all | solution.py:615
  57.4 8.4 %sums.1.refs_9_ = f32[256,128]{1,0:T(8,128)} custom-call(bf16[3,256,2048]{2,1,0:T(8,128)(2,1)} %refs_0_.7, bf16[136,2048]{1,0:T(8,128)(2,1)} %collective-permute-done.refs_1_.refs_3_, bf16[256,2048]{1,0:T(8,128)(2,1)} %get-tuple-element.41.refs_2_, bf16[256,2048]{1,0:T(8,128)(2,1)} %get-tuple-element.39.refs_3_.refs_7_, ...), custom_call_target="tpu_custom_call" | custom-call | bytes 8000 | tf_op jit(solution)/shard_map/sums/pallas_call | solution.py:483
  65.8 3.9 %collective-permute-done.1.refs_8_ = bf16[144,2048]{1,0:T(8,128)(2,1)} collective-permute-done((bf16[144,2048]{1,0:T(8,128)(2,1)}, bf16[144,2048]{1,0:T(8,128)(2,1)}, u32[]{:S(2)}, u32[]{:S(2)}) %collective-permute-start.1) | collective-permute-done | bytes 589856 | tf_op jit(solution)/shard_map/ppermute | solution.py:371
  69.7 10.8 %backward.1 = (bf16[3,256,2048]{2,1,0:T(8,128)(2,1)}, bf16[384,128]{1,0:T(8,128)(2,1)}) custom-call(bf16[3,256,2048]{2,1,0:T(8,128)(2,1)} %refs_0_.7, bf16[136,2048]{1,0:T(8,128)(2,1)} %collective-permute-done.refs_1_.refs_3_, f32[3,3,2048]{2,1,0:T(4,128)} %refs_2_.5, f32[1,2048]{1,0:T(1,128)} %bitcast.11, bf16[128,64,256]{2,1,0:T(8,128)(2,1)} %get-tuple-element.32.refs_4_, ...), custom_call_target="tpu_custom_call" | custom-call | bytes 8000 | tf_op jit(solution)/shard_map/backward/pallas_call | solution.py:483
  80.5 3.7 %collective-permute-start.4 = (bf16[384,128]{1,0:T(8,128)(2,1)}, bf16[384,128]{1,0:T(8,128)(2,1)S(1)}, u32[]{:S(2)}, u32[]{:S(2)}) collective-permute-start(bf16[384,128]{1,0:T(8,128)(2,1)} %get-tuple-element.43), channel_id=1, source_target_pairs={{0,12},{4,8},{8,4},{12,0},{16,28},{20,24},{24,20},{28,16},{1,13},{... | collective-permute-start | bytes 294920 | tf_op jit(solution)/shard_map/ppermute | solution.py:380
  84.2 0.4 collective-permute-start.3
  84.7 0.2 collective-permute-start.2
  84.9 2.6 %collective-permute-done.4 = bf16[384,128]{1,0:T(8,128)(2,1)S(1)} collective-permute-done((bf16[384,128]{1,0:T(8,128)(2,1)}, bf16[384,128]{1,0:T(8,128)(2,1)S(1)}, u32[]{:S(2)}, u32[]{:S(2)}) %collective-permute-start.4) | collective-permute-done | bytes 98336 | tf_op jit(solution)/shard_map/ppermute | solution.py:380
  87.4 1.6 %collective-permute-done.3 = bf16[384,128]{1,0:T(8,128)(2,1)S(1)} collective-permute-done((bf16[384,128]{1,0:T(8,128)(2,1)}, bf16[384,128]{1,0:T(8,128)(2,1)S(1)}, u32[]{:S(2)}, u32[]{:S(2)}) %collective-permute-start.3) | collective-permute-done | bytes 98336 | tf_op jit(solution)/shard_map/ppermute | solution.py:380
  89.1 0.4 collective-permute-done.2
  89.5 1.0 fusion
  90.4 2.7 %collective-permute-start.5 = (bf16[384,128]{1,0:T(8,128)(2,1)S(1)}, bf16[384,128]{1,0:T(8,128)(2,1)S(1)}, u32[]{:S(2)}, u32[]{:S(2)}) collective-permute-start(bf16[384,128]{1,0:T(8,128)(2,1)S(1)} %get-tuple-element.55), channel_id=1, source_target_pairs={{0,16},{4,20},{8,24},{12,28},{16,0},{20,4},{24,8},{28,12},{1,17},{... | collective-permute-start | bytes 294920 | tf_op jit(solution)/shard_map/ppermute | solution.py:380
  93.1 0.0 all-to-all-done.1.received_ref
  93.1 3.9 %norm.1 = (bf16[64,8192]{1,0:T(8,128)(2,1)}, bf16[64,8192]{1,0:T(8,128)(2,1)}) custom-call(bf16[4,64,2048]{2,1,0:T(8,128)(2,1)} %all-to-all-done.1.received_ref, bf16[64,8192]{1,0:T(8,128)(2,1)} %residual_ref.3, bf16[64,8192]{1,0:T(8,128)(2,1)} %cot_ref.3, f32[1,8192]{1,0:T(1,128)} %bitcast.12), custom_call_target="tpu_custom_call" | custom-call | bytes 4000 | tf_op jit(solution)/shard_map/norm/pallas_call | solution.py:663
  97.0 0.0 collective-permute-done.5.other_ref
  97.0 0.7 close.1
Async XLA Ops:
  5.1 30.8 %all-to-all-start = ((bf16[4,2,64,2048]{3,2,1,0:T(8,128)(2,1)}), bf16[4,2,64,2048]{3,2,1,0:T(8,128)(2,1)}, u32[]{:S(2)}, u32[]{:S(2)}) async-start(bf16[4,2,64,2048]{3,2,1,0:T(8,128)(2,1)} %get-tuple-element.33), calls=%async_computation | async-start | bytes 4194304 | tf_op jit(solution)/shard_map/all_to_all | solution.py:549
  9.5 17.7 %collective-permute-start = (bf16[136,2048]{1,0:T(8,128)(2,1)}, bf16[136,2048]{1,0:T(8,128)(2,1)}, u32[]{:S(2)}, u32[]{:S(2)}) collective-permute-start(bf16[136,2048]{1,0:T(8,128)(2,1)} %get-tuple-element.31), channel_id=1, source_target_pairs={{0,4},{4,8},{8,12},{12,16},{16,20},{20,24},{24,28},{1,5},{5,9},{9,... | collective-permute-start | bytes 1671176 | tf_op jit(solution)/shard_map/ppermute | solution.py:371
  51.9 17.8 %collective-permute-start.1 = (bf16[144,2048]{1,0:T(8,128)(2,1)}, bf16[144,2048]{1,0:T(8,128)(2,1)}, u32[]{:S(2)}, u32[]{:S(2)}) collective-permute-start(bf16[144,2048]{1,0:T(8,128)(2,1)} %get-tuple-element.40), channel_id=1, source_target_pairs={{4,0},{8,4},{12,8},{16,12},{20,16},{24,20},{28,24},{5,1},{9,5},{13... | collective-permute-start | bytes 1769480 | tf_op jit(solution)/shard_map/ppermute | solution.py:371
  53.2 40.0 %all-to-all-start.1 = ((bf16[4,64,2048]{2,1,0:T(8,128)(2,1)}), bf16[4,64,2048]{2,1,0:T(8,128)(2,1)}, u32[]{:S(2)}, u32[]{:S(2)}) async-start(bf16[4,64,2048]{2,1,0:T(8,128)(2,1)} %bitcast.6), calls=%async_computation.1 | async-start | bytes 2097152 | tf_op jit(solution)/shard_map/all_to_all | solution.py:615
  80.5 6.9 %collective-permute-start.4 = (bf16[384,128]{1,0:T(8,128)(2,1)}, bf16[384,128]{1,0:T(8,128)(2,1)S(1)}, u32[]{:S(2)}, u32[]{:S(2)}) collective-permute-start(bf16[384,128]{1,0:T(8,128)(2,1)} %get-tuple-element.43), channel_id=1, source_target_pairs={{0,12},{4,8},{8,4},{12,0},{16,28},{20,24},{24,20},{28,16},{1,13},{... | collective-permute-start | bytes 294920 | tf_op jit(solution)/shard_map/ppermute | solution.py:380
  84.2 4.8 %collective-permute-start.3 = (bf16[384,128]{1,0:T(8,128)(2,1)}, bf16[384,128]{1,0:T(8,128)(2,1)S(1)}, u32[]{:S(2)}, u32[]{:S(2)}) collective-permute-start(bf16[384,128]{1,0:T(8,128)(2,1)} %get-tuple-element.43), channel_id=1, source_target_pairs={{0,8},{4,12},{8,0},{12,4},{16,24},{20,28},{24,16},{28,20},{1,9},{5... | collective-permute-start | bytes 294920 | tf_op jit(solution)/shard_map/ppermute | solution.py:380
  84.7 4.8 %collective-permute-start.2 = (bf16[384,128]{1,0:T(8,128)(2,1)}, bf16[384,128]{1,0:T(8,128)(2,1)S(1)}, u32[]{:S(2)}, u32[]{:S(2)}) collective-permute-start(bf16[384,128]{1,0:T(8,128)(2,1)} %get-tuple-element.43), channel_id=1, source_target_pairs={{0,4},{4,0},{8,12},{12,8},{16,20},{20,16},{24,28},{28,24},{1,5},{5... | collective-permute-start | bytes 294920 | tf_op jit(solution)/shard_map/ppermute | solution.py:380
  90.4 6.5 %collective-permute-start.5 = (bf16[384,128]{1,0:T(8,128)(2,1)S(1)}, bf16[384,128]{1,0:T(8,128)(2,1)S(1)}, u32[]{:S(2)}, u32[]{:S(2)}) collective-permute-start(bf16[384,128]{1,0:T(8,128)(2,1)S(1)} %get-tuple-element.55), channel_id=1, source_target_pairs={{0,16},{4,20},{8,24},{12,28},{16,0},{20,4},{24,8},{28,12},{1,17},{... | collective-permute-start | bytes 294920 | tf_op jit(solution)/shard_map/ppermute | solution.py:380

commit v6 on v5

--- a/solution.py
+++ b/solution.py
@@ -274,9 +274,7 @@
         scratch[4:6, :] = (grad_gated * features[0])[:2]
         scratch[6:8, :] = jnp.zeros((2, LANES), f32)
         rows = scratch[0:8, :]
-        high = rows.astype(bf16)
-        first_ref[TAPS : TAPS + 8, lanes] = high
-        first_ref[TAPS + 8 : TAPS + 16, lanes] = (rows - high.astype(f32)).astype(bf16)
+        first_ref[TAPS : TAPS + 8, lanes] = rows.astype(bf16)
 
 
 def sums_kernel(index, streams_ref, halo_ref, gated_ref, inner_ref, grad_ref, mixed_ref, gain_ref, early_ref, scratch):
@@ -347,8 +345,7 @@
             grad_gated * features[2],
             grad_gated * features[1],
         )
-        following = after_ref[TAPS : TAPS + 16, lanes].astype(f32)
-        following = following[:8] + following[8:]
+        following = after_ref[TAPS : TAPS + 8, lanes].astype(f32)
         for s in range(3):
             ahead[s, 0:length, :] = grads[s]
             ahead[s, length : length + 2, :] = following[2 * s : 2 * s + 2]
@@ -604,7 +601,7 @@
                     ((tokens_here, part), bf16, 1),
                     ((tokens_here, part), bf16, 1),
                     ((1, part), f32, (1,)),
-                    ((TAPS + 16, part), bf16, 1),
+                    ((TAPS + 8, part), bf16, 1),
                 ],
                 [padded()] + [pltpu.VMEM((tokens_here, LANES), f32)] * 2,
             )

time: 98.4 us -> 97.7 us (level)
  transfers between devices with their start and end apart: 8 -> 8, of which waited for: 6 -> 6; matrix products, arithmetic and copies ran while one was open for 2% -> 2% of each run, Pallas kernels for 37% -> 38%
where the time goes in v6:
time: 97.7 us; the launch traced here: 97 us
  Pallas kernels  51.2 us (52%)
  starting transfers between devices  22.7 us (23%)
  waiting for transfers between devices  13.6 us (14%)
  blocking collectives  6.47 us (7%)
  local copies, waits for them, and re-layouts  1.29 us (1%)
    pallas_call x5, Pallas kernels, streamed(): pl.pallas_call(kernel, in_specs=[pl.BlockSpec(memory_space=pl.ANY)] * fir...  35.5 us
    ppermute x2, waiting for transfers between devices, from_behind(): lax.ppermute(value, axis, [(source, source + steps) for source in range(f...  7.2 us
    ppermute x2, starting transfers between devices, from_behind(): lax.ppermute(value, axis, [(source, source + steps) for source in range(f...  7.02 us
    ppermute x4, starting transfers between devices, sent_to(): lax.ppermute(half, axis, [(i, i ^ d) for i in range(count)])  7 us
    pallas_call x1, Pallas kernels, local(): kernel(bands_kernel, 'bands', 5, grid=(groups // each,), in_specs=[spec((...  6.66 us
    psum x1, blocking collectives, local(): stats = lax.psum(stats, 'tensor')  6.47 us
    ppermute x4, waiting for transfers between devices, sent_to(): lax.ppermute(half, axis, [(i, i ^ d) for i in range(count)])  4.64 us
    all_to_all x1, starting transfers between devices, local(): lax.all_to_all(packed, 'tensor', split_axis=0, concat_axis=0, tiled=True)  4.46 us
  transfers between devices with their start and end apart: 8, of which 6 were waited for; matrix products, arithmetic and copies ran while one was open for 2% of the time, Pallas kernels for 38%

profile of v6, /device:TPU:0, one launch (start us, length us, event | category | flops | bytes accessed | tf_op | source)
XLA Modules:
  0.0 97.0 jit_solution(14755339916323119315)
XLA Ops:
  0.6 4.4 %open.1 = (bf16[4,2,64,2048]{3,2,1,0:T(8,128)(2,1)}, bf16[136,2048]{1,0:T(8,128)(2,1)}) custom-call(bf16[64,8192]{1,0:T(8,128)(2,1)} %cot_ref.3, bf16[64,8192]{1,0:T(8,128)(2,1)} %residual_ref.3, bf16[3,256,2048]{2,1,0:T(8,128)(2,1)} %refs_0_.7, f32[3,3,2048]{2,1,0:T(4,128)} %refs_2_.5), custom_call_target="tpu_custom_call" | custom-call | bytes 3000 | tf_op jit(solution)/shard_map/open/pallas_call | solution.py:524
  5.1 4.5 %all-to-all-start = ((bf16[4,2,64,2048]{3,2,1,0:T(8,128)(2,1)}), bf16[4,2,64,2048]{3,2,1,0:T(8,128)(2,1)}, u32[]{:S(2)}, u32[]{:S(2)}) async-start(bf16[4,2,64,2048]{3,2,1,0:T(8,128)(2,1)} %get-tuple-element.33), calls=%async_computation | async-start | bytes 4194304 | tf_op jit(solution)/shard_map/all_to_all | solution.py:546
  9.5 5.7 %collective-permute-start = (bf16[136,2048]{1,0:T(8,128)(2,1)}, bf16[136,2048]{1,0:T(8,128)(2,1)}, u32[]{:S(2)}, u32[]{:S(2)}) collective-permute-start(bf16[136,2048]{1,0:T(8,128)(2,1)} %get-tuple-element.31), channel_id=1, source_target_pairs={{0,4},{4,8},{8,12},{12,16},{16,20},{20,24},{24,28},{1,5},{5,9},{9,... | collective-permute-start | bytes 1671176 | tf_op jit(solution)/shard_map/ppermute | solution.py:368
  15.3 6.7 %bands.1 = (bf16[128,64,256]{2,1,0:T(8,128)(2,1)}, bf16[128,64,256]{2,1,0:T(8,128)(2,1)}) custom-call(f32[128,128]{1,0:T(8,128)} %refs_6_.1), custom_call_target="tpu_custom_call" | custom-call | bytes 5000 | tf_op jit(solution)/shard_map/bands/pallas_call | solution.py:550
  21.9 1.3 %dynamic_slice.3 = f32[2048]{0:T(1024)} dynamic-slice(f32[8192]{0:T(1024)} %param.12, s32[]{:T(128)S(6)} %select_n.3), dynamic_slice_sizes={2048} | dynamic-slice | bytes 16388 | tf_op jit(solution)/shard_map/dynamic_slice | solution.py:507
  23.2 4.0 %collective-permute-done.refs_1_.refs_3_ = bf16[136,2048]{1,0:T(8,128)(2,1)} collective-permute-done((bf16[136,2048]{1,0:T(8,128)(2,1)}, bf16[136,2048]{1,0:T(8,128)(2,1)}, u32[]{:S(2)}, u32[]{:S(2)}) %collective-permute-start) | collective-permute-done | bytes 557088 | tf_op jit(solution)/shard_map/ppermute | solution.py:368
  27.2 6.9 %forward.1 = (bf16[256,2048]{1,0:T(8,128)(2,1)}, f32[256,2048]{1,0:T(8,128)}, bf16[256,2048]{1,0:T(8,128)(2,1)}) custom-call(bf16[3,256,2048]{2,1,0:T(8,128)(2,1)} %refs_0_.7, bf16[136,2048]{1,0:T(8,128)(2,1)} %collective-permute-done.refs_1_.refs_3_, f32[3,3,2048]{2,1,0:T(4,128)} %refs_2_.5, f32[1,2048]{1,0:T(1,128)} %bitcast.9, ...), custom_call_target="tpu_custom_call" | custom-call | bytes 8000 | tf_op jit(solution)/shard_map/forward/pallas_call | solution.py:480
  34.1 1.8 %all-to-all-done.refs_0_.refs_8_ = bf16[4,2,64,2048]{3,2,1,0:T(8,128)(2,1)} async-done(((bf16[4,2,64,2048]{3,2,1,0:T(8,128)(2,1)}), bf16[4,2,64,2048]{3,2,1,0:T(8,128)(2,1)}, u32[]{:S(2)}, u32[]{:S(2)}) %all-to-all-start) | async-done | bytes 2097184 | tf_op jit(solution)/shard_map/all_to_all | solution.py:546
  35.9 2.9 %stats.1 = f32[2,256]{1,0:T(2,128)} custom-call(bf16[4,2,64,2048]{3,2,1,0:T(8,128)(2,1)} %all-to-all-done.refs_0_.refs_8_, bf16[256,2048]{1,0:T(8,128)(2,1)} %get-tuple-element.44.refs_1_.refs_9_, f32[1,2048]{1,0:T(1,128)} %bitcast.7), custom_call_target="tpu_custom_call" | custom-call | bytes 8000 | tf_op jit(solution)/shard_map/stats/pallas_call | solution.py:480
  38.8 6.5 %psum.7.refs_7_ = f32[2,256]{1,0:T(2,128)} all-reduce(f32[2,256]{1,0:T(2,128)} %stats.1), channel_id=1, replica_groups=mesh['dp'=8,'tensor'=4] {'tensor'}, use_global_device_ids=true, to_apply=%region_0.0 | all-reduce | flops 512 | bytes 4096 | tf_op jit(solution)/shard_map/psum | solution.py:577
  45.3 6.6 %head.1 = (bf16[256,2048]{1,0:T(8,128)(2,1)}, bf16[256,2048]{1,0:T(8,128)(2,1)}, f32[1,2048]{1,0:T(1,128)}, bf16[136,2048]{1,0:T(8,128)(2,1)}) custom-call(bf16[3,256,2048]{2,1,0:T(8,128)(2,1)} %refs_0_.7, bf16[3,256,2048]{2,1,0:T(8,128)(2,1)} %refs_0_.7, bf16[3,256,2048]{2,1,0:T(8,128)(2,1)} %refs_0_.7, ...), custom_call_target="tpu_custom_call" | custom-call | bytes 8000 | tf_op jit(solution)/shard_map/head/pallas_call | solution.py:480
  51.8 1.3 %collective-permute-start.1 = (bf16[136,2048]{1,0:T(8,128)(2,1)}, bf16[136,2048]{1,0:T(8,128)(2,1)}, u32[]{:S(2)}, u32[]{:S(2)}) collective-permute-start(bf16[136,2048]{1,0:T(8,128)(2,1)} %get-tuple-element.40), channel_id=1, source_target_pairs={{4,0},{8,4},{12,8},{16,12},{20,16},{24,20},{28,24},{5,1},{9,5},{13... | collective-permute-start | bytes 1671176 | tf_op jit(solution)/shard_map/ppermute | solution.py:368
  53.1 4.3 %all-to-all-start.1 = ((bf16[4,64,2048]{2,1,0:T(8,128)(2,1)}), bf16[4,64,2048]{2,1,0:T(8,128)(2,1)}, u32[]{:S(2)}, u32[]{:S(2)}) async-start(bf16[4,64,2048]{2,1,0:T(8,128)(2,1)} %bitcast.6), calls=%async_computation.1 | async-start | bytes 2097152 | tf_op jit(solution)/shard_map/all_to_all | solution.py:612
  57.4 8.4 %sums.1.refs_9_ = f32[256,128]{1,0:T(8,128)} custom-call(bf16[3,256,2048]{2,1,0:T(8,128)(2,1)} %refs_0_.7, bf16[136,2048]{1,0:T(8,128)(2,1)} %collective-permute-done.refs_1_.refs_3_, bf16[256,2048]{1,0:T(8,128)(2,1)} %get-tuple-element.41.refs_2_, bf16[256,2048]{1,0:T(8,128)(2,1)} %get-tuple-element.39.refs_3_.refs_7_, ...), custom_call_target="tpu_custom_call" | custom-call | bytes 8000 | tf_op jit(solution)/shard_map/sums/pallas_call | solution.py:480
  65.8 3.2 %collective-permute-done.1.refs_8_ = bf16[136,2048]{1,0:T(8,128)(2,1)} collective-permute-done((bf16[136,2048]{1,0:T(8,128)(2,1)}, bf16[136,2048]{1,0:T(8,128)(2,1)}, u32[]{:S(2)}, u32[]{:S(2)}) %collective-permute-start.1) | collective-permute-done | bytes 557088 | tf_op jit(solution)/shard_map/ppermute | solution.py:368
  69.0 10.8 %backward.1 = (bf16[3,256,2048]{2,1,0:T(8,128)(2,1)}, bf16[384,128]{1,0:T(8,128)(2,1)}) custom-call(bf16[3,256,2048]{2,1,0:T(8,128)(2,1)} %refs_0_.7, bf16[136,2048]{1,0:T(8,128)(2,1)} %collective-permute-done.refs_1_.refs_3_, f32[3,3,2048]{2,1,0:T(4,128)} %refs_2_.5, f32[1,2048]{1,0:T(1,128)} %bitcast.11, bf16[128,64,256]{2,1,0:T(8,128)(2,1)} %get-tuple-element.32.refs_4_, ...), custom_call_target="tpu_custom_call" | custom-call | bytes 8000 | tf_op jit(solution)/shard_map/backward/pallas_call | solution.py:480
  79.8 3.7 %collective-permute-start.4 = (bf16[384,128]{1,0:T(8,128)(2,1)}, bf16[384,128]{1,0:T(8,128)(2,1)S(1)}, u32[]{:S(2)}, u32[]{:S(2)}) collective-permute-start(bf16[384,128]{1,0:T(8,128)(2,1)} %get-tuple-element.43), channel_id=1, source_target_pairs={{0,12},{4,8},{8,4},{12,0},{16,28},{20,24},{24,20},{28,16},{1,13},{... | collective-permute-start | bytes 294920 | tf_op jit(solution)/shard_map/ppermute | solution.py:377
  83.5 0.5 collective-permute-start.3
  84.0 0.2 collective-permute-start.2
  84.2 3.0 %collective-permute-done.4 = bf16[384,128]{1,0:T(8,128)(2,1)S(1)} collective-permute-done((bf16[384,128]{1,0:T(8,128)(2,1)}, bf16[384,128]{1,0:T(8,128)(2,1)S(1)}, u32[]{:S(2)}, u32[]{:S(2)}) %collective-permute-start.4) | collective-permute-done | bytes 98336 | tf_op jit(solution)/shard_map/ppermute | solution.py:377
  87.2 1.1 %collective-permute-done.3 = bf16[384,128]{1,0:T(8,128)(2,1)S(1)} collective-permute-done((bf16[384,128]{1,0:T(8,128)(2,1)}, bf16[384,128]{1,0:T(8,128)(2,1)S(1)}, u32[]{:S(2)}, u32[]{:S(2)}) %collective-permute-start.3) | collective-permute-done | bytes 98336 | tf_op jit(solution)/shard_map/ppermute | solution.py:377
  88.4 0.5 collective-permute-done.2
  88.8 1.0 fusion
  89.8 2.7 %collective-permute-start.5 = (bf16[384,128]{1,0:T(8,128)(2,1)S(1)}, bf16[384,128]{1,0:T(8,128)(2,1)S(1)}, u32[]{:S(2)}, u32[]{:S(2)}) collective-permute-start(bf16[384,128]{1,0:T(8,128)(2,1)S(1)} %get-tuple-element.55), channel_id=1, source_target_pairs={{0,16},{4,20},{8,24},{12,28},{16,0},{20,4},{24,8},{28,12},{1,17},{... | collective-permute-start | bytes 294920 | tf_op jit(solution)/shard_map/ppermute | solution.py:377
  92.4 0.0 all-to-all-done.1.received_ref
  92.4 3.9 %norm.1 = (bf16[64,8192]{1,0:T(8,128)(2,1)}, bf16[64,8192]{1,0:T(8,128)(2,1)}) custom-call(bf16[4,64,2048]{2,1,0:T(8,128)(2,1)} %all-to-all-done.1.received_ref, bf16[64,8192]{1,0:T(8,128)(2,1)} %residual_ref.3, bf16[64,8192]{1,0:T(8,128)(2,1)} %cot_ref.3, f32[1,8192]{1,0:T(1,128)} %bitcast.12), custom_call_target="tpu_custom_call" | custom-call | bytes 4000 | tf_op jit(solution)/shard_map/norm/pallas_call | solution.py:660
  96.3 0.0 collective-permute-done.5.other_ref
  96.3 0.7 close.1
Async XLA Ops:
  5.1 30.8 %all-to-all-start = ((bf16[4,2,64,2048]{3,2,1,0:T(8,128)(2,1)}), bf16[4,2,64,2048]{3,2,1,0:T(8,128)(2,1)}, u32[]{:S(2)}, u32[]{:S(2)}) async-start(bf16[4,2,64,2048]{3,2,1,0:T(8,128)(2,1)} %get-tuple-element.33), calls=%async_computation | async-start | bytes 4194304 | tf_op jit(solution)/shard_map/all_to_all | solution.py:546
  9.5 17.7 %collective-permute-start = (bf16[136,2048]{1,0:T(8,128)(2,1)}, bf16[136,2048]{1,0:T(8,128)(2,1)}, u32[]{:S(2)}, u32[]{:S(2)}) collective-permute-start(bf16[136,2048]{1,0:T(8,128)(2,1)} %get-tuple-element.31), channel_id=1, source_target_pairs={{0,4},{4,8},{8,12},{12,16},{16,20},{20,24},{24,28},{1,5},{5,9},{9,... | collective-permute-start | bytes 1671176 | tf_op jit(solution)/shard_map/ppermute | solution.py:368
  51.8 17.1 %collective-permute-start.1 = (bf16[136,2048]{1,0:T(8,128)(2,1)}, bf16[136,2048]{1,0:T(8,128)(2,1)}, u32[]{:S(2)}, u32[]{:S(2)}) collective-permute-start(bf16[136,2048]{1,0:T(8,128)(2,1)} %get-tuple-element.40), channel_id=1, source_target_pairs={{4,0},{8,4},{12,8},{16,12},{20,16},{24,20},{28,24},{5,1},{9,5},{13... | collective-permute-start | bytes 1671176 | tf_op jit(solution)/shard_map/ppermute | solution.py:368
  53.1 39.3 %all-to-all-start.1 = ((bf16[4,64,2048]{2,1,0:T(8,128)(2,1)}), bf16[4,64,2048]{2,1,0:T(8,128)(2,1)}, u32[]{:S(2)}, u32[]{:S(2)}) async-start(bf16[4,64,2048]{2,1,0:T(8,128)(2,1)} %bitcast.6), calls=%async_computation.1 | async-start | bytes 2097152 | tf_op jit(solution)/shard_map/all_to_all | solution.py:612
  79.8 7.4 %collective-permute-start.4 = (bf16[384,128]{1,0:T(8,128)(2,1)}, bf16[384,128]{1,0:T(8,128)(2,1)S(1)}, u32[]{:S(2)}, u32[]{:S(2)}) collective-permute-start(bf16[384,128]{1,0:T(8,128)(2,1)} %get-tuple-element.43), channel_id=1, source_target_pairs={{0,12},{4,8},{8,4},{12,0},{16,28},{20,24},{24,20},{28,16},{1,13},{... | collective-permute-start | bytes 294920 | tf_op jit(solution)/shard_map/ppermute | solution.py:377
  83.5 4.8 %collective-permute-start.3 = (bf16[384,128]{1,0:T(8,128)(2,1)}, bf16[384,128]{1,0:T(8,128)(2,1)S(1)}, u32[]{:S(2)}, u32[]{:S(2)}) collective-permute-start(bf16[384,128]{1,0:T(8,128)(2,1)} %get-tuple-element.43), channel_id=1, source_target_pairs={{0,8},{4,12},{8,0},{12,4},{16,24},{20,28},{24,16},{28,20},{1,9},{5... | collective-permute-start | bytes 294920 | tf_op jit(solution)/shard_map/ppermute | solution.py:377
  84.0 4.8 %collective-permute-start.2 = (bf16[384,128]{1,0:T(8,128)(2,1)}, bf16[384,128]{1,0:T(8,128)(2,1)S(1)}, u32[]{:S(2)}, u32[]{:S(2)}) collective-permute-start(bf16[384,128]{1,0:T(8,128)(2,1)} %get-tuple-element.43), channel_id=1, source_target_pairs={{0,4},{4,0},{8,12},{12,8},{16,20},{20,16},{24,28},{28,24},{1,5},{5... | collective-permute-start | bytes 294920 | tf_op jit(solution)/shard_map/ppermute | solution.py:377
  89.8 6.5 %collective-permute-start.5 = (bf16[384,128]{1,0:T(8,128)(2,1)S(1)}, bf16[384,128]{1,0:T(8,128)(2,1)S(1)}, u32[]{:S(2)}, u32[]{:S(2)}) collective-permute-start(bf16[384,128]{1,0:T(8,128)(2,1)S(1)} %get-tuple-element.55), channel_id=1, source_target_pairs={{0,16},{4,20},{8,24},{12,28},{16,0},{20,4},{24,8},{28,12},{1,17},{... | collective-permute-start | bytes 294920 | tf_op jit(solution)/shard_map/ppermute | solution.py:377

commit v7 on v6

--- a/solution.py
+++ b/solution.py
@@ -39,11 +39,18 @@
 
 
 def pick_groups(stacked, rows):
-    out = stacked[:rows]
-    which = lane_group(out.shape)
-    for g in range(1, PER):
-        out = jnp.where(which == g, stacked[g * rows : (g + 1) * rows], out)
-    return out
+    lane = lane_group((rows, LANES))
+    picked = []
+    for at in range(0, stacked.shape[1], LANES):
+        parts = [stacked[g * rows : (g + 1) * rows, at : at + LANES] for g in range(PER)]
+        bit = PER // 2
+        while len(parts) > 1:
+            upper = lane % (2 * bit) >= bit
+            half = len(parts) // 2
+            parts = [jnp.where(upper, parts[i + half], parts[i]) for i in range(half)]
+            bit //= 2
+        picked.append(parts[0])
+    return jnp.concatenate(picked, axis=1)
 
 
 def shifted(scratch, halo, current):

time: 97.7 us -> 97.7 us (level)
  no operation moved by 1% of the time
where the time goes in v7:
time: 97.7 us; the launch traced here: 97 us
  Pallas kernels  51.3 us (53%)
  starting transfers between devices  22.8 us (23%)
  waiting for transfers between devices  13.5 us (14%)
  blocking collectives  6.47 us (7%)
  local copies, waits for them, and re-layouts  1.29 us (1%)
    pallas_call x5, Pallas kernels, streamed(): pl.pallas_call(kernel, in_specs=[pl.BlockSpec(memory_space=pl.ANY)] * fir...  35.7 us
    ppermute x2, waiting for transfers between devices, from_behind(): lax.ppermute(value, axis, [(source, source + steps) for source in range(f...  7.2 us
    ppermute x2, starting transfers between devices, from_behind(): lax.ppermute(value, axis, [(source, source + steps) for source in range(f...  7.02 us
    ppermute x4, starting transfers between devices, sent_to(): lax.ppermute(half, axis, [(i, i ^ d) for i in range(count)])  7.02 us
    pallas_call x1, Pallas kernels, local(): kernel(bands_kernel, 'bands', 5, grid=(groups // each,), in_specs=[spec((...  6.66 us
    psum x1, blocking collectives, local(): stats = lax.psum(stats, 'tensor')  6.47 us
    ppermute x4, waiting for transfers between devices, sent_to(): lax.ppermute(half, axis, [(i, i ^ d) for i in range(count)])  4.64 us
    all_to_all x1, starting transfers between devices, local(): lax.all_to_all(packed, 'tensor', split_axis=0, concat_axis=0, tiled=True)  4.46 us
  transfers between devices with their start and end apart: 8, of which 6 were waited for; matrix products, arithmetic and copies ran while one was open for 2% of the time, Pallas kernels for 38%

profile of v7, /device:TPU:0, one launch (start us, length us, event | category | flops | bytes accessed | tf_op | source)
XLA Modules:
  0.0 97.0 jit_solution(1880977628933288870)
XLA Ops:
  0.6 4.4 %open.1 = (bf16[4,2,64,2048]{3,2,1,0:T(8,128)(2,1)}, bf16[136,2048]{1,0:T(8,128)(2,1)}) custom-call(bf16[64,8192]{1,0:T(8,128)(2,1)} %cot_ref.3, bf16[64,8192]{1,0:T(8,128)(2,1)} %residual_ref.3, bf16[3,256,2048]{2,1,0:T(8,128)(2,1)} %refs_0_.7, f32[3,3,2048]{2,1,0:T(4,128)} %refs_2_.5), custom_call_target="tpu_custom_call" | custom-call | bytes 3000 | tf_op jit(solution)/shard_map/open/pallas_call | solution.py:531
  5.1 4.5 %all-to-all-start = ((bf16[4,2,64,2048]{3,2,1,0:T(8,128)(2,1)}), bf16[4,2,64,2048]{3,2,1,0:T(8,128)(2,1)}, u32[]{:S(2)}, u32[]{:S(2)}) async-start(bf16[4,2,64,2048]{3,2,1,0:T(8,128)(2,1)} %get-tuple-element.33), calls=%async_computation | async-start | bytes 4194304 | tf_op jit(solution)/shard_map/all_to_all | solution.py:553
  9.5 5.7 %collective-permute-start = (bf16[136,2048]{1,0:T(8,128)(2,1)}, bf16[136,2048]{1,0:T(8,128)(2,1)}, u32[]{:S(2)}, u32[]{:S(2)}) collective-permute-start(bf16[136,2048]{1,0:T(8,128)(2,1)} %get-tuple-element.31), channel_id=1, source_target_pairs={{0,4},{4,8},{8,12},{12,16},{16,20},{20,24},{24,28},{1,5},{5,9},{9,... | collective-permute-start | bytes 1671176 | tf_op jit(solution)/shard_map/ppermute | solution.py:375
  15.3 6.7 %bands.1 = (bf16[128,64,256]{2,1,0:T(8,128)(2,1)}, bf16[128,64,256]{2,1,0:T(8,128)(2,1)}) custom-call(f32[128,128]{1,0:T(8,128)} %refs_6_.1), custom_call_target="tpu_custom_call" | custom-call | bytes 5000 | tf_op jit(solution)/shard_map/bands/pallas_call | solution.py:557
  21.9 1.3 %dynamic_slice.3 = f32[2048]{0:T(1024)} dynamic-slice(f32[8192]{0:T(1024)} %param.12, s32[]{:T(128)S(6)} %select_n.3), dynamic_slice_sizes={2048} | dynamic-slice | bytes 16388 | tf_op jit(solution)/shard_map/dynamic_slice | solution.py:514
  23.2 4.0 %collective-permute-done.refs_1_.refs_3_ = bf16[136,2048]{1,0:T(8,128)(2,1)} collective-permute-done((bf16[136,2048]{1,0:T(8,128)(2,1)}, bf16[136,2048]{1,0:T(8,128)(2,1)}, u32[]{:S(2)}, u32[]{:S(2)}) %collective-permute-start) | collective-permute-done | bytes 557088 | tf_op jit(solution)/shard_map/ppermute | solution.py:375
  27.2 7.1 %forward.1 = (bf16[256,2048]{1,0:T(8,128)(2,1)}, f32[256,2048]{1,0:T(8,128)}, bf16[256,2048]{1,0:T(8,128)(2,1)}) custom-call(bf16[3,256,2048]{2,1,0:T(8,128)(2,1)} %refs_0_.7, bf16[136,2048]{1,0:T(8,128)(2,1)} %collective-permute-done.refs_1_.refs_3_, f32[3,3,2048]{2,1,0:T(4,128)} %refs_2_.5, f32[1,2048]{1,0:T(1,128)} %bitcast.9, ...), custom_call_target="tpu_custom_call" | custom-call | bytes 8000 | tf_op jit(solution)/shard_map/forward/pallas_call | solution.py:487
  34.3 1.6 %all-to-all-done.refs_0_.refs_8_ = bf16[4,2,64,2048]{3,2,1,0:T(8,128)(2,1)} async-done(((bf16[4,2,64,2048]{3,2,1,0:T(8,128)(2,1)}), bf16[4,2,64,2048]{3,2,1,0:T(8,128)(2,1)}, u32[]{:S(2)}, u32[]{:S(2)}) %all-to-all-start) | async-done | bytes 2097184 | tf_op jit(solution)/shard_map/all_to_all | solution.py:553
  35.9 2.9 %stats.1 = f32[2,256]{1,0:T(2,128)} custom-call(bf16[4,2,64,2048]{3,2,1,0:T(8,128)(2,1)} %all-to-all-done.refs_0_.refs_8_, bf16[256,2048]{1,0:T(8,128)(2,1)} %get-tuple-element.44.refs_1_.refs_9_, f32[1,2048]{1,0:T(1,128)} %bitcast.7), custom_call_target="tpu_custom_call" | custom-call | bytes 8000 | tf_op jit(solution)/shard_map/stats/pallas_call | solution.py:487
  38.8 6.5 %psum.7.refs_7_ = f32[2,256]{1,0:T(2,128)} all-reduce(f32[2,256]{1,0:T(2,128)} %stats.1), channel_id=1, replica_groups=mesh['dp'=8,'tensor'=4] {'tensor'}, use_global_device_ids=true, to_apply=%region_0.0 | all-reduce | flops 512 | bytes 4096 | tf_op jit(solution)/shard_map/psum | solution.py:584
  45.3 6.6 %head.1 = (bf16[256,2048]{1,0:T(8,128)(2,1)}, bf16[256,2048]{1,0:T(8,128)(2,1)}, f32[1,2048]{1,0:T(1,128)}, bf16[136,2048]{1,0:T(8,128)(2,1)}) custom-call(bf16[3,256,2048]{2,1,0:T(8,128)(2,1)} %refs_0_.7, bf16[3,256,2048]{2,1,0:T(8,128)(2,1)} %refs_0_.7, bf16[3,256,2048]{2,1,0:T(8,128)(2,1)} %refs_0_.7, ...), custom_call_target="tpu_custom_call" | custom-call | bytes 8000 | tf_op jit(solution)/shard_map/head/pallas_call | solution.py:487
  51.9 1.3 %collective-permute-start.1 = (bf16[136,2048]{1,0:T(8,128)(2,1)}, bf16[136,2048]{1,0:T(8,128)(2,1)}, u32[]{:S(2)}, u32[]{:S(2)}) collective-permute-start(bf16[136,2048]{1,0:T(8,128)(2,1)} %get-tuple-element.40), channel_id=1, source_target_pairs={{4,0},{8,4},{12,8},{16,12},{20,16},{24,20},{28,24},{5,1},{9,5},{13... | collective-permute-start | bytes 1671176 | tf_op jit(solution)/shard_map/ppermute | solution.py:375
  53.2 4.3 %all-to-all-start.1 = ((bf16[4,64,2048]{2,1,0:T(8,128)(2,1)}), bf16[4,64,2048]{2,1,0:T(8,128)(2,1)}, u32[]{:S(2)}, u32[]{:S(2)}) async-start(bf16[4,64,2048]{2,1,0:T(8,128)(2,1)} %bitcast.6), calls=%async_computation.1 | async-start | bytes 2097152 | tf_op jit(solution)/shard_map/all_to_all | solution.py:619
  57.4 8.4 %sums.1.refs_9_ = f32[256,128]{1,0:T(8,128)} custom-call(bf16[3,256,2048]{2,1,0:T(8,128)(2,1)} %refs_0_.7, bf16[136,2048]{1,0:T(8,128)(2,1)} %collective-permute-done.refs_1_.refs_3_, bf16[256,2048]{1,0:T(8,128)(2,1)} %get-tuple-element.41.refs_2_, bf16[256,2048]{1,0:T(8,128)(2,1)} %get-tuple-element.39.refs_3_.refs_7_, ...), custom_call_target="tpu_custom_call" | custom-call | bytes 8000 | tf_op jit(solution)/shard_map/sums/pallas_call | solution.py:487
  65.8 3.2 %collective-permute-done.1.refs_8_ = bf16[136,2048]{1,0:T(8,128)(2,1)} collective-permute-done((bf16[136,2048]{1,0:T(8,128)(2,1)}, bf16[136,2048]{1,0:T(8,128)(2,1)}, u32[]{:S(2)}, u32[]{:S(2)}) %collective-permute-start.1) | collective-permute-done | bytes 557088 | tf_op jit(solution)/shard_map/ppermute | solution.py:375
  69.0 10.8 %backward.1 = (bf16[3,256,2048]{2,1,0:T(8,128)(2,1)}, bf16[384,128]{1,0:T(8,128)(2,1)}) custom-call(bf16[3,256,2048]{2,1,0:T(8,128)(2,1)} %refs_0_.7, bf16[136,2048]{1,0:T(8,128)(2,1)} %collective-permute-done.refs_1_.refs_3_, f32[3,3,2048]{2,1,0:T(4,128)} %refs_2_.5, f32[1,2048]{1,0:T(1,128)} %bitcast.11, bf16[128,64,256]{2,1,0:T(8,128)(2,1)} %get-tuple-element.32.refs_4_, ...), custom_call_target="tpu_custom_call" | custom-call | bytes 8000 | tf_op jit(solution)/shard_map/backward/pallas_call | solution.py:487
  79.8 3.7 %collective-permute-start.4 = (bf16[384,128]{1,0:T(8,128)(2,1)}, bf16[384,128]{1,0:T(8,128)(2,1)S(1)}, u32[]{:S(2)}, u32[]{:S(2)}) collective-permute-start(bf16[384,128]{1,0:T(8,128)(2,1)} %get-tuple-element.43), channel_id=1, source_target_pairs={{0,12},{4,8},{8,4},{12,0},{16,28},{20,24},{24,20},{28,16},{1,13},{... | collective-permute-start | bytes 294920 | tf_op jit(solution)/shard_map/ppermute | solution.py:384
  83.5 0.4 collective-permute-start.3
  84.0 0.2 collective-permute-start.2
  84.2 3.0 %collective-permute-done.4 = bf16[384,128]{1,0:T(8,128)(2,1)S(1)} collective-permute-done((bf16[384,128]{1,0:T(8,128)(2,1)}, bf16[384,128]{1,0:T(8,128)(2,1)S(1)}, u32[]{:S(2)}, u32[]{:S(2)}) %collective-permute-start.4) | collective-permute-done | bytes 98336 | tf_op jit(solution)/shard_map/ppermute | solution.py:384
  87.2 1.2 %collective-permute-done.3 = bf16[384,128]{1,0:T(8,128)(2,1)S(1)} collective-permute-done((bf16[384,128]{1,0:T(8,128)(2,1)}, bf16[384,128]{1,0:T(8,128)(2,1)S(1)}, u32[]{:S(2)}, u32[]{:S(2)}) %collective-permute-start.3) | collective-permute-done | bytes 98336 | tf_op jit(solution)/shard_map/ppermute | solution.py:384
  88.3 0.4 collective-permute-done.2
  88.8 1.0 fusion
  89.7 2.7 %collective-permute-start.5 = (bf16[384,128]{1,0:T(8,128)(2,1)S(1)}, bf16[384,128]{1,0:T(8,128)(2,1)S(1)}, u32[]{:S(2)}, u32[]{:S(2)}) collective-permute-start(bf16[384,128]{1,0:T(8,128)(2,1)S(1)} %get-tuple-element.55), channel_id=1, source_target_pairs={{0,16},{4,20},{8,24},{12,28},{16,0},{20,4},{24,8},{28,12},{1,17},{... | collective-permute-start | bytes 294920 | tf_op jit(solution)/shard_map/ppermute | solution.py:384
  92.4 0.0 all-to-all-done.1.received_ref
  92.4 3.9 %norm.1 = (bf16[64,8192]{1,0:T(8,128)(2,1)}, bf16[64,8192]{1,0:T(8,128)(2,1)}) custom-call(bf16[4,64,2048]{2,1,0:T(8,128)(2,1)} %all-to-all-done.1.received_ref, bf16[64,8192]{1,0:T(8,128)(2,1)} %residual_ref.3, bf16[64,8192]{1,0:T(8,128)(2,1)} %cot_ref.3, f32[1,8192]{1,0:T(1,128)} %bitcast.12), custom_call_target="tpu_custom_call" | custom-call | bytes 4000 | tf_op jit(solution)/shard_map/norm/pallas_call | solution.py:667
  96.3 0.0 collective-permute-done.5.other_ref
  96.3 0.7 close.1
Async XLA Ops:
  5.1 30.8 %all-to-all-start = ((bf16[4,2,64,2048]{3,2,1,0:T(8,128)(2,1)}), bf16[4,2,64,2048]{3,2,1,0:T(8,128)(2,1)}, u32[]{:S(2)}, u32[]{:S(2)}) async-start(bf16[4,2,64,2048]{3,2,1,0:T(8,128)(2,1)} %get-tuple-element.33), calls=%async_computation | async-start | bytes 4194304 | tf_op jit(solution)/shard_map/all_to_all | solution.py:553
  9.5 17.7 %collective-permute-start = (bf16[136,2048]{1,0:T(8,128)(2,1)}, bf16[136,2048]{1,0:T(8,128)(2,1)}, u32[]{:S(2)}, u32[]{:S(2)}) collective-permute-start(bf16[136,2048]{1,0:T(8,128)(2,1)} %get-tuple-element.31), channel_id=1, source_target_pairs={{0,4},{4,8},{8,12},{12,16},{16,20},{20,24},{24,28},{1,5},{5,9},{9,... | collective-permute-start | bytes 1671176 | tf_op jit(solution)/shard_map/ppermute | solution.py:375
  51.9 17.1 %collective-permute-start.1 = (bf16[136,2048]{1,0:T(8,128)(2,1)}, bf16[136,2048]{1,0:T(8,128)(2,1)}, u32[]{:S(2)}, u32[]{:S(2)}) collective-permute-start(bf16[136,2048]{1,0:T(8,128)(2,1)} %get-tuple-element.40), channel_id=1, source_target_pairs={{4,0},{8,4},{12,8},{16,12},{20,16},{24,20},{28,24},{5,1},{9,5},{13... | collective-permute-start | bytes 1671176 | tf_op jit(solution)/shard_map/ppermute | solution.py:375
  53.2 39.2 %all-to-all-start.1 = ((bf16[4,64,2048]{2,1,0:T(8,128)(2,1)}), bf16[4,64,2048]{2,1,0:T(8,128)(2,1)}, u32[]{:S(2)}, u32[]{:S(2)}) async-start(bf16[4,64,2048]{2,1,0:T(8,128)(2,1)} %bitcast.6), calls=%async_computation.1 | async-start | bytes 2097152 | tf_op jit(solution)/shard_map/all_to_all | solution.py:619
  79.8 7.4 %collective-permute-start.4 = (bf16[384,128]{1,0:T(8,128)(2,1)}, bf16[384,128]{1,0:T(8,128)(2,1)S(1)}, u32[]{:S(2)}, u32[]{:S(2)}) collective-permute-start(bf16[384,128]{1,0:T(8,128)(2,1)} %get-tuple-element.43), channel_id=1, source_target_pairs={{0,12},{4,8},{8,4},{12,0},{16,28},{20,24},{24,20},{28,16},{1,13},{... | collective-permute-start | bytes 294920 | tf_op jit(solution)/shard_map/ppermute | solution.py:384
  83.5 4.8 %collective-permute-start.3 = (bf16[384,128]{1,0:T(8,128)(2,1)}, bf16[384,128]{1,0:T(8,128)(2,1)S(1)}, u32[]{:S(2)}, u32[]{:S(2)}) collective-permute-start(bf16[384,128]{1,0:T(8,128)(2,1)} %get-tuple-element.43), channel_id=1, source_target_pairs={{0,8},{4,12},{8,0},{12,4},{16,24},{20,28},{24,16},{28,20},{1,9},{5... | collective-permute-start | bytes 294920 | tf_op jit(solution)/shard_map/ppermute | solution.py:384
  84.0 4.8 %collective-permute-start.2 = (bf16[384,128]{1,0:T(8,128)(2,1)}, bf16[384,128]{1,0:T(8,128)(2,1)S(1)}, u32[]{:S(2)}, u32[]{:S(2)}) collective-permute-start(bf16[384,128]{1,0:T(8,128)(2,1)} %get-tuple-element.43), channel_id=1, source_target_pairs={{0,4},{4,0},{8,12},{12,8},{16,20},{20,16},{24,28},{28,24},{1,5},{5... | collective-permute-start | bytes 294920 | tf_op jit(solution)/shard_map/ppermute | solution.py:384
  89.7 6.5 %collective-permute-start.5 = (bf16[384,128]{1,0:T(8,128)(2,1)S(1)}, bf16[384,128]{1,0:T(8,128)(2,1)S(1)}, u32[]{:S(2)}, u32[]{:S(2)}) collective-permute-start(bf16[384,128]{1,0:T(8,128)(2,1)S(1)} %get-tuple-element.55), channel_id=1, source_target_pairs={{0,16},{4,20},{8,24},{12,28},{16,0},{20,4},{24,8},{28,12},{1,17},{... | collective-permute-start | bytes 294920 | tf_op jit(solution)/shard_map/ppermute | solution.py:384
